TPU v7x, 128 devices: a whole 4x4x4 slice. The times are simulated.
128 devices in a mesh: gy: 8 (over z_hi, y), gx: 16 (over x, z_lo, core).
Axes of the slice: x: 4, y: 4, z: 4 (z_hi: 2, z_lo: 2; z = z_hi * 2 + z_lo), core: 2. Of those that a mesh axis runs over, the one named last changes fastest.
Arguments:
- ocean_state: bfloat16 [3072, 16, 4096], P('gy', None, 'gx'), may hold values from -6 to 6
- atm_blocks: bfloat16 [24576, 16, 128], P(('gy', 'gx')), may hold values from -6 to 6
- dest_tile: int32 [24576, 1], P(('gy', 'gx')), may hold values from 0 to 127; in each aligned block of 192 rows (0 to 191, 192 to 383, ...) at most 3 rows name the same one
- dest_row: int32 [24576], P(('gy', 'gx')), may hold values from 0 to 191
- live_entry: int32 [24576], P(('gy', 'gx')), may hold values 0 or 1
- land_mask: int32 [3072, 4096], P('gy', 'gx'), may hold values 0 or 1
- fold_pair: int32 [16], replicated, may hold values from 0 to 15, as said below
- first_weight: bfloat16 [3, 3, 64, 32], replicated, may hold values from -0.375 to 0.375
- first_bias: float32 [64], replicated, may hold values from -3 to 3
- second_weight: bfloat16 [3, 3, 8, 64], replicated, may hold values from -0.25 to 0.25
- second_bias: float32 [8], replicated, may hold values from -3 to 3
Outputs:
- eddy_forcing: bfloat16 [3072, 8, 4096], P('gy', None, 'gx')
Inputs may be any that keep to these rules, and one draw needn't show every extreme that they name: `dest_tile`: at most 3 of the 192 entries held by one device name the same tile, and some device names some tile exactly 3 times. fold_pair[fold_pair[t]] = t and fold_pair[t] != t for every tile t.
All inputs are finite; a program needn't handle non-finite values. No bound on the sum of `live_entry` or of `land_mask` on one device may be relied on, other than what follows from the above.
Results may differ from a plain program's by a relative error of at most 0.005.
Values may be sent and summed in bfloat16 or wider, within the bound.
No kernel may reach another device: no remote copies, remote signals or barrier semaphores. Data moves between devices by JAX's collectives and lax.ppermute only.
A program may use at most 192 MiB of HBM per device.

v0:
```python
import jax
import jax.numpy as jnp
from jax import lax
from jax.sharding import PartitionSpec as P

row_block = 32


def with_halo(shard, sides, width, wrap):
    for axis, dim in sides:
        size, length = (lax.axis_size(axis), shard.shape[dim])
        up = [(i, (i + 1) % size) for i in range(size if wrap else size - 1)]
        down = [(j, i) for i, j in up]
        last = lax.slice_in_dim(shard, length - width, length, axis=dim)
        leading = lax.slice_in_dim(shard, 0, width, axis=dim)
        before = lax.ppermute(last, axis, up)
        after = lax.ppermute(leading, axis, down)
        shard = jnp.concatenate([before, shard, after], axis=dim)
    return shard


def fold_row(gathered, fold_pair, margin, signs):
    columns = gathered.shape[1]
    tile_count = fold_pair.shape[0]
    tile_cols = columns // tile_count
    placed = lax.axis_index("gx") * tile_cols + jnp.arange(
        -margin, tile_cols + margin, dtype=jnp.int32
    )
    placed = placed % columns
    tile_of = placed // tile_cols
    matches = tile_of[:, None] == jnp.arange(tile_count, dtype=jnp.int32)[None, :]
    partner_tile = jnp.sum(jnp.where(matches, fold_pair[None, :], 0), axis=1)
    partner = partner_tile * tile_cols + tile_cols - 1 - placed % tile_cols
    return jnp.take(gathered, partner, axis=1) * signs[:, None]


def convolve(padded, weight, finish):
    out_rows = padded.shape[0] - 2
    out_cols = padded.shape[2] - 2

    def block_out(start, count):
        piece = lax.dynamic_slice_in_dim(padded, start, count + 2, 0)
        total = jnp.zeros((count, weight.shape[2], out_cols), jnp.float32)
        for shift_y in range(3):
            for shift_x in range(3):
                total = total + jnp.einsum(
                    "oc,ycx->yox",
                    weight[shift_y, shift_x],
                    piece[shift_y : shift_y + count, :, shift_x : shift_x + out_cols],
                    preferred_element_type=jnp.float32,
                )
        return finish(total, start, count)

    whole_blocks = out_rows // row_block
    mapped = lax.map(
        lambda number: block_out(number * row_block, row_block),
        jnp.arange(whole_blocks, dtype=jnp.int32),
    )
    pieces = mapped.reshape((whole_blocks * row_block,) + mapped.shape[2:])
    return pieces


def per_device(
    ocean_state,
    atm_blocks,
    dest_tile,
    dest_row,
    live_entry,
    land_mask,
    fold_pair,
    first_weight,
    first_bias,
    second_weight,
    second_bias,
):
    tile_rows = ocean_state.shape[0]
    half_rows = tile_rows // 2
    fields = atm_blocks.shape[1]
    block_cols = atm_blocks.shape[2]
    held = atm_blocks.shape[0]
    lat_tiles = lax.axis_size("gy")
    lon_tiles = lax.axis_size("gx")
    devices = lat_tiles * lon_tiles
    capacity = max(2, 2 * held // devices)
    targets = dest_tile[:, 0]
    is_live = live_entry == 1
    hits = (
        (targets[:, None] == jnp.arange(devices, dtype=jnp.int32)[None, :]) & is_live[:, None]
    ).astype(jnp.int32)
    earlier = jnp.cumsum(hits, axis=0) - hits
    ranks = jnp.sum(earlier * hits, axis=1)
    placing = jnp.where(is_live, targets * capacity + ranks, devices * capacity)
    outgoing = (
        jnp.zeros((devices * capacity, fields, block_cols), jnp.bfloat16)
        .at[placing]
        .set(atm_blocks, mode="drop")
    )
    outgoing_rows = (
        jnp.full((devices * capacity,), -1, jnp.int32).at[placing].set(dest_row, mode="drop")
    )
    incoming, incoming_rows = (
        lax.all_to_all(
            outgoing.reshape(devices, capacity, fields, block_cols),
            ("gy", "gx"),
            split_axis=0,
            concat_axis=0,
            tiled=True,
        ),
        lax.all_to_all(
            outgoing_rows.reshape(devices, capacity),
            ("gy", "gx"),
            split_axis=0,
            concat_axis=0,
            tiled=True,
        ),
    )
    selector = (
        incoming_rows.reshape(1, -1) == jnp.arange(half_rows, dtype=jnp.int32)[:, None]
    ).astype(jnp.bfloat16)
    coarse = jnp.dot(
        selector, incoming.reshape(-1, fields * block_cols), preferred_element_type=jnp.float32
    ).astype(jnp.bfloat16)
    coarse = coarse.reshape(half_rows, fields, block_cols)
    forcing = jnp.repeat(jnp.repeat(coarse, 2, axis=0), 2, axis=2)
    mask_values = land_mask.astype(jnp.bfloat16)[:, None, :]
    inputs = jnp.concatenate([ocean_state, forcing], axis=1) * mask_values
    levels = ocean_state.shape[1] // 4
    channel = jnp.arange(inputs.shape[1])
    in_signs = jnp.where(
        (channel < 2 * levels) | (channel == 4 * levels) | (channel == 4 * levels + 1), -1.0, 1.0
    ).astype(jnp.bfloat16)
    is_top = lax.axis_index("gy") == lat_tiles - 1
    top_inputs = lax.all_gather(inputs[-1], "gx", axis=1, tiled=True)

    def hidden_finish(total, start, count):
        return jnp.maximum(total + first_bias[None, :, None], 0.0).astype(jnp.bfloat16)

    sides = with_halo(inputs, (("gx", 2),), 1, True)
    padded = with_halo(sides, (("gy", 0),), 1, False)
    folded = fold_row(top_inputs, fold_pair, 1, in_signs)
    padded = padded.at[tile_rows + 1].set(jnp.where(is_top, folded, padded[tile_rows + 1]))
    hidden = convolve(padded, first_weight, hidden_finish)
    top_hidden = hidden[-1]
    gathered_hidden = lax.all_gather(top_hidden, "gx", axis=1, tiled=True)
    hidden_signs = jnp.ones((first_weight.shape[2],), jnp.bfloat16)
    hidden_folded = fold_row(gathered_hidden, fold_pair, 1, hidden_signs)
    hidden_sides = with_halo(hidden, (("gx", 2),), 1, True)
    padded_hidden = with_halo(hidden_sides, (("gy", 0),), 1, False)
    padded_hidden = padded_hidden.at[tile_rows + 1].set(
        jnp.where(is_top, hidden_folded, padded_hidden[tile_rows + 1])
    )

    def output_finish(total, start, count):
        mask_rows = lax.dynamic_slice_in_dim(mask_values, start, count, 0)
        return ((total + second_bias[None, :, None]) * mask_rows).astype(jnp.bfloat16)

    return convolve(padded_hidden, second_weight, output_finish)


def solution(mesh):
    return jax.shard_map(
        per_device,
        mesh=mesh,
        in_specs=(
            P("gy", None, "gx"),
            P(("gy", "gx"), None, None),
            P(("gy", "gx"), None),
            P(("gy", "gx")),
            P(("gy", "gx")),
            P("gy", "gx"),
            P(),
            P(),
            P(),
            P(),
            P(),
        ),
        out_specs=P("gy", None, "gx"),
        check_vma=False,
    )
```

profile of v0, /device:TPU:66, one launch (start us, length us, event | category | flops | bytes accessed | tf_op | source)
XLA Modules:
  0.0 821.5 jit_solution(12551753886219388473)
XLA Ops:
  5.5 10.0 %all-to-all-start = ((s32[128,1,3]{2,1,0:T(1,128)}), s32[128,1,3]{2,1,0:T(1,128)S(1)}, u32[]{:S(2)}, u32[]{:S(2)}) async-start(s32[128,1,3]{2,1,0:T(1,128)} %bitcast.48), calls=%async_computation | async-start | bytes 131072 | tf_op jit(solution)/shard_map/all_to_all | solution.py:109
  16.9 21.3 %scatter_fusion = bf16[384,16,128]{2,1,0:T(8,128)(2,1)} fusion(bf16[384,16,128]{2,1,0:T(8,128)(2,1)} %broadcast_in_dim.98, s32[192]{0:T(256)S(1)} %compare_select_fusion.6, bf16[192,16,128]{2,1,0:T(8,128)(2,1)} %param.20), kind=kCustom, calls=%fused_computation.3 | custom fusion | bytes 2360064 | tf_op jit(solution)/shard_map/scatter | solution.py:96
  38.2 9.8 %all-to-all-start.1 = ((bf16[128,3,16,128]{3,2,1,0:T(8,128)(2,1)}), bf16[128,3,16,128]{3,2,1,0:T(8,128)(2,1)S(1)}, u32[]{:S(2)}, u32[]{:S(2)}) async-start(bf16[128,3,16,128]{3,2,1,0:T(8,128)(2,1)} %bitcast.49), calls=%async_computation.1 | async-start | bytes 3145728 | tf_op jit(solution)/shard_map/all_to_all | solution.py:102
  48.0 17.6 %copy.114 = bf16[384,16,256]{1,2,0:T(8,128)(2,1)} copy(bf16[384,16,256]{2,1,0:T(8,128)(2,1)} %param.19) | data formatting | bytes 6291456 | tf_op args[0]
  73.4 19.0 %copy.115 = bf16[384,16,256]{1,2,0:T(8,128)(2,1)} copy(bf16[384,16,256]{0,1,2:T(8,128)(2,1)S(1)} %bitcast.203) | data formatting | bytes 6291456 | tf_op jit(solution)/shard_map/reshape | solution.py:124
  92.4 24.9 %maximum_multiply_fusion = bf16[384,32,256]{1,2,0:T(8,128)(2,1)} fusion(bf16[384,16,256]{1,2,0:T(8,128)(2,1)} %copy.115, bf16[384,16,256]{1,2,0:T(8,128)(2,1)} %copy.114, bf16[384,256]{1,0:T(8,128)(2,1)} %convert_element_type.27), kind=kLoop, calls=%fused_computation.104 | loop fusion | flops 18874368 | bytes 12779520 | tf_op jit(solution)/shard_map/mul | solution.py:126
  125.2 16.4 %pad_maximum_fusion.1 = bf16[384,32,258]{1,2,0:T(8,128)(2,1)S(1)} fusion(bf16[384,32,1]{1,2,0:T(2,128)(2,1)S(1)} %collective-permute-done.1, bf16[384,32,256]{1,2,0:T(8,128)(2,1)} %maximum_multiply_fusion, bf16[384,32,1]{1,2,0:T(2,128)(2,1)S(1)} %collective-permute-done), kind=kLoop, calls=%fused_computation.103 | loop fusion | flops 19021824 | bytes 12681216 | tf_op jit(solution)/shard_map/concatenate | solution.py:18
  141.6 8.6 %copy-done = bf16[384,32,258]{1,2,0:T(8,128)(2,1)} copy-done((bf16[384,32,258]{1,2,0:T(8,128)(2,1)}, bf16[384,32,258]{1,2,0:T(8,128)(2,1)S(1)}, u32[]{:S(2)}) %copy-start) | copy-done | bytes 6340632
  150.1 6.3 collective-permute-start.3
  156.5 21.7 %all-gather = bf16[1,32,4096]{1,2,0:T(8,128)(2,1)S(1)} all-gather(bf16[1,32,256]{1,2,0:T(8,128)(2,1)S(1)} %slice-done), channel_id=2, replica_groups=mesh['gy'=8,'gx'=16] {'gx'}, dimensions={2}, use_global_device_ids=true | all-gather | bytes 278528 | tf_op jit(solution)/shard_map/all_gather | solution.py:133
  179.5 33.0 %copy.118 = bf16[384,32,258]{0,1,2:T(8,128)(2,1)} copy(bf16[384,32,258]{1,2,0:T(8,128)(2,1)} %copy-done) | data formatting | bytes 12681216 | tf_op jit(solution)/shard_map/concatenate | solution.py:18
  225.2 9.6 %pad_maximum_fusion.2 = bf16[386,32,258]{0,1,2:T(8,128)(2,1)} fusion(bf16[1,32,258]{0,1,2:T(8,128)(2,1)S(1)} %copy.119, bf16[384,32,258]{0,1,2:T(8,128)(2,1)} %copy.118, bf16[1,32,258]{0,1,2:T(8,128)(2,1)} %copy.117), kind=kLoop, calls=%fused_computation.105 | loop fusion | flops 19120896 | bytes 12747264 | tf_op jit(solution)/shard_map/concatenate | solution.py:18
  234.8 25.1 %scatter.26 = bf16[386,32,258]{0,1,2:T(8,128)(2,1)} dynamic-update-slice(bf16[386,32,258]{0,1,2:T(8,128)(2,1)} %pad_maximum_fusion.2, bf16[1,32,258]{0,1,2:T(8,128)(2,1)} %copy.120, s32[]{:T(128)} %constant.198.clone.1, s32[]{:T(128)} %constant.177.clone.1, s32[]{:T(128)} %constant.177.clone.1) | dynamic-update-slice | bytes 33028 | tf_op jit(solution)/shard_map/scatter | solution.py:141
  260.0 15.9 %copy.121 = bf16[386,32,258]{2,1,0:T(8,128)(2,1)} copy(bf16[386,32,258]{0,1,2:T(8,128)(2,1)} %scatter.26) | data formatting | bytes 12747264 | tf_op jit(solution)/shard_map/while | solution.py:55
  275.9 213.5 %while.22 = (s32[]{:T(128)}, bf16[12,32,64,256]{3,2,1,0:T(8,128)(2,1)}, s32[12]{0:T(128)S(1)}, bf16[386,32,258]{2,1,0:T(8,128)(2,1)}, bf16[3,3,64,32]{2,3,1,0:T(...) while((s32[]{:T(128)}, ...), condition=%wide.region_7.8_spmd, body=%wide.region_6.7_spmd.sunk | while | flops 307757056 | bytes 39396632 | solution.py:55
  290.1 3.7 fusion.190
  307.9 3.6 fusion.190
  325.7 3.7 fusion.190
  343.5 3.6 fusion.190
  379.0 3.7 fusion.190
  396.8 3.6 fusion.190
  414.6 3.6 fusion.190
  432.4 3.7 fusion.190
  450.2 3.6 fusion.190
  468.0 3.6 fusion.190
  485.8 3.6 fusion.190
  489.4 22.9 %copy.122 = bf16[12,32,64,256]{2,3,1,0:T(8,128)(2,1)} copy(bf16[12,32,64,256]{3,2,1,0:T(8,128)(2,1)} %get-tuple-element.98) | data formatting | bytes 25165824 | tf_op jit(solution)/shard_map/while | solution.py:55
  523.1 7.5 collective-permute-start.7
  530.7 21.9 %all-gather.1 = bf16[1,64,4096]{1,2,0:T(8,128)(2,1)S(1)} all-gather(bf16[1,64,256]{1,2,0:T(8,128)(2,1)S(1)} %slice.213), channel_id=3, replica_groups=mesh['gy'=8,'gx'=16] {'gx'}, dimensions={2}, use_global_device_ids=true | all-gather | bytes 557056 | tf_op jit(solution)/shard_map/all_gather | solution.py:144
  554.1 24.6 %pad_maximum_fusion = bf16[386,64,258]{1,2,0:T(8,128)(2,1)} fusion(bf16[1,64,258]{1,2,0:T(8,128)(2,1)S(1)} %collective-permute-done.7, bf16[384,64,1]{1,2,0:T(2,128)(2,1)S(1)} %collective-permute-done.5, bf16[384,64,256]{1,2,0:T(8,128)(2,1)} %bitcast.202, bf16[384,64,1]{1,2,0:T(2,128)(2,1)S(1)} %collective-permute-done.4, bf16[1,64,258]{1,2,0:T(8,128)(2,1)S(1)} %copy.124), kind=kLoop, calls=%fused_computation.102 | loop fusion | flops 63736320 | bytes 25494528 | tf_op jit(solution)/shard_map/concatenate | solution.py:18
  579.4 29.0 %copy.125 = bf16[386,64,258]{2,1,0:T(8,128)(2,1)} copy(bf16[386,64,258]{1,2,0:T(8,128)(2,1)} %fusion.101) | data formatting | bytes 25494528 | tf_op jit(solution)/shard_map/while | solution.py:55
  608.4 213.0 %while.23 = (s32[]{:T(128)}, bf16[12,32,8,256]{3,2,1,0:T(8,128)(2,1)}, s32[12]{0:T(128)S(1)}, bf16[386,64,258]{2,1,0:T(8,128)(2,1)}, bf16[3,3,8,64]{3,2,1,0:T(8,...) while((s32[]{:T(128)}, ...), condition=%wide.region_9.10_spmd, body=%wide.region_8.9_spmd.sunk | while | flops 76226568 | bytes 13864264 | solution.py:55
  (323 shorter events, 420.3 us)
Async XLA Ops:
  5.5 32.7 %all-to-all-start = ((s32[128,1,3]{2,1,0:T(1,128)}), s32[128,1,3]{2,1,0:T(1,128)S(1)}, u32[]{:S(2)}, u32[]{:S(2)}) async-start(s32[128,1,3]{2,1,0:T(1,128)} %bitcast.48), calls=%async_computation | async-start | bytes 131072 | tf_op jit(solution)/shard_map/all_to_all | solution.py:109
  38.2 30.1 %all-to-all-start.1 = ((bf16[128,3,16,128]{3,2,1,0:T(8,128)(2,1)}), bf16[128,3,16,128]{3,2,1,0:T(8,128)(2,1)S(1)}, u32[]{:S(2)}, u32[]{:S(2)}) async-start(bf16[128,3,16,128]{3,2,1,0:T(8,128)(2,1)} %bitcast.49), calls=%async_computation.1 | async-start | bytes 3145728 | tf_op jit(solution)/shard_map/all_to_all | solution.py:102
  48.0 17.7 %copy-start.2 = (s32[384,256]{1,0:T(8,128)S(1)}, s32[384,256]{1,0:T(8,128)}, u32[]{:S(2)}) copy-start(s32[384,256]{1,0:T(8,128)} %param.24) | copy-start | bytes 1179652
  48.0 18.4 %copy-start.6 = (s32[16]{0:T(128)S(1)}, s32[16]{0:T(128)}, u32[]{:S(2)}) copy-start(s32[16]{0:T(128)} %param.25) | copy-start | bytes 196
  119.0 6.2 collective-permute-start
  119.1 6.1 collective-permute-start.1
  121.7 34.7 %slice-start = ((bf16[384,32,256]{1,2,0:T(8,128)(2,1)}), bf16[1,32,256]{1,2,0:T(8,128)(2,1)S(1)}, s32[]{:S(2)}) async-start(bf16[384,32,256]{1,2,0:T(8,128)(2,1)} %maximum_multiply_fusion), calls=%async_computation.2 | async-start | bytes 131072 | tf_op jit(solution)/shard_map/slice | solution.py:133
  141.6 8.6 %copy-start = (bf16[384,32,258]{1,2,0:T(8,128)(2,1)}, bf16[384,32,258]{1,2,0:T(8,128)(2,1)S(1)}, u32[]{:S(2)}) copy-start(bf16[384,32,258]{1,2,0:T(8,128)(2,1)S(1)} %pad_maximum_fusion.1) | copy-start | bytes 19021828
  150.1 64.6 %collective-permute-start.3 = (bf16[1,32,258]{1,2,0:T(8,128)(2,1)S(1)}, bf16[1,32,258]{1,2,0:T(8,128)(2,1)S(1)}, u32[]{:S(2)}, u32[]{:S(2)}) collective-permute-start(bf16[1,32,258]{1,2,0:T(8,128)(2,1)S(1)} %get-tuple-element.218), channel_id=1, source_target_pairs={{16,0},{32,16},{48,32},{64,48},{80,64},{96,80},{112,96},{17,1},{33... | collective-permute-start | bytes 49544 | tf_op jit(solution)/shard_map/ppermute | solution.py:17
  212.6 9.3 %collective-permute-start.2 = (bf16[1,32,258]{2,1,0:T(8,128)(2,1)S(1)}, bf16[1,32,258]{2,1,0:T(8,128)(2,1)S(1)}, u32[]{:S(2)}, u32[]{:S(2)}) collective-permute-start(bf16[1,32,258]{2,1,0:T(8,128)(2,1)S(1)} %copy.116), channel_id=1, source_target_pairs={{0,16},{16,32},{32,48},{48,64},{64,80},{80,96},{96,112},{1,17},{17... | collective-permute-start | bytes 49544 | tf_op jit(solution)/shard_map/ppermute | solution.py:16
  260.0 15.9 %copy-start.1 = (bf16[3,3,64,32]{2,3,1,0:T(8,128)(2,1)S(1)}, bf16[3,3,64,32]{2,3,1,0:T(8,128)(2,1)}, u32[]{:S(2)}) copy-start(bf16[3,3,64,32]{2,3,1,0:T(8,128)(2,1)} %param.26) | copy-start | bytes 110596
  260.0 15.9 %copy-start.4 = (f32[64]{0:T(128)S(1)}, f32[64]{0:T(128)}, u32[]{:S(2)}) copy-start(f32[64]{0:T(128)} %param.27) | copy-start | bytes 772
  514.0 6.2 collective-permute-start.4
  514.1 6.1 collective-permute-start.5
  521.2 32.8 %collective-permute-start.6 = (bf16[1,64,258]{2,1,0:T(8,128)(2,1)S(1)}, bf16[1,64,258]{2,1,0:T(8,128)(2,1)S(1)}, u32[]{:S(2)}, u32[]{:S(2)}) collective-permute-start(bf16[1,64,258]{2,1,0:T(8,128)(2,1)S(1)} %copy.123), channel_id=1, source_target_pairs={{0,16},{16,32},{32,48},{48,64},{64,80},{80,96},{96,112},{1,17},{17... | collective-permute-start | bytes 99080 | tf_op jit(solution)/shard_map/ppermute | solution.py:16
  523.1 31.0 %collective-permute-start.7 = (bf16[1,64,258]{1,2,0:T(8,128)(2,1)S(1)}, bf16[1,64,258]{1,2,0:T(8,128)(2,1)S(1)}, u32[]{:S(2)}, u32[]{:S(2)}) collective-permute-start(bf16[1,64,258]{1,2,0:T(8,128)(2,1)S(1)} %get-tuple-element.220), channel_id=1, source_target_pairs={{16,0},{32,16},{48,32},{64,48},{80,64},{96,80},{112,96},{17,1},{33... | collective-permute-start | bytes 99080 | tf_op jit(solution)/shard_map/ppermute | solution.py:17
  579.4 29.0 %copy-start.3 = (bf16[3,3,8,64]{3,2,1,0:T(8,128)(2,1)S(1)}, bf16[3,3,8,64]{3,2,1,0:T(8,128)(2,1)}, u32[]{:S(2)}) copy-start(bf16[3,3,8,64]{3,2,1,0:T(8,128)(2,1)} %param.28) | copy-start | bytes 27652
  579.4 29.0 %copy-start.5 = (f32[8]{0:T(128)S(1)}, f32[8]{0:T(128)}, u32[]{:S(2)}) copy-start(f32[8]{0:T(128)} %param.29) | copy-start | bytes 100
where the time goes:
time: 836 us; the launch traced here: 821 us
  matrix products  397 us (47%)
  local copies, waits for them, and re-layouts  232 us (28%)
  other arithmetic  82.2 us (10%)
  blocking collectives  43.6 us (5%)
  starting transfers between devices  43.1 us (5%)
  loops' own time  15.5 us (2%)
    dot_general x216, matrix products, block_out(): jnp.einsum('oc,ycx->yox', weight[shift_y, shift_x], piece[shift_y:shift_y...  396 us
    while x3, local copies, waits for them, and re-layouts, convolve(): lax.map(lambda number: block_out(number * row_block, row_block), jnp.aran...  67.8 us
    concatenate x3, other arithmetic, with_halo(): shard = jnp.concatenate([before, shard, after], axis=dim)  50.6 us
    concatenate x1, local copies, waits for them, and re-layouts, with_halo(): shard = jnp.concatenate([before, shard, after], axis=dim)  33 us
    unnamed x17, local copies, waits for them, and re-layouts  26.4 us
    scatter x1, local copies, waits for them, and re-layouts, per_device(): padded.at[tile_rows + 1]  25.1 us
    mul x1, other arithmetic, per_device(): inputs = jnp.concatenate([ocean_state, forcing], axis=1) * mask_values  24.9 us
    all_gather x1, blocking collectives, per_device(): gathered_hidden = lax.all_gather(top_hidden, 'gx', axis=1, tiled=True)  21.9 us
  transfers between devices with their start and end apart: 10, of which 4 were waited for; matrix products, arithmetic and copies ran while one was open for 10% of the time, Pallas kernels for 0%

commit v1 on v0

v1 whole, which is shorter than its diff:
```python
import functools

import jax
import jax.numpy as jnp
from jax import lax
from jax.experimental import pallas as pl
from jax.experimental.pallas import tpu as pltpu
from jax.sharding import PartitionSpec as P

BF = jnp.bfloat16
F32 = jnp.float32
I32 = jnp.int32
VMEM_LIMIT = 56 << 20
ROWS = 384
COLS = 256
HALF = 192
DEV = 128
CAP = 3
FLD = 16
HID = 64
OUT = 8


def lanes(shape):
    return lax.broadcasted_iota(I32, shape, len(shape) - 1)


def subs(shape):
    return lax.broadcasted_iota(I32, shape, len(shape) - 2)


def pack_kernel(code_ref, atm_ref, out_ref, rows_ref, count_ref):
    def clear(t, carry):
        count_ref[t] = 0
        for k in range(CAP):
            rows_ref[t, k] = HALF
        return carry

    lax.fori_loop(0, DEV, clear, 0, unroll=8)

    def place(i, carry):
        code = code_ref[i]

        @pl.when(code >= 0)
        def _():
            tile = code // 256
            rank = count_ref[tile]
            count_ref[tile] = rank + 1
            rows_ref[tile, rank] = code - tile * 256
            out_ref[tile * CAP + rank] = atm_ref[i]

        return carry

    lax.fori_loop(0, HALF, place, 0, unroll=4)


def pack(code, atm):
    return pl.pallas_call(
        pack_kernel,
        out_shape=(
            jax.ShapeDtypeStruct((DEV * CAP, FLD, 128), BF),
            jax.ShapeDtypeStruct((DEV, CAP), I32),
        ),
        in_specs=[
            pl.BlockSpec(memory_space=pltpu.SMEM),
            pl.BlockSpec(memory_space=pltpu.VMEM),
        ],
        out_specs=(
            pl.BlockSpec(memory_space=pltpu.VMEM),
            pl.BlockSpec(memory_space=pltpu.SMEM),
        ),
        scratch_shapes=[pltpu.SMEM((DEV,), I32)],
        name="pack",
    )(code, atm)


def coarse_kernel(rows_ref, inc_ref, out_ref, cols_ref, acc_ref):
    acc_ref[...] = jnp.zeros_like(acc_ref)

    def add(s, carry):
        for k in range(CAP):
            r = rows_ref[s, k]
            acc_ref[k, r] = acc_ref[k, r] + inc_ref[s * CAP + k].astype(F32)
        return carry

    lax.fori_loop(0, DEV, add, 0, unroll=4)
    lane = lanes((FLD, 128))
    for chunk, count in ((0, 128), (128, 64)):

        def finish(i, carry):
            first, last = carry
            r = chunk + i
            total = (acc_ref[0, r] + acc_ref[1, r] + acc_ref[2, r]).astype(BF)
            out_ref[r] = total
            total = total.astype(F32)
            here = lane == i
            first = jnp.where(here, pltpu.roll(total, i, 1), first)
            last = jnp.where(here, pltpu.roll(total, i + 1, 1), last)
            return first, last

        zero = jnp.zeros((FLD, 128), F32)
        first, last = lax.fori_loop(0, count, finish, (zero, zero), unroll=4)
        cols_ref[0, :, chunk : chunk + 128] = first.astype(BF)
        cols_ref[1, :, chunk : chunk + 128] = last.astype(BF)


def coarse_sums(rows, incoming):
    return pl.pallas_call(
        coarse_kernel,
        out_shape=(
            jax.ShapeDtypeStruct((HALF, FLD, 128), BF),
            jax.ShapeDtypeStruct((2, FLD, 256), BF),
        ),
        in_specs=[
            pl.BlockSpec(memory_space=pltpu.SMEM),
            pl.BlockSpec(memory_space=pltpu.VMEM),
        ],
        out_specs=(
            pl.BlockSpec(memory_space=pltpu.VMEM),
            pl.BlockSpec(memory_space=pltpu.VMEM),
        ),
        scratch_shapes=[pltpu.VMEM((CAP, HALF + 1, FLD, 128), F32)],
        compiler_params=pltpu.CompilerParams(vmem_limit_bytes=VMEM_LIMIT),
        name="coarse",
    )(rows, incoming)


def edge_kernel(ocean_ref, mask_ref, out_ref):
    lane = lanes((2 * FLD, 128))
    for chunk in range(3):

        def take(i, carry):
            y = chunk * 128 + i
            m = mask_ref[pl.ds(y, 1), :].astype(F32)
            m = jnp.broadcast_to(m, (FLD, COLS))
            x = jnp.concatenate([ocean_ref[y].astype(F32) * m, m], axis=0)
            left, right = x[:, :128], x[:, 128:]
            here = lane == i
            c0, c1, c2, c3 = carry
            c0 = jnp.where(here, pltpu.roll(left, i, 1), c0)
            c1 = jnp.where(here, pltpu.roll(left, i + 127, 1), c1)
            c2 = jnp.where(here, pltpu.roll(right, i + 2, 1), c2)
            c3 = jnp.where(here, pltpu.roll(right, i + 1, 1), c3)
            return c0, c1, c2, c3

        zero = jnp.zeros((2 * FLD, 128), F32)
        got = lax.fori_loop(0, 128, take, (zero,) * 4, unroll=2)
        for k in range(4):
            out_ref[k, :, chunk * 128 : chunk * 128 + 128] = got[k].astype(BF)


def edge_columns(ocean, mask):
    return pl.pallas_call(
        edge_kernel,
        out_shape=jax.ShapeDtypeStruct((4, 2 * FLD, ROWS), BF),
        compiler_params=pltpu.CompilerParams(vmem_limit_bytes=VMEM_LIMIT),
        name="edges",
    )(ocean, mask)


def main_kernel(
    ocean_ref, mask_ref, coarse_ref, own_ref, west_ref, east_ref, cown_ref, cwest_ref, ceast_ref,
    w1_ref, w1t_ref, b1_ref, w2_ref, w2l_ref, w2r_ref, b2_ref, out_ref,
    fine_ref, xs_ref, h_ref, side_ref, add_ref,
):
    rep = (subs((256, ROWS)) == lanes((256, ROWS)) // 2).astype(BF)

    def column(coarse_t, strip):
        fine = jnp.dot(coarse_t, rep, preferred_element_type=F32)
        return jnp.concatenate([strip[:FLD], (fine * strip[FLD:].astype(F32)).astype(BF)], axis=0)

    w2c = column(cwest_ref[...], west_ref[0])
    w1c = column(cwest_ref[...], west_ref[1])
    o0c = column(cown_ref[0], own_ref[0])
    o255c = column(cown_ref[1], own_ref[3])
    e1c = column(ceast_ref[...], east_ref[0])
    e2c = column(ceast_ref[...], east_ref[1])
    side_ref[0] = w1c.astype(F32)
    side_ref[1] = e1c.astype(F32)
    b1 = b1_ref[...]
    for side, cols, w2s in ((0, (w2c, w1c, o0c), w2l_ref), (1, (o255c, e1c, e2c), w2r_ref)):
        x = jnp.concatenate([c.astype(F32) for c in cols], axis=0)
        xt = jnp.concatenate([pltpu.roll(x, 1, 1), x, pltpu.roll(x, ROWS - 1, 1)], axis=0).astype(BF)
        hid = jnp.dot(w1t_ref[...], xt, preferred_element_type=F32)
        hid = jnp.maximum(hid + b1[:HID], 0.0).astype(BF).astype(F32)
        ht = jnp.concatenate([pltpu.roll(hid, 1, 1), hid, pltpu.roll(hid, ROWS - 1, 1)], axis=0)
        add_ref[side] = jnp.dot(w2s[...], ht.astype(BF), preferred_element_type=F32)

    spread = (subs((128, COLS)) == lanes((128, COLS)) // 2).astype(BF)
    for k in range(6):
        part = coarse_ref[k * 32 : k * 32 + 32].reshape(512, 128)
        fine = jnp.dot(part, spread, preferred_element_type=F32)
        fine_ref[k * 32 : k * 32 + 32] = fine.astype(BF).reshape(32, FLD, COLS)

    lane = lanes((2 * FLD, 128))
    zero = jnp.zeros((96, COLS), BF)
    xs_ref[0] = zero
    xs_ref[ROWS + 1] = zero
    for chunk in range(3):

        def build(i, carry):
            y = chunk * 128 + i
            m = jnp.broadcast_to(mask_ref[pl.ds(y, 1), :].astype(F32), (FLD, COLS))
            x = jnp.concatenate(
                [ocean_ref[y].astype(F32) * m, fine_ref[y // 2].astype(F32) * m], axis=0
            )
            west = pltpu.roll(side_ref[0, :, chunk * 128 : chunk * 128 + 128], 128 - i, 1)
            east = pltpu.roll(side_ref[1, :, chunk * 128 : chunk * 128 + 128], 127 - i, 1)
            up = pltpu.roll(x, 1, 1)
            down = pltpu.roll(x, COLS - 1, 1)
            up0 = jnp.where(lane == 0, west, up[:, :128])
            down1 = jnp.where(lane == 127, east, down[:, 128:])
            xs_ref[y + 1, 0:32, 0:128] = up0.astype(BF)
            xs_ref[y + 1, 0:32, 128:256] = up[:, 128:].astype(BF)
            xs_ref[y + 1, 32:64, :] = x.astype(BF)
            xs_ref[y + 1, 64:96, 0:128] = down[:, :128].astype(BF)
            xs_ref[y + 1, 64:96, 128:256] = down1.astype(BF)
            return carry

        lax.fori_loop(0, 128, build, 0, unroll=2)

    hzero = jnp.zeros((HID, COLS), BF)
    h_ref[0] = hzero
    h_ref[ROWS + 1] = hzero

    def conv1(block, carry):
        for k in range(8):
            g = block * 8 + k
            x = xs_ref[pl.ds(3 * g, 5)].reshape(480, COLS)
            t = jnp.dot(w1_ref[...], x, preferred_element_type=F32)
            t = jnp.maximum(t + b1, 0.0).astype(BF)
            h_ref[pl.ds(3 * g + 1, 3)] = t.reshape(3, HID, COLS)
        return carry

    lax.fori_loop(0, 16, conv1, 0)

    b2 = b2_ref[...]
    lane8 = lanes((OUT, 128))

    def conv2(block, carry):
        for k in range(4):
            j = block * 4 + k
            x = h_ref[pl.ds(6 * j, 8)].reshape(512, COLS)
            t = jnp.dot(w2_ref[...], x, preferred_element_type=F32).reshape(6, 3, OUT, COLS)
            for r in range(6):
                y = 6 * j + r
                base = pl.multiple_of((y // 128) * 128, 128)
                i = y % 128
                west = pltpu.roll(add_ref[0, :, pl.ds(base, 128)], 128 - i, 1)
                east = pltpu.roll(add_ref[1, :, pl.ds(base, 128)], 127 - i, 1)
                up = pltpu.roll(t[r, 0], 1, 1)
                down = pltpu.roll(t[r, 2], COLS - 1, 1)
                mid = t[r, 1] + b2
                m = mask_ref[pl.ds(y, 1), :].astype(F32)
                lo = mid[:, :128] + jnp.where(lane8 == 0, west, up[:, :128]) + down[:, :128]
                hi = mid[:, 128:] + up[:, 128:] + jnp.where(lane8 == 127, east, down[:, 128:])
                out_ref[y, :, 0:128] = (lo * m[:, :128]).astype(BF)
                out_ref[y, :, 128:256] = (hi * m[:, 128:]).astype(BF)
        return carry

    lax.fori_loop(0, 16, conv2, 0)


def main_conv(*args):
    return pl.pallas_call(
        main_kernel,
        out_shape=jax.ShapeDtypeStruct((ROWS, OUT, COLS), BF),
        scratch_shapes=[
            pltpu.VMEM((HALF, FLD, COLS), BF),
            pltpu.VMEM((ROWS + 2, 96, COLS), BF),
            pltpu.VMEM((ROWS + 2, HID, COLS), BF),
            pltpu.VMEM((2, 2 * FLD, ROWS), F32),
            pltpu.VMEM((2, OUT, ROWS), F32),
        ],
        compiler_params=pltpu.CompilerParams(vmem_limit_bytes=VMEM_LIMIT),
        name="convs",
    )(*args)


PAD = 384
SHIFT = 2


def onehot(pairs, rows, cols):
    src = subs((rows, cols))
    dst = lanes((rows, cols))
    hit = jnp.zeros((rows, cols), jnp.bool_)
    for source, cond in pairs:
        hit = hit | ((src == source(dst)) & cond(dst))
    return hit.astype(BF)


def patch_kernel(
    pos_ref, fold_ref, ocean_ref, coarse_ref, tops_ref, ctops_ref, w1_ref, b1_ref, w2_ref, b2_ref, main_ref,
    out_ref, in_ref, res_ref, sem,
):
    gy, gx = pos_ref[0], pos_ref[1]
    spread = (subs((256, PAD)) == lanes((256, PAD)) // 2).astype(BF)
    spread = jnp.where(lanes((256, PAD)) < COLS + 4, spread, jnp.zeros_like(spread))
    signs = jnp.where(
        (subs((2 * FLD, PAD)) < 8) | (subs((2 * FLD, PAD)) == 16) | (subs((2 * FLD, PAD)) == 17), -1.0, 1.0
    )

    def inputs(strip, coarse):
        fine = jnp.dot(coarse, spread, preferred_element_type=F32)
        return jnp.concatenate(
            [strip[:FLD], (fine * strip[FLD:].astype(F32)).astype(BF)], axis=0
        )

    for k in range(12):
        in_ref[k] = inputs(ocean_ref[k], coarse_ref[k // 2]).astype(F32)
    for k in range(3):
        in_ref[12 + k] = jnp.zeros((2 * FLD, PAD), F32)

    wrap = lambda t: jnp.where(t < 0, t + 16, jnp.where(t > 15, t - 16, t))
    near = wrap(gx - 1)
    far = wrap(gx + 1)
    p = fold_ref[gx]
    a = fold_ref[near]
    b = fold_ref[far]

    @pl.when(gy == 7)
    def _():
        def tile(t, row):
            return inputs(tops_ref[t, row], ctops_ref[t])

        def move(x, pairs):
            return jnp.dot(x, onehot(pairs, PAD, PAD), preferred_element_type=F32)

        def inside(lo, hi):
            return lambda d: (d >= lo) & (d <= hi)

        mirror = lambda d: 2 * SHIFT + COLS - 1 - d
        a1 = tile(a, 1)
        b1 = tile(b, 1)
        p1 = tile(p, 1)
        row = move(p1, [(mirror, inside(SHIFT, SHIFT + 255))])
        row = row + move(a1, [(lambda d: SHIFT + 1 - d, inside(0, 1))])
        row = row + move(b1, [(lambda d: SHIFT + 255 - (d - (SHIFT + 256)), inside(SHIFT + 256, SHIFT + 257))])
        in_ref[10] = row * signs
        corner_a = [(lambda d: SHIFT + 1 - (d - 264), inside(264, 266))]
        corner_b = [(lambda d: SHIFT + 256 - (d - 272), inside(272, 274))]
        whole = [(mirror, inside(SHIFT - 1, SHIFT + 256))]
        for k in range(2):
            in_ref[12 + k] = (
                move(p1 if k else tile(p, 0), whole)
                + move(a1 if k else tile(a, 0), corner_a)
                + move(b1 if k else tile(b, 0), corner_b)
            )
        own = in_ref[9].astype(BF)
        low = tile(fold_ref[wrap(p + 1)], 1)
        high = tile(fold_ref[wrap(p - 1)], 1)
        side_a = tile(fold_ref[wrap(a - 1)], 1)
        side_b = tile(fold_ref[wrap(b + 1)], 1)
        last = move(
            own,
            [
                (lambda d: d, inside(SHIFT, SHIFT + 255)),
                (lambda d: d - 264, inside(264, 265)),
                (lambda d: d - 273 + SHIFT + 256, inside(273, 274)),
            ],
        )
        last = last + move(low, [(lambda d: d - d + SHIFT + 255, inside(SHIFT - 1, SHIFT - 1))])
        last = last + move(high, [(lambda d: d - d + SHIFT, inside(SHIFT + 256, SHIFT + 256))])
        last = last + move(side_a, [(lambda d: d - d + SHIFT, inside(266, 266))])
        last = last + move(side_b, [(lambda d: d - d + SHIFT + 255, inside(272, 272))])
        in_ref[14] = last * signs

    def hidden(rows, flip):
        total = jnp.broadcast_to(b1_ref[...], (HID, PAD))
        for u in range(3):
            x = in_ref[rows + u]
            for v in range(3):
                shifted = pltpu.roll(x, (1 - v) % PAD, 1) if v != 1 else x
                total = total + jnp.dot(
                    w1_ref[u, 2 - v if flip else v], shifted.astype(BF), preferred_element_type=F32
                )
        return jnp.maximum(total, 0.0).astype(BF)

    virtual = hidden(12, True).astype(F32)
    lane = lanes((HID, PAD))
    virtual = jnp.where(
        lane == SHIFT - 1,
        pltpu.roll(virtual, (SHIFT - 1 - 265) % PAD, 1),
        jnp.where(lane == SHIFT + 256, pltpu.roll(virtual, (SHIFT + 256 - 273) % PAD, 1), virtual),
    )
    for half in range(2):
        hid = [hidden(6 * half + k, False).astype(F32) for k in range(4)]
        if half == 0:
            hid[0] = jnp.where(gy == 0, jnp.zeros_like(hid[0]), hid[0])
        else:
            hid[3] = jnp.where(gy == 7, virtual, hid[3])
        for r in range(2):
            total = jnp.broadcast_to(b2_ref[...], (OUT, PAD))
            for u in range(3):
                x = hid[r + u]
                for v in range(3):
                    shifted = pltpu.roll(x, (1 - v) % PAD, 1) if v != 1 else x
                    total = total + jnp.dot(w2_ref[u, v], shifted.astype(BF), preferred_element_type=F32)
            m = ocean_ref[6 * half + 2 + r][FLD : FLD + OUT].astype(F32)
            total = pltpu.roll(total * m, PAD - SHIFT, 1)
            res_ref[2 * half + r] = total[:, :COLS].astype(BF)
    copies = [
        pltpu.make_async_copy(res_ref.at[pl.ds(0, 2)], out_ref.at[pl.ds(0, 2)], sem.at[0]),
        pltpu.make_async_copy(res_ref.at[pl.ds(2, 2)], out_ref.at[pl.ds(ROWS - 2, 2)], sem.at[1]),
    ]
    for c in copies:
        c.start()
    for c in copies:
        c.wait()


def patch_rows(pos, fold_pair, ocean, coarse, tops, ctops, w1, b1, w2, b2, main):
    smem = pl.BlockSpec(memory_space=pltpu.SMEM)
    vmem = pl.BlockSpec(memory_space=pltpu.VMEM)
    hbm = pl.BlockSpec(memory_space=pl.ANY)
    return pl.pallas_call(
        patch_kernel,
        out_shape=jax.ShapeDtypeStruct((ROWS, OUT, COLS), BF),
        in_specs=[smem, smem] + [vmem] * 8 + [hbm],
        out_specs=hbm,
        scratch_shapes=[
            pltpu.VMEM((15, 2 * FLD, PAD), F32),
            pltpu.VMEM((4, OUT, COLS), BF),
            pltpu.SemaphoreType.DMA((2,)),
        ],
        input_output_aliases={10: 0},
        compiler_params=pltpu.CompilerParams(vmem_limit_bytes=VMEM_LIMIT),
        name="patch",
    )(pos, fold_pair, ocean, coarse, tops, ctops, w1, b1, w2, b2, main)


def shift_gx(x, step):
    n = lax.axis_size("gx")
    return lax.ppermute(x, "gx", [(i, (i + step) % n) for i in range(n)])


def shift_gy(x, step):
    n = lax.axis_size("gy")
    return lax.ppermute(x, "gy", [(i, i + step) for i in range(n) if 0 <= i + step < n])


def to_all_gx(x):
    n = lax.axis_size("gx")
    return lax.all_to_all(
        jnp.broadcast_to(x[None], (n,) + x.shape), "gx", split_axis=0, concat_axis=0, tiled=True
    )


def per_device(
    ocean, atm, dest_tile, dest_row, live, land_mask, fold_pair, w1, b1, w2, b2
):
    code = jnp.where(live == 1, dest_tile[:, 0] * 256 + dest_row, -1)
    outgoing, out_rows = pack(code, atm)
    incoming = lax.all_to_all(
        outgoing.reshape(DEV, CAP, FLD, 128), ("gy", "gx"), split_axis=0, concat_axis=0, tiled=True
    )
    in_rows = lax.all_to_all(out_rows, ("gy", "gx"), split_axis=0, concat_axis=0, tiled=True)

    w1b = jnp.zeros((3, HID, 5, 3, 2 * FLD), BF)
    for r in range(3):
        w1b = w1b.at[r, :, r : r + 3].set(w1.transpose(2, 0, 1, 3))
    w1b = w1b.reshape(192, 480)
    w1t = w1.transpose(2, 0, 1, 3).reshape(HID, 288)
    w2b = jnp.zeros((6, 3, OUT, 8, HID), BF)
    for r in range(6):
        w2b = w2b.at[r, :, :, r : r + 3].set(w2.transpose(1, 2, 0, 3))
    w2b = w2b.reshape(144, 512)
    w2l = w2[:, 0].transpose(1, 0, 2).reshape(OUT, 192)
    w2r = w2[:, 2].transpose(1, 0, 2).reshape(OUT, 192)
    b1c = jnp.tile(b1, 3)[:, None]
    b2c = b2[:, None]

    edges = edge_columns(ocean, land_mask)
    west = shift_gx(edges[2:4], 1)
    east = shift_gx(edges[0:2], -1)
    strip = jnp.concatenate([ocean[0:4], ocean[ROWS - 4 :]], axis=0)
    strip_mask = jnp.concatenate([land_mask[0:4], land_mask[ROWS - 4 :]], axis=0).astype(BF)
    strip_mask = jnp.broadcast_to(strip_mask[:, None, :], strip.shape)
    strip = jnp.concatenate([strip * strip_mask, strip_mask], axis=1)

    def beside(cols):
        picked = jnp.concatenate([cols[:, :, 0:4], cols[:, :, ROWS - 4 :]], axis=2)
        return picked.transpose(2, 1, 0)

    strip = jnp.concatenate([beside(west), strip, beside(east)], axis=2)
    strip = jnp.pad(strip, ((0, 0), (0, 0), (0, PAD - COLS - 4)))
    south = shift_gy(strip[6:8], 1)
    north = shift_gy(strip[0:2], -1)
    tops = to_all_gx(strip[6:8])
    ocean_strip = jnp.concatenate([south, strip, north], axis=0)

    coarse, ccols = coarse_sums(in_rows, incoming.reshape(DEV * CAP, FLD, 128))
    cwest = shift_gx(ccols[1], 1)
    ceast = shift_gx(ccols[0], -1)

    def pick(c):
        return jnp.concatenate([c[:, 0:2], c[:, HALF - 2 : HALF]], axis=1).T[:, :, None]

    cstrip = jnp.concatenate([coarse[0:2], coarse[HALF - 2 :]], axis=0)
    cstrip = jnp.concatenate([pick(cwest), cstrip, pick(ceast)], axis=2)
    cstrip = jnp.pad(cstrip, ((0, 0), (0, 0), (0, 126)))
    csouth = shift_gy(cstrip[3:4], 1)
    cnorth = shift_gy(cstrip[0:1], -1)
    ctops = to_all_gx(cstrip[3])
    coarse_strip = jnp.concatenate([csouth, cstrip, cnorth], axis=0)

    out = main_conv(
        ocean, land_mask, coarse, edges, west, east, ccols, cwest, ceast,
        w1b, w1t, b1c, w2b, w2l, w2r, b2c,
    )
    pos = jnp.stack([lax.axis_index("gy"), lax.axis_index("gx")]).astype(I32)
    return patch_rows(
        pos, fold_pair, ocean_strip, coarse_strip, tops, ctops, w1, b1[:, None], w2, b2c, out
    )


def solution(mesh):
    return jax.shard_map(
        per_device,
        mesh=mesh,
        in_specs=(
            P("gy", None, "gx"),
            P(("gy", "gx"), None, None),
            P(("gy", "gx"), None),
            P(("gy", "gx")),
            P(("gy", "gx")),
            P("gy", "gx"),
            P(),
            P(),
            P(),
            P(),
            P(),
        ),
        out_specs=P("gy", None, "gx"),
        check_vma=False,
    )
```

time: 836 us -> 163 us (0.19); the launches traced: 821 us -> 162 us
  matrix products: 397 us -> 0 us
  local copies, waits for them, and re-layouts: 232 us -> 16 us
  Pallas kernels: 0 us -> 82.2 us
  other arithmetic: 82.2 us -> 2.96 us
  blocking collectives: 43.6 us -> 0 us
  loops' own time: 15.5 us -> 0 us
  starting transfers between devices: 43.1 us -> 53.1 us
    dot_general x217 -> x0, matrix products: 397 us -> none  [the longest x216 396 us: block_out(): jnp.einsum('oc,ycx->yox', weight[shift_y, shift_x], piece[shift_y:shift_y...]
    pallas_call x0 -> x5, Pallas kernels: none -> 82.2 us  [the longest x1 41.7 us: main_conv(): pl.pallas_call(main_kernel, out_shape=jax.ShapeDtypeStruct((ROWS, OUT, CO...]
    while x3 -> x0, local copies, waits for them, and re-layouts: 67.8 us -> none  [convolve(): lax.map(lambda number: block_out(number * row_block, row_block), jnp.aran...]
    concatenate x3 -> x5, other arithmetic: 50.6 us -> 1.64 us  [the longest x1 0.77 us: per_device(): ocean_strip = jnp.concatenate([south, strip, north], axis=0)]
    scatter x3 -> x11, local copies, waits for them, and re-layouts: 47.8 us -> 0.47 us  [the longest x4 0.34 us: per_device(): w1b = w1b.at[r, :, r:r + 3].set(w1.transpose(2, 0, 1, 3))]
    all_gather x2 -> x0, blocking collectives: 43.6 us -> none  [the longest x1 21.9 us: per_device(): gathered_hidden = lax.all_gather(top_hidden, 'gx', axis=1, tiled=True)]
    concatenate x1 -> x0, local copies, waits for them, and re-layouts: 33 us -> none  [with_halo(): shard = jnp.concatenate([before, shard, after], axis=dim)]
    mul x13 -> x2, other arithmetic: 25 us -> 0.01 us  [the longest x1 0.01 us: per_device(): strip = jnp.concatenate([strip * strip_mask, strip_mask], axis=1)]
  transfers between devices with their start and end apart: 10 -> 12, of which waited for: 4 -> 3; matrix products, arithmetic and copies ran while one was open for 10% -> 10% of each run, Pallas kernels for 0% -> 35%
where the time goes in v1:
time: 163 us; the launch traced here: 162 us
  Pallas kernels  82.2 us (50%)
  starting transfers between devices  53.1 us (33%)
  local copies, waits for them, and re-layouts  16 us (10%)
  waiting for transfers between devices  7.29 us (4%)
  other arithmetic  2.96 us (2%)
    pallas_call x1, Pallas kernels, main_conv(): pl.pallas_call(main_kernel, out_shape=jax.ShapeDtypeStruct((ROWS, OUT, CO...  41.7 us
    pallas_call x1, Pallas kernels, edge_columns(): pl.pallas_call(edge_kernel, out_shape=jax.ShapeDtypeStruct((4, 2 * FLD, R...  21.3 us
    ppermute x4, starting transfers between devices, shift_gy(): lax.ppermute(x, 'gy', [(i, i + step) for i in range(n) if 0 <= i + step <...  18.9 us
    all_to_all x2, starting transfers between devices, to_all_gx(): lax.all_to_all(jnp.broadcast_to(x[None], (n,) + x.shape), 'gx', split_axi...  11.5 us
    all_to_all x1, starting transfers between devices, per_device(): lax.all_to_all(out_rows, ('gy', 'gx'), split_axis=0, concat_axis=0, tiled...  9.87 us
    pallas_call x1, Pallas kernels, coarse_sums(): pl.pallas_call(coarse_kernel, out_shape=(jax.ShapeDtypeStruct((HALF, FLD,...  8.08 us
    all_to_all x1, starting transfers between devices, per_device(): lax.all_to_all(outgoing.reshape(DEV, CAP, FLD, 128), ('gy', 'gx'), split_...  7.46 us
    pallas_call x1, Pallas kernels, pack(): pl.pallas_call(pack_kernel, out_shape=(jax.ShapeDtypeStruct((DEV * CAP, F...  6.67 us
  transfers between devices with their start and end apart: 12, of which 3 were waited for; matrix products, arithmetic and copies ran while one was open for 10% of the time, Pallas kernels for 35%

profile of v1, /device:TPU:66, one launch (start us, length us, event | category | flops | bytes accessed | tf_op | source)
XLA Modules:
  0.0 161.9 jit_solution(15392539576639492873)
XLA Ops:
  0.0 21.3 %edges.1.own_ref = bf16[4,32,384]{2,1,0:T(8,128)(2,1)} custom-call(bf16[384,16,256]{2,1,0:T(8,128)(2,1)} %ocean_ref.3, s32[384,256]{1,0:T(8,128)} %mask_ref.3), custom_call_target="tpu_custom_call" | custom-call | tf_op jit(solution)/shard_map/edges/pallas_call | solution.py:153
  21.3 0.8 fusion.18
  22.3 2.6 %collective-permute-start.1 = (bf16[2,32,384]{2,1,0:T(8,128)(2,1)S(1)}, bf16[2,32,384]{2,1,0:T(8,128)(2,1)S(1)}, u32[]{:S(2)}, u32[]{:S(2)}) collective-permute-start(bf16[2,32,384]{2,1,0:T(8,128)(2,1)S(1)} %get-tuple-element.130), channel_id=1, source_target_pairs={{0,15},{1,0},{2,1},{3,2},{4,3},{5,4},{6,5},{7,6},{8,7},{9,8},{10,9... | collective-permute-start | bytes 147464 | tf_op jit(solution)/shard_map/ppermute | solution.py:435
  25.5 6.7 %pack.1 = (bf16[384,16,128]{2,1,0:T(8,128)(2,1)}, s32[128,3]{1,0:T(8,128)}) custom-call(s32[192]{0:T(256)} %compare_select_fusion.code_ref, bf16[192,16,128]{2,1,0:T(8,128)(2,1)} %atm_ref.1), custom_call_target="tpu_custom_call" | custom-call | tf_op jit(solution)/shard_map/pack/pallas_call | solution.py:58
  32.2 9.9 %all-to-all-start = ((s32[128,1,3]{2,1,0:T(1,128)}), s32[128,1,3]{2,1,0:T(1,128)S(1)}, u32[]{:S(2)}, u32[]{:S(2)}) async-start(s32[128,1,3]{2,1,0:T(1,128)} %bitcast.62), calls=%async_computation | async-start | bytes 131072 | tf_op jit(solution)/shard_map/all_to_all | solution.py:458
  42.1 0.8 fusion.14
  43.0 5.7 %all-to-all-done = s32[128,1,3]{2,1,0:T(1,128)S(1)} async-done(((s32[128,1,3]{2,1,0:T(1,128)}), s32[128,1,3]{2,1,0:T(1,128)S(1)}, u32[]{:S(2)}, u32[]{:S(2)}) %all-to-all-start) | async-done | bytes 1568 | tf_op jit(solution)/shard_map/all_to_all | solution.py:458
  49.4 7.5 %all-to-all-start.1 = ((bf16[128,3,16,128]{3,2,1,0:T(8,128)(2,1)}), bf16[128,3,16,128]{3,2,1,0:T(8,128)(2,1)S(1)}, u32[]{:S(2)}, u32[]{:S(2)}) async-start(bf16[128,3,16,128]{3,2,1,0:T(8,128)(2,1)} %bitcast.59), calls=%async_computation.1 | async-start | bytes 3145728 | tf_op jit(solution)/shard_map/all_to_all | solution.py:455
  57.6 0.8 copy.92.w1_ref
  58.4 0.7 reshape.415.w2l_ref
  59.1 0.7 reshape.416.w2r_ref
  60.5 0.9 reshape.414.w2_ref
  62.0 0.8 copy.88.w1_ref
  62.8 0.8 broadcast_in_dim_tile.4.b1_ref
  63.5 0.7 copy.89.w1t_ref
  64.3 0.7 copy.93.b1_ref
  66.8 3.4 %collective-permute-start.2 = (bf16[2,32,384]{2,1,0:T(8,128)(2,1)S(1)}, bf16[2,32,384]{2,1,0:T(8,128)(2,1)S(1)}, u32[]{:S(2)}, u32[]{:S(2)}) collective-permute-start(bf16[2,32,384]{2,1,0:T(8,128)(2,1)S(1)} %get-tuple-element.125), channel_id=1, source_target_pairs={{0,16},{16,32},{32,48},{48,64},{64,80},{80,96},{96,112},{1,17},{17... | collective-permute-start | bytes 147464 | tf_op jit(solution)/shard_map/ppermute | solution.py:440
  70.2 6.0 %collective-permute-start.3 = (bf16[2,32,384]{2,1,0:T(8,128)(2,1)S(1)}, bf16[2,32,384]{2,1,0:T(8,128)(2,1)S(1)}, u32[]{:S(2)}, u32[]{:S(2)}) collective-permute-start(bf16[2,32,384]{2,1,0:T(8,128)(2,1)S(1)} %get-tuple-element.126), channel_id=1, source_target_pairs={{16,0},{32,16},{48,32},{64,48},{80,64},{96,80},{112,96},{17,1},{33... | collective-permute-start | bytes 147464 | tf_op jit(solution)/shard_map/ppermute | solution.py:440
  76.2 1.0 all-to-all-done.1
  77.2 1.1 broadcast_in_dim.41
  78.3 5.9 %all-to-all-start.2 = ((bf16[16,2,32,384]{3,2,1,0:T(8,128)(2,1)}), bf16[16,2,32,384]{3,2,1,0:T(8,128)(2,1)S(1)}, u32[]{:S(2)}, u32[]{:S(2)}) async-start(bf16[16,2,32,384]{3,2,1,0:T(8,128)(2,1)} %broadcast_in_dim.41), calls=%async_computation.2 | async-start | bytes 1572864 | tf_op jit(solution)/shard_map/all_to_all | solution.py:445
  84.2 8.1 %coarse.1 = (bf16[192,16,128]{2,1,0:T(8,128)(2,1)}, bf16[2,16,256]{2,1,0:T(8,128)(2,1)}) custom-call(s32[128,3]{1,0:T(8,128)} %bitcast.61, bf16[384,16,128]{2,1,0:T(8,128)(2,1)} %bitcast.56), custom_call_target="tpu_custom_call" | custom-call | tf_op jit(solution)/shard_map/coarse/pallas_call | solution.py:108
  92.3 0.7 slice_bitcast_fusion.1
  93.2 2.5 %collective-permute-start.5 = (bf16[16,256]{1,0:T(8,128)(2,1)S(1)}, bf16[16,256]{1,0:T(8,128)(2,1)S(1)}, u32[]{:S(2)}, u32[]{:S(2)}) collective-permute-start(bf16[16,256]{1,0:T(8,128)(2,1)S(1)} %get-tuple-element.141), channel_id=1, source_target_pairs={{0,15},{1,0},{2,1},{3,2},{4,3},{5,4},{6,5},{7,6},{8,7},{9,8},{10,9... | collective-permute-start | bytes 24584 | tf_op jit(solution)/shard_map/ppermute | solution.py:435
  95.7 0.7 fusion.15
  97.9 2.7 %collective-permute-start.6 = (bf16[1,16,256]{2,1,0:T(8,128)(2,1)S(1)}, bf16[1,16,256]{2,1,0:T(8,128)(2,1)S(1)}, u32[]{:S(2)}, u32[]{:S(2)}) collective-permute-start(bf16[1,16,256]{2,1,0:T(8,128)(2,1)S(1)} %get-tuple-element.137), channel_id=1, source_target_pairs={{0,16},{16,32},{32,48},{48,64},{64,80},{80,96},{96,112},{1,17},{17... | collective-permute-start | bytes 24584 | tf_op jit(solution)/shard_map/ppermute | solution.py:440
  100.6 6.7 %collective-permute-start.7 = (bf16[1,16,256]{2,1,0:T(8,128)(2,1)S(1)}, bf16[1,16,256]{2,1,0:T(8,128)(2,1)S(1)}, u32[]{:S(2)}, u32[]{:S(2)}) collective-permute-start(bf16[1,16,256]{2,1,0:T(8,128)(2,1)S(1)} %get-tuple-element.136), channel_id=1, source_target_pairs={{16,0},{32,16},{48,32},{64,48},{80,64},{96,80},{112,96},{17,1},{33... | collective-permute-start | bytes 24584 | tf_op jit(solution)/shard_map/ppermute | solution.py:440
  107.4 0.7 broadcast_in_dim.43
  108.1 5.6 %all-to-all-start.3 = ((bf16[16,16,256]{2,1,0:T(8,128)(2,1)}), bf16[16,16,256]{2,1,0:T(8,128)(2,1)S(1)}, u32[]{:S(2)}, u32[]{:S(2)}) async-start(bf16[16,16,256]{2,1,0:T(8,128)(2,1)} %broadcast_in_dim.43), calls=%async_computation.3 | async-start | bytes 262144 | tf_op jit(solution)/shard_map/all_to_all | solution.py:445
  113.8 0.8 pad_maximum_fusion.ocean_ref
  114.6 41.7 %convs.1.main_ref = bf16[384,8,256]{2,1,0:T(8,128)(2,1)} custom-call(bf16[384,16,256]{2,1,0:T(8,128)(2,1)} %ocean_ref.3, s32[384,256]{1,0:T(8,128)} %mask_ref.3, bf16[192,16,128]{2,1,0:T(8,128)(2,1)} %get-tuple-element.120.coarse_ref, bf16[4,32,384]{2,1,0:T(8,128)(2,1)} %edges.1.own_ref, bf16[2,32,384]{2,1,0:T(8,128)(2,1)} %copy-done.7, ...), custom_call_target="tpu_custom_call" | custom-call | tf_op jit(solution)/shard_map/convs/pallas_call | solution.py:265
  157.6 4.4 %patch.1 = bf16[384,8,256]{2,1,0:T(8,128)(2,1)} custom-call(s32[2]{0:T(128)} %pad_add_fusion.pos_ref, s32[16]{0:T(128)} %fold_ref.1, bf16[12,32,384]{2,1,0:T(8,128)(2,1)} %pad_maximum_fusion.ocean_ref, bf16[6,16,256]{2,1,0:T(8,128)(2,1)} %pad_maximum_fusion.1.coarse_ref, bf16[16,2,32,384]{3,2,1,0:T(8,128)(2,1)} %copy-done.2, ...), custom_call_target="tpu_custom_call", output_to_operand_aliasing={{}: (10, {})} | custom-call | tf_op jit(solution)/shard_map/patch/pallas_call | solution.py:417
  (91 shorter events, 8.2 us)
Async XLA Ops:
  0.0 42.1 %copy-start.1 = (s32[384,256]{1,0:T(8,128)S(1)}, s32[384,256]{1,0:T(8,128)}, u32[]{:S(2)}) copy-start(s32[384,256]{1,0:T(8,128)} %mask_ref.3) | copy-start | bytes 1179652
  0.0 24.9 %copy-start.12 = (s32[192,1]{0,1:T(1,128)S(1)}, s32[192,1]{0,1:T(1,128)}, u32[]{:S(2)}) copy-start(s32[192,1]{0,1:T(1,128)} %param.31) | copy-start | bytes 2308
  0.0 24.9 %copy-start.14 = (s32[192]{0:T(256)S(1)}, s32[192]{0:T(256)}, u32[]{:S(2)}) copy-start(s32[192]{0:T(256)} %param.32) | copy-start | bytes 2308
  0.0 24.9 %copy-start.13 = (s32[192]{0:T(256)S(1)}, s32[192]{0:T(256)}, u32[]{:S(2)}) copy-start(s32[192]{0:T(256)} %param.33) | copy-start | bytes 2308
  21.3 21.5 %copy-start.4 = (bf16[3,3,8,64]{3,2,1,0:T(8,128)(2,1)S(1)}, bf16[3,3,8,64]{3,2,1,0:T(8,128)(2,1)}, u32[]{:S(2)}) copy-start(bf16[3,3,8,64]{3,2,1,0:T(8,128)(2,1)} %w2_ref.1) | copy-start | bytes 27652
  22.2 42.8 %collective-permute-start = (bf16[2,32,384]{2,1,0:T(8,128)(2,1)S(1)}, bf16[2,32,384]{2,1,0:T(8,128)(2,1)S(1)}, u32[]{:S(2)}, u32[]{:S(2)}) collective-permute-start(bf16[2,32,384]{2,1,0:T(8,128)(2,1)S(1)} %get-tuple-element.129), channel_id=1, source_target_pairs={{0,1},{1,2},{2,3},{3,4},{4,5},{5,6},{6,7},{7,8},{8,9},{9,10},{10,1... | collective-permute-start | bytes 147464 | tf_op jit(solution)/shard_map/ppermute | solution.py:435
  22.3 43.5 %collective-permute-start.1 = (bf16[2,32,384]{2,1,0:T(8,128)(2,1)S(1)}, bf16[2,32,384]{2,1,0:T(8,128)(2,1)S(1)}, u32[]{:S(2)}, u32[]{:S(2)}) collective-permute-start(bf16[2,32,384]{2,1,0:T(8,128)(2,1)S(1)} %get-tuple-element.130), channel_id=1, source_target_pairs={{0,15},{1,0},{2,1},{3,2},{4,3},{5,4},{6,5},{7,6},{8,7},{9,8},{10,9... | collective-permute-start | bytes 147464 | tf_op jit(solution)/shard_map/ppermute | solution.py:435
  32.2 16.6 %all-to-all-start = ((s32[128,1,3]{2,1,0:T(1,128)}), s32[128,1,3]{2,1,0:T(1,128)S(1)}, u32[]{:S(2)}, u32[]{:S(2)}) async-start(s32[128,1,3]{2,1,0:T(1,128)} %bitcast.62), calls=%async_computation | async-start | bytes 131072 | tf_op jit(solution)/shard_map/all_to_all | solution.py:458
  48.7 0.6 copy-start.6
  48.7 8.1 %copy-start.3 = (bf16[3,3,64,32]{2,3,1,0:T(8,128)(2,1)S(1)}, bf16[3,3,64,32]{2,3,1,0:T(8,128)(2,1)}, u32[]{:S(2)}) copy-start(bf16[3,3,64,32]{2,3,1,0:T(8,128)(2,1)} %param.36) | copy-start | bytes 110596
  48.7 11.0 %copy-start.15 = (f32[8]{0:T(128)S(1)}, f32[8]{0:T(128)}, u32[]{:S(2)}) copy-start(f32[8]{0:T(128)} %param.39) | copy-start | bytes 100
  49.4 27.8 %all-to-all-start.1 = ((bf16[128,3,16,128]{3,2,1,0:T(8,128)(2,1)}), bf16[128,3,16,128]{3,2,1,0:T(8,128)(2,1)S(1)}, u32[]{:S(2)}, u32[]{:S(2)}) async-start(bf16[128,3,16,128]{3,2,1,0:T(8,128)(2,1)} %bitcast.59), calls=%async_computation.1 | async-start | bytes 3145728 | tf_op jit(solution)/shard_map/all_to_all | solution.py:455
  58.4 4.4 %copy-start.11 = (f32[64]{0:T(128)S(1)}, f32[64]{0:T(128)}, u32[]{:S(2)}) copy-start(f32[64]{0:T(128)} %param.37) | copy-start | bytes 772
  65.0 13.4 %copy-start.7 = (bf16[2,32,384]{2,1,0:T(8,128)(2,1)}, bf16[2,32,384]{2,1,0:T(8,128)(2,1)S(1)}, u32[]{:S(2)}) copy-start(bf16[2,32,384]{2,1,0:T(8,128)(2,1)S(1)} %collective-permute-done.west_ref) | copy-start | bytes 147460
  65.8 12.6 %copy-start.8 = (bf16[2,32,384]{2,1,0:T(8,128)(2,1)}, bf16[2,32,384]{2,1,0:T(8,128)(2,1)S(1)}, u32[]{:S(2)}) copy-start(bf16[2,32,384]{2,1,0:T(8,128)(2,1)S(1)} %collective-permute-done.1.east_ref) | copy-start | bytes 147460
  66.8 47.0 %collective-permute-start.2 = (bf16[2,32,384]{2,1,0:T(8,128)(2,1)S(1)}, bf16[2,32,384]{2,1,0:T(8,128)(2,1)S(1)}, u32[]{:S(2)}, u32[]{:S(2)}) collective-permute-start(bf16[2,32,384]{2,1,0:T(8,128)(2,1)S(1)} %get-tuple-element.125), channel_id=1, source_target_pairs={{0,16},{16,32},{32,48},{48,64},{64,80},{80,96},{96,112},{1,17},{17... | collective-permute-start | bytes 147464 | tf_op jit(solution)/shard_map/ppermute | solution.py:440
  70.2 43.6 %collective-permute-start.3 = (bf16[2,32,384]{2,1,0:T(8,128)(2,1)S(1)}, bf16[2,32,384]{2,1,0:T(8,128)(2,1)S(1)}, u32[]{:S(2)}, u32[]{:S(2)}) collective-permute-start(bf16[2,32,384]{2,1,0:T(8,128)(2,1)S(1)} %get-tuple-element.126), channel_id=1, source_target_pairs={{16,0},{32,16},{48,32},{64,48},{80,64},{96,80},{112,96},{17,1},{33... | collective-permute-start | bytes 147464 | tf_op jit(solution)/shard_map/ppermute | solution.py:440
  77.2 7.0 %copy-start = (bf16[128,3,16,128]{3,2,1,0:T(8,128)(2,1)}, bf16[128,3,16,128]{3,2,1,0:T(8,128)(2,1)S(1)}, u32[]{:S(2)}) copy-start(bf16[128,3,16,128]{3,2,1,0:T(8,128)(2,1)S(1)} %all-to-all-done.1) | copy-start | bytes 4718596
  78.3 29.1 %all-to-all-start.2 = ((bf16[16,2,32,384]{3,2,1,0:T(8,128)(2,1)}), bf16[16,2,32,384]{3,2,1,0:T(8,128)(2,1)S(1)}, u32[]{:S(2)}, u32[]{:S(2)}) async-start(bf16[16,2,32,384]{3,2,1,0:T(8,128)(2,1)} %broadcast_in_dim.41), calls=%async_computation.2 | async-start | bytes 1572864 | tf_op jit(solution)/shard_map/all_to_all | solution.py:445
  93.0 4.0 %collective-permute-start.4 = (bf16[16,256]{1,0:T(8,128)(2,1)S(1)}, bf16[16,256]{1,0:T(8,128)(2,1)S(1)}, u32[]{:S(2)}, u32[]{:S(2)}) collective-permute-start(bf16[16,256]{1,0:T(8,128)(2,1)S(1)} %get-tuple-element.140), channel_id=1, source_target_pairs={{0,1},{1,2},{2,3},{3,4},{4,5},{5,6},{6,7},{7,8},{8,9},{9,10},{10,1... | collective-permute-start | bytes 24584 | tf_op jit(solution)/shard_map/ppermute | solution.py:435
  93.2 4.2 %collective-permute-start.5 = (bf16[16,256]{1,0:T(8,128)(2,1)S(1)}, bf16[16,256]{1,0:T(8,128)(2,1)S(1)}, u32[]{:S(2)}, u32[]{:S(2)}) collective-permute-start(bf16[16,256]{1,0:T(8,128)(2,1)S(1)} %get-tuple-element.141), channel_id=1, source_target_pairs={{0,15},{1,0},{2,1},{3,2},{4,3},{5,4},{6,5},{7,6},{8,7},{9,8},{10,9... | collective-permute-start | bytes 24584 | tf_op jit(solution)/shard_map/ppermute | solution.py:435
  97.0 17.6 %copy-start.9 = (bf16[16,256]{1,0:T(8,128)(2,1)}, bf16[16,256]{1,0:T(8,128)(2,1)S(1)}, u32[]{:S(2)}) copy-start(bf16[16,256]{1,0:T(8,128)(2,1)S(1)} %collective-permute-done.4.cwest_ref) | copy-start | bytes 24580
  97.4 17.2 %copy-start.10 = (bf16[16,256]{1,0:T(8,128)(2,1)}, bf16[16,256]{1,0:T(8,128)(2,1)S(1)}, u32[]{:S(2)}) copy-start(bf16[16,256]{1,0:T(8,128)(2,1)S(1)} %collective-permute-done.5.ceast_ref) | copy-start | bytes 24580
  97.9 58.4 %collective-permute-start.6 = (bf16[1,16,256]{2,1,0:T(8,128)(2,1)S(1)}, bf16[1,16,256]{2,1,0:T(8,128)(2,1)S(1)}, u32[]{:S(2)}, u32[]{:S(2)}) collective-permute-start(bf16[1,16,256]{2,1,0:T(8,128)(2,1)S(1)} %get-tuple-element.137), channel_id=1, source_target_pairs={{0,16},{16,32},{32,48},{48,64},{64,80},{80,96},{96,112},{1,17},{17... | collective-permute-start | bytes 24584 | tf_op jit(solution)/shard_map/ppermute | solution.py:440
  100.6 55.7 %collective-permute-start.7 = (bf16[1,16,256]{2,1,0:T(8,128)(2,1)S(1)}, bf16[1,16,256]{2,1,0:T(8,128)(2,1)S(1)}, u32[]{:S(2)}, u32[]{:S(2)}) collective-permute-start(bf16[1,16,256]{2,1,0:T(8,128)(2,1)S(1)} %get-tuple-element.136), channel_id=1, source_target_pairs={{16,0},{32,16},{48,32},{64,48},{80,64},{96,80},{112,96},{17,1},{33... | collective-permute-start | bytes 24584 | tf_op jit(solution)/shard_map/ppermute | solution.py:440
  107.4 48.9 %copy-start.2 = (bf16[16,2,32,384]{3,2,1,0:T(8,128)(2,1)}, bf16[16,2,32,384]{3,2,1,0:T(8,128)(2,1)S(1)}, u32[]{:S(2)}) copy-start(bf16[16,2,32,384]{3,2,1,0:T(8,128)(2,1)S(1)} %all-to-all-done.2.tops_ref) | copy-start | bytes 2359300
  108.1 48.8 %all-to-all-start.3 = ((bf16[16,16,256]{2,1,0:T(8,128)(2,1)}), bf16[16,16,256]{2,1,0:T(8,128)(2,1)S(1)}, u32[]{:S(2)}, u32[]{:S(2)}) async-start(bf16[16,16,256]{2,1,0:T(8,128)(2,1)} %broadcast_in_dim.43), calls=%async_computation.3 | async-start | bytes 262144 | tf_op jit(solution)/shard_map/all_to_all | solution.py:445
  156.9 0.6 copy-start.5

commit v2 on v1

v2 whole, which is shorter than its diff:
```python
import functools

import jax
import jax.numpy as jnp
from jax import lax
from jax.experimental import pallas as pl
from jax.experimental.pallas import tpu as pltpu
from jax.sharding import PartitionSpec as P

BF = jnp.bfloat16
F32 = jnp.float32
I32 = jnp.int32
VMEM_LIMIT = 56 << 20
ROWS = 384
COLS = 256
HALF = 192
DEV = 128
CAP = 3
FLD = 16
HID = 64
OUT = 8
PAD = 384
SHIFT = 2


def lanes(shape):
    return lax.broadcasted_iota(I32, shape, len(shape) - 1)


def subs(shape):
    return lax.broadcasted_iota(I32, shape, len(shape) - 2)


STEP = 2 * CAP + 1


def pack_kernel(info_ref, row_ref, atm_ref, out_ref, q_ref):
    lane = lanes((FLD, 128))
    first, last = [], []
    for chunk, count in ((0, 128), (128, 64)):

        def place(i, carry):
            c0, c1 = carry
            n = chunk + i
            code = info_ref[0, n]
            block = atm_ref[pl.ds(2 * n, 2)]
            out_ref[pl.ds(STEP * (code >> 2) + 2 * (code & 3), 2)] = block
            block = block.reshape(FLD, 128)
            here = lane == i
            c0 = jnp.where(here, pltpu.roll(block, i, 1), c0)
            c1 = jnp.where(here, pltpu.roll(block, i + 1, 1), c1)
            return c0, c1

        zero = jnp.zeros((FLD, 128), BF)
        c0, c1 = lax.fori_loop(0, count, place, (zero, zero), unroll=16)
        first.append(c0)
        last.append(c1)
    values = [jnp.concatenate(last, axis=1), jnp.concatenate(first, axis=1)]
    code = jnp.broadcast_to(row_ref[0:1, :], (DEV, 256))
    row = row_ref[1:2, :].astype(F32).astype(BF)
    total = jnp.zeros((DEV, 128), F32)
    tile = subs((DEV, 256))
    none = jnp.zeros((FLD, 256), BF)
    for k in range(CAP):
        hit = (code == 4 * tile + k).astype(BF)
        rows = jnp.where(subs((FLD, 256)) == k, jnp.broadcast_to(row, (FLD, 256)), none)
        parts = [rows] + [values[0] if i == k else none for i in range(3)]
        parts = parts + [values[1] if i == k else none for i in range(3)] + [none]
        total = total + lax.dot_general(
            hit, jnp.concatenate(parts, axis=0), (((1,), (1,)), ((), ())), preferred_element_type=F32
        )
    q_ref[...] = total
    sub = subs((8, 128))

    def head(t, carry):
        near = (t & -16) + ((t + 15) & 15)
        far = (t & -16) + ((t + 1) & 15)
        own, west, east = [
            jnp.broadcast_to(q_ref[pl.ds(i, 1), :], (8, 128)) for i in (t, near, far)
        ]
        out_ref[STEP * t + STEP - 1] = jnp.where(sub == 0, own, jnp.where(sub == 1, west, east)).astype(BF)
        return carry

    lax.fori_loop(0, DEV, head, 0, unroll=16)


def pack(info, atm):
    return pl.pallas_call(
        pack_kernel,
        out_shape=jax.ShapeDtypeStruct((DEV * STEP, 8, 128), BF),
        in_specs=[
            pl.BlockSpec(memory_space=pltpu.SMEM),
            pl.BlockSpec(memory_space=pltpu.VMEM),
            pl.BlockSpec(memory_space=pltpu.VMEM),
        ],
        out_specs=pl.BlockSpec(memory_space=pltpu.VMEM),
        scratch_shapes=[pltpu.VMEM((DEV, 128), F32)],
        name="pack",
    )(info, info, atm)


def coarse_kernel(
    inc_ref, strip_ref, out_ref, cols_ref, west_ref, east_ref, low_ref, mid_ref, top_ref, tops_ref,
    acc_ref, head_ref, idx_ref, where_ref, sem,
):
    few = lanes((8, 128)) < CAP
    for g in range(4):

        def gather(s, total):
            head = inc_ref[STEP * (32 * g + s) + STEP - 1].astype(F32)
            head_ref[32 * g + s] = head
            return total + pltpu.roll(jnp.where(few, head, 0.0), 4 * s, 1)

        idx_ref[g] = lax.fori_loop(0, 32, gather, jnp.zeros((8, 128), F32), unroll=32).astype(I32)
    copy = pltpu.make_async_copy(idx_ref, where_ref, sem)
    copy.start()
    acc_ref[...] = jnp.zeros_like(acc_ref)
    copy.wait()
    for g in range(4):

        def add(s, carry):
            for k in range(CAP):
                r = where_ref[g, 0, 4 * s + k]
                block = inc_ref[pl.ds(STEP * (32 * g + s) + 2 * k, 2)]
                acc_ref[k, r] = acc_ref[k, r] + block.astype(F32)
            return carry

        lax.fori_loop(0, 32, add, 0, unroll=8)
    lane = lanes((FLD, 128))

    def finish(r, carry):
        total = acc_ref[0, r + 1] + acc_ref[1, r + 1] + acc_ref[2, r + 1]
        out_ref[r] = total.reshape(FLD, 128).astype(BF)
        return carry

    lax.fori_loop(0, HALF, finish, 0, unroll=16)
    target = (lanes((DEV, 256)) + 1).astype(F32)
    for j, wanted in (
        (0, ((4 * FLD, cols_ref.at[0]), (FLD, cols_ref.at[1]))),
        (1, ((FLD, west_ref),)),
        (2, ((4 * FLD, east_ref),)),
    ):
        heads = head_ref[:, j, :]
        turned = heads.T.astype(BF)
        hits = [
            (jnp.broadcast_to(heads[:, k : k + 1], (DEV, 256)) == target).astype(BF) for k in range(CAP)
        ]
        for first, ref in wanted:
            total = jnp.zeros((FLD, 256), F32)
            for k in range(CAP):
                at = first + FLD * k
                total = total + jnp.dot(turned[at : at + FLD], hits[k], preferred_element_type=F32)
            ref[...] = total.astype(BF)
    spread = (subs((256, PAD)) == lanes((256, PAD)) // 2).astype(BF)
    for k, r in enumerate((0, 1, HALF - 2, HALF - 1)):
        chunk, i = (r // 128) * 128, r % 128
        west = pltpu.roll(west_ref[:, chunk : chunk + 128].astype(F32), (128 - i) % 128, 1)
        east = pltpu.roll(east_ref[:, chunk : chunk + 128].astype(F32), (129 - i) % 128, 1)
        row = pltpu.roll(out_ref[r].astype(F32), 1, 1)
        wide = jnp.concatenate(
            [
                jnp.where(lane == 0, west, row),
                jnp.where(lane == 0, row, jnp.where(lane == 1, east, 0.0)),
            ],
            axis=1,
        ).astype(BF)
        fine = jnp.dot(wide, spread, preferred_element_type=F32).astype(BF)
        for h in range(2):
            n = 2 * k + h
            ref, at = ((low_ref, n), (mid_ref, n - 2), (mid_ref, n - 2), (top_ref, n - 6))[k]
            ref[at, 0:FLD, :] = strip_ref[n, 0:FLD, :]
            ref[at, FLD : 2 * FLD, :] = fine * strip_ref[n, FLD : 2 * FLD, :]
    for h in range(2):
        row = pltpu.roll(top_ref[h].astype(F32), PAD - SHIFT, 1)[:, :COLS].astype(BF)
        for t in range(16):
            tops_ref[t, h] = row


def coarse_sums(incoming, strip):
    return pl.pallas_call(
        coarse_kernel,
        out_shape=(
            jax.ShapeDtypeStruct((HALF, FLD, 128), BF),
            jax.ShapeDtypeStruct((2, FLD, 256), BF),
            jax.ShapeDtypeStruct((FLD, 256), BF),
            jax.ShapeDtypeStruct((FLD, 256), BF),
            jax.ShapeDtypeStruct((2, 2 * FLD, PAD), BF),
            jax.ShapeDtypeStruct((4, 2 * FLD, PAD), BF),
            jax.ShapeDtypeStruct((2, 2 * FLD, PAD), BF),
            jax.ShapeDtypeStruct((16, 2, 2 * FLD, COLS), BF),
        ),
        scratch_shapes=[
            pltpu.VMEM((CAP, HALF + 1, 2, 8, 128), F32),
            pltpu.VMEM((DEV, 8, 128), F32),
            pltpu.VMEM((4, 8, 128), I32),
            pltpu.SMEM((4, 8, 128), I32),
            pltpu.SemaphoreType.DMA,
        ],
        compiler_params=pltpu.CompilerParams(vmem_limit_bytes=24 << 20),
        name="coarse",
    )(incoming, strip)


def edge_kernel(ocean_ref, mask_ref, out_ref):
    lane = lanes((FLD, 128))
    for chunk in range(3):
        block = mask_ref[chunk * 128 : chunk * 128 + 128, :].astype(F32)
        m_left = block[:, :128].T
        m_right = block[:, 128:].T

        def take(i, carry):
            x = ocean_ref[chunk * 128 + i]
            left, right = x[:, :128], x[:, 128:]
            here = lane == i
            c0, c1, c2, c3 = carry
            c0 = jnp.where(here, pltpu.roll(left, i, 1), c0)
            c1 = jnp.where(here, pltpu.roll(left, i + 127, 1), c1)
            c2 = jnp.where(here, pltpu.roll(right, i + 2, 1), c2)
            c3 = jnp.where(here, pltpu.roll(right, i + 1, 1), c3)
            return c0, c1, c2, c3

        zero = jnp.zeros((FLD, 128), BF)
        got = lax.fori_loop(0, 128, take, (zero,) * 4, unroll=16)
        rows = (m_left[0:1], m_left[1:2], m_right[126:127], m_right[127:128])
        for k in range(4):
            m = jnp.broadcast_to(rows[k], (FLD, 128)).astype(BF)
            out_ref[k, :, chunk * 128 : chunk * 128 + 128] = jnp.concatenate([got[k] * m, m], axis=0)


def edge_columns(ocean, mask):
    return pl.pallas_call(
        edge_kernel,
        out_shape=jax.ShapeDtypeStruct((4, 2 * FLD, ROWS), BF),
        compiler_params=pltpu.CompilerParams(vmem_limit_bytes=24 << 20),
        name="edges",
    )(ocean, mask)


BLOCKS = 16


def banded(w_ref, dst_ref, first):
    dst_ref[...] = jnp.zeros_like(dst_ref)
    for r in range(3):
        for u in range(3):
            for v in range(3):
                at = ((r + u) * 3 + v) * FLD
                dst_ref[r * HID : r * HID + HID, at : at + FLD] = w_ref[u, v, :, first : first + FLD]


def ocean_kernel(
    ocean_ref, mask_ref, west_ref, east_ref, w_ref, b_ref, part_ref, m3_ref, strip_ref,
    xs_ref, h_ref, band_ref, sem,
):
    banded(w_ref, band_ref, 0)
    bias = jnp.concatenate([b_ref[...]] * 3, axis=0)
    lane = lanes((128, 128))
    for chunk in range(3):
        at = slice(chunk * 128, chunk * 128 + 128)
        m = mask_ref[at, :].astype(F32)
        up, down = pltpu.roll(m, 1, 1), pltpu.roll(m, COLS - 1, 1)
        west = jnp.broadcast_to(west_ref[1, FLD : FLD + 1, at].astype(F32), (128, 128)).T
        east = jnp.broadcast_to(east_ref[0, FLD : FLD + 1, at].astype(F32), (128, 128)).T
        m3_ref[0, at, 0:128] = jnp.where(lane == 0, west, up[:, :128])
        m3_ref[0, at, 128:256] = up[:, 128:]
        m3_ref[1, at, :] = m
        m3_ref[2, at, 0:128] = down[:, :128]
        m3_ref[2, at, 128:256] = jnp.where(lane == 127, east, down[:, 128:])

    lane16 = lanes((FLD, 128))
    zero = jnp.zeros((48, COLS), BF)
    xs_ref[0] = zero
    xs_ref[ROWS + 1] = zero

    def build(y):
        base = pl.multiple_of((y // 128) * 128, 128)
        i = y % 128
        m = jnp.broadcast_to(m3_ref[1, pl.ds(y, 1), :], (FLD, COLS)).astype(BF)
        x = ocean_ref[y] * m
        west = pltpu.roll(west_ref[1, 0:FLD, pl.ds(base, 128)], 128 - i, 1)
        east = pltpu.roll(east_ref[0, 0:FLD, pl.ds(base, 128)], 127 - i, 1)
        up, down = pltpu.roll(x, 1, 1), pltpu.roll(x, COLS - 1, 1)
        xs_ref[y + 1, 0:16, 0:128] = jnp.where(lane16 == 0, west, up[:, :128])
        xs_ref[y + 1, 0:16, 128:256] = up[:, 128:]
        xs_ref[y + 1, 16:32, :] = x
        xs_ref[y + 1, 32:48, 0:128] = down[:, :128]
        xs_ref[y + 1, 32:48, 128:256] = jnp.where(lane16 == 127, east, down[:, 128:])

    wide_lane = lanes((2 * FLD, 128))
    for n, y in enumerate((0, 1, 2, 3, ROWS - 4, ROWS - 3, ROWS - 2, ROWS - 1)):
        base, i = (y // 128) * 128, y % 128
        m = jnp.broadcast_to(m3_ref[1, y : y + 1, :], (FLD, COLS))
        x = jnp.concatenate([ocean_ref[y].astype(F32) * m, m], axis=0)
        x = jnp.concatenate([x, jnp.zeros((2 * FLD, 128), F32)], axis=1)
        x = pltpu.roll(x, SHIFT, 1)

        def beside(ref, k, lane_at):
            return pltpu.roll(ref[k, :, base : base + 128].astype(F32), (128 + lane_at - i) % 128, 1)

        lo = jnp.where(wide_lane == 0, beside(west_ref, 0, 0), x[:, 0:128])
        lo = jnp.where(wide_lane == 1, beside(west_ref, 1, 1), lo)
        hi = jnp.where(wide_lane == 2, beside(east_ref, 0, 2), x[:, 256:])
        hi = jnp.where(wide_lane == 3, beside(east_ref, 1, 3), hi)
        strip_ref[n, :, 0:128] = lo.astype(BF)
        strip_ref[n, :, 128:256] = x[:, 128:256].astype(BF)
        strip_ref[n, :, 256:384] = hi.astype(BF)

    def first(i, carry):
        build(i)
        return carry

    lax.fori_loop(0, 24, first, 0, unroll=8)

    def conv(block, carry):
        for k in range(8):
            g = block * 8 + k
            for r in range(3):
                build(jnp.minimum(3 * g + 24 + r, ROWS - 1))
            x = xs_ref[pl.ds(3 * g, 5)].reshape(240, COLS)
            t = jnp.dot(band_ref[...], x, preferred_element_type=F32) + bias
            h_ref[pl.ds(3 * g, 3)] = t.astype(BF).reshape(3, HID, COLS)
        at = pl.ds(block * 24, 24)
        pltpu.make_async_copy(h_ref.at[at], part_ref.at[at], sem.at[block]).start()
        return carry

    lax.fori_loop(0, BLOCKS, conv, 0)
    for block in range(BLOCKS):
        at = pl.ds(block * 24, 24)
        pltpu.make_async_copy(h_ref.at[at], part_ref.at[at], sem.at[block]).wait()


def ocean_part(ocean, mask, west, east, w1, b1):
    return pl.pallas_call(
        ocean_kernel,
        out_shape=(
            jax.ShapeDtypeStruct((ROWS, HID, COLS), BF),
            jax.ShapeDtypeStruct((3, ROWS, COLS), F32),
            jax.ShapeDtypeStruct((8, 2 * FLD, PAD), BF),
        ),
        out_specs=(
            pl.BlockSpec(memory_space=pl.ANY),
            pl.BlockSpec(memory_space=pltpu.VMEM),
            pl.BlockSpec(memory_space=pltpu.VMEM),
        ),
        scratch_shapes=[
            pltpu.VMEM((ROWS + 2, 48, COLS), BF),
            pltpu.VMEM((ROWS, HID, COLS), BF),
            pltpu.VMEM((192, 240), BF),
            pltpu.SemaphoreType.DMA((BLOCKS,)),
        ],
        compiler_params=pltpu.CompilerParams(vmem_limit_bytes=44 << 20),
        name="ocean",
    )(ocean, mask, west, east, w1, b1)


def main_kernel(
    part_ref, m3_ref, coarse_ref, own_ref, west_ref, east_ref, cown_ref, cwest_ref, ceast_ref,
    w1_ref, b1_ref, w2_ref, b2_ref, out_ref,
    cx_ref, fine_ref, p_ref, h_ref, add_ref, band1_ref, band2_ref, side1_ref, side2_ref, sem,
):
    def fetch(block):
        return pltpu.make_async_copy(
            part_ref.at[pl.ds(block * 24, 24)], p_ref.at[pl.ds(block * 24, 24)], sem.at[block]
        )

    for block in range(BLOCKS):
        fetch(block).start()

    banded(w1_ref, band1_ref, FLD)
    band2_ref[...] = jnp.zeros_like(band2_ref)
    for u in range(3):
        for v in range(3):
            w = w2_ref[u, v]
            for r in range(6):
                at = (r * 3 + v) * OUT
                band2_ref[at : at + OUT, (r + u) * HID : (r + u) * HID + HID] = w
            w1 = w1_ref[u, v]
            at = (u * 3 + v) * 2 * FLD
            side1_ref[:, at : at + 2 * FLD] = w1
        side2_ref[0, :, u * HID : u * HID + HID] = w2_ref[u, 0]
        side2_ref[1, :, u * HID : u * HID + HID] = w2_ref[u, 2]

    rep = (subs((256, ROWS)) == lanes((256, ROWS)) // 2).astype(BF)

    def column(coarse_t, strip):
        fine = jnp.dot(coarse_t, rep, preferred_element_type=F32)
        return jnp.concatenate([strip[:FLD], (fine * strip[FLD:].astype(F32)).astype(BF)], axis=0)

    w2c = column(cwest_ref[...], west_ref[0])
    w1c = column(cwest_ref[...], west_ref[1])
    o0c = column(cown_ref[0], own_ref[0])
    o255c = column(cown_ref[1], own_ref[3])
    e1c = column(ceast_ref[...], east_ref[0])
    e2c = column(ceast_ref[...], east_ref[1])
    for side, cols in ((0, (w2c, w1c, o0c)), (1, (o255c, e1c, e2c))):
        x = jnp.concatenate(cols, axis=0)
        xt = jnp.concatenate([pltpu.roll(x, 1, 1), x, pltpu.roll(x, ROWS - 1, 1)], axis=0)
        hid = jnp.dot(side1_ref[...], xt, preferred_element_type=F32)
        hid = jnp.maximum(hid + b1_ref[...], 0.0).astype(BF)
        ht = jnp.concatenate([pltpu.roll(hid, 1, 1), hid, pltpu.roll(hid, ROWS - 1, 1)], axis=0)
        add_ref[side] = jnp.dot(side2_ref[side], ht, preferred_element_type=F32)

    lane = lanes((FLD, 128))
    for chunk, count in ((0, 128), (128, 64)):

        def extend(i, carry):
            r = chunk + i
            west = pltpu.roll(cwest_ref[:, chunk : chunk + 128], 128 - i, 1)
            east = pltpu.roll(ceast_ref[:, chunk : chunk + 128], 129 - i, 1)
            cx_ref[r, :, 0:128] = coarse_ref[r]
            both = jnp.where(lane == 0, west, jnp.where(lane == 1, east, jnp.zeros_like(east)))
            cx_ref[r, :, 128:256] = both
            return carry

        lax.fori_loop(0, count, extend, 0, unroll=16)

    src, dst = subs((256, COLS)), lanes((256, COLS))
    spread = [
        (src == jnp.where(dst == 0, 128, (dst - 1) // 2)).astype(BF),
        (src == dst // 2).astype(BF),
        (src == jnp.where(dst == COLS - 1, 129, (dst + 1) // 2)).astype(BF),
    ]
    fine_ref[0] = jnp.zeros((48, COLS), BF)
    fine_ref[HALF + 1] = jnp.zeros((48, COLS), BF)

    def widen(k, carry):
        part = cx_ref[pl.ds(k * 16, 16)].reshape(256, 256)
        for v in range(3):
            fine = jnp.dot(part, spread[v], preferred_element_type=F32).astype(BF)
            fine_ref[pl.ds(k * 16 + 1, 16), 16 * v : 16 * v + 16, :] = fine.reshape(16, FLD, COLS)
        return carry

    lax.fori_loop(0, 12, widen, 0, unroll=2)

    hzero = jnp.zeros((HID, COLS), BF)
    h_ref[0] = hzero
    h_ref[ROWS + 1] = hzero

    def conv1(block):
        fetch(block).wait()
        for j in range(4):
            y0 = block * 24 + j * 6
            rows = []
            for i in range(8):
                y = y0 - 1 + i
                half = (block * 12 + j * 3) + (i + 1) // 2
                ym = y if 0 < i < 7 else jnp.clip(y, 0, ROWS - 1)
                for v in range(3):
                    m = jnp.broadcast_to(m3_ref[v, pl.ds(ym, 1), :], (FLD, COLS)).astype(BF)
                    rows.append(fine_ref[half, 16 * v : 16 * v + 16, :] * m)
            for k in range(2):
                x = jnp.concatenate(rows[9 * k : 9 * k + 15], axis=0)
                t = jnp.dot(band1_ref[...], x, preferred_element_type=F32)
                t = t + p_ref[pl.ds(y0 + 3 * k, 3)].reshape(192, COLS).astype(F32)
                h_ref[pl.ds(y0 + 3 * k + 1, 3)] = jnp.maximum(t, 0.0).astype(BF).reshape(3, HID, COLS)

    b2 = b2_ref[...]
    lane8 = lanes((OUT, 128))

    def conv2(first, count):
        for k in range(count):
            j = jnp.maximum(first + k, 0)
            x = h_ref[pl.ds(6 * j, 8)].reshape(512, COLS)
            t = jnp.dot(band2_ref[...], x, preferred_element_type=F32).reshape(6, 3, OUT, COLS)
            for r in range(6):
                y = 6 * j + r
                base = pl.multiple_of((y // 128) * 128, 128)
                i = y % 128
                west = pltpu.roll(add_ref[0, :, pl.ds(base, 128)], 128 - i, 1)
                east = pltpu.roll(add_ref[1, :, pl.ds(base, 128)], 127 - i, 1)
                up = pltpu.roll(t[r, 0], 1, 1)
                down = pltpu.roll(t[r, 2], COLS - 1, 1)
                mid = t[r, 1] + b2
                m = m3_ref[1, pl.ds(y, 1), :]
                lo = mid[:, :128] + jnp.where(lane8 == 0, west, up[:, :128]) + down[:, :128]
                hi = mid[:, 128:] + up[:, 128:] + jnp.where(lane8 == 127, east, down[:, 128:])
                out_ref[y, :, 0:128] = (lo * m[:, :128]).astype(BF)
                out_ref[y, :, 128:256] = (hi * m[:, 128:]).astype(BF)

    def both(block, carry):
        conv2(4 * block - 5, 4)
        conv1(block)
        return carry

    lax.fori_loop(0, BLOCKS, both, 0)
    conv2(4 * BLOCKS - 5, 5)


def main_conv(*args):
    vmem = pl.BlockSpec(memory_space=pltpu.VMEM)
    return pl.pallas_call(
        main_kernel,
        out_shape=jax.ShapeDtypeStruct((ROWS, OUT, COLS), BF),
        in_specs=[pl.BlockSpec(memory_space=pl.ANY)] + [vmem] * 12,
        scratch_shapes=[
            pltpu.VMEM((HALF, FLD, COLS), BF),
            pltpu.VMEM((HALF + 2, 48, COLS), BF),
            pltpu.VMEM((ROWS, HID, COLS), BF),
            pltpu.VMEM((ROWS + 2, HID, COLS), BF),
            pltpu.VMEM((2, OUT, ROWS), F32),
            pltpu.VMEM((192, 240), BF),
            pltpu.VMEM((144, 512), BF),
            pltpu.VMEM((HID, 288), BF),
            pltpu.VMEM((2, OUT, 192), BF),
            pltpu.SemaphoreType.DMA((BLOCKS,)),
        ],
        compiler_params=pltpu.CompilerParams(vmem_limit_bytes=44 << 20),
        name="convs",
    )(*args)


def onehot(pairs, rows, cols):
    src = subs((rows, cols))
    dst = lanes((rows, cols))
    hit = jnp.zeros((rows, cols), jnp.bool_)
    for source, cond in pairs:
        hit = hit | ((src == source(dst)) & cond(dst))
    return hit.astype(BF)


def patch_kernel(
    pos_ref, fold_ref, south_ref, low_ref, mid_ref, top_ref, north_ref, tops_ref, strip_ref,
    w1_ref, b1_ref, w2_ref, b2_ref, main_ref, out_ref, in_ref, res_ref, sem,
):
    gy, gx = pos_ref[0], pos_ref[1]
    signs = jnp.where(
        (subs((2 * FLD, PAD)) < 8) | (subs((2 * FLD, PAD)) == 16) | (subs((2 * FLD, PAD)) == 17), -1.0, 1.0
    )
    at = 0
    for ref, count in ((south_ref, 2), (low_ref, 2), (mid_ref, 4), (top_ref, 2), (north_ref, 2)):
        for k in range(count):
            in_ref[at] = ref[k].astype(F32)
            at += 1
    for k in range(3):
        in_ref[12 + k] = jnp.zeros((2 * FLD, PAD), F32)

    wrap = lambda t: jnp.where(t < 0, t + 16, jnp.where(t > 15, t - 16, t))
    near = wrap(gx - 1)
    far = wrap(gx + 1)
    p = fold_ref[gx]
    a = fold_ref[near]
    b = fold_ref[far]

    @pl.when(gy == 7)
    def _():
        def move(x, pairs):
            return jnp.dot(x, onehot(pairs, x.shape[1], PAD), preferred_element_type=F32)

        def inside(lo, hi):
            return lambda d: (d >= lo) & (d <= hi)

        def put(column, lane_at, step=0):
            count = 2 if step else 1
            return [(lambda d: column + step * (d - lane_at), inside(lane_at, lane_at + count - 1))]

        mirror = lambda d: SHIFT + COLS - 1 - d
        row = move(tops_ref[p, 1], [(mirror, inside(SHIFT, SHIFT + 255))])
        row = row + move(tops_ref[a, 1], put(1, 0, -1))
        row = row + move(tops_ref[b, 1], put(COLS - 1, SHIFT + COLS, -1))
        in_ref[10] = row * signs
        for k in range(2):
            in_ref[12 + k] = (
                move(tops_ref[p, k], [(mirror, inside(SHIFT, SHIFT + 255))])
                + move(tops_ref[wrap(p + 1), k], put(0, SHIFT - 1))
                + move(tops_ref[wrap(p - 1), k], put(COLS - 1, SHIFT + COLS))
                + move(tops_ref[a, k], put(1, 264, -1))
                + move(tops_ref[wrap(a - 1), k], put(COLS - 1, 266))
                + move(tops_ref[b, k], put(COLS - 1, 273, -1))
                + move(tops_ref[wrap(b + 1), k], put(0, 272))
            )
        last = move(
            in_ref[9].astype(BF),
            [(lambda d: d, inside(SHIFT, SHIFT + 255))] + put(0, 264, 1) + put(SHIFT + COLS, 273, 1),
        )
        last = last + move(tops_ref[fold_ref[wrap(p + 1)], 1], put(COLS - 1, SHIFT - 1))
        last = last + move(tops_ref[fold_ref[wrap(p - 1)], 1], put(0, SHIFT + COLS))
        last = last + move(tops_ref[fold_ref[wrap(a - 1)], 1], put(0, 266))
        last = last + move(tops_ref[fold_ref[wrap(b + 1)], 1], put(COLS - 1, 272))
        in_ref[14] = last * signs

    def hidden(rows, flip):
        total = jnp.broadcast_to(b1_ref[...], (HID, PAD))
        for u in range(3):
            x = in_ref[rows + u]
            for v in range(3):
                shifted = pltpu.roll(x, (1 - v) % PAD, 1) if v != 1 else x
                total = total + jnp.dot(
                    w1_ref[u, 2 - v if flip else v], shifted.astype(BF), preferred_element_type=F32
                )
        return jnp.maximum(total, 0.0).astype(BF)

    virtual = hidden(12, True).astype(F32)
    lane = lanes((HID, PAD))
    virtual = jnp.where(
        lane == SHIFT - 1,
        pltpu.roll(virtual, (SHIFT - 1 - 265) % PAD, 1),
        jnp.where(lane == SHIFT + 256, pltpu.roll(virtual, (SHIFT + 256 - 273) % PAD, 1), virtual),
    )
    for half in range(2):
        hid = [hidden(6 * half + k, False).astype(F32) for k in range(4)]
        if half == 0:
            hid[0] = jnp.where(gy == 0, jnp.zeros_like(hid[0]), hid[0])
        else:
            hid[3] = jnp.where(gy == 7, virtual, hid[3])
        for r in range(2):
            total = jnp.broadcast_to(b2_ref[...], (OUT, PAD))
            for u in range(3):
                x = hid[r + u]
                for v in range(3):
                    shifted = pltpu.roll(x, (1 - v) % PAD, 1) if v != 1 else x
                    total = total + jnp.dot(w2_ref[u, v], shifted.astype(BF), preferred_element_type=F32)
            m = strip_ref[6 * half + r, FLD : 2 * FLD, :].astype(F32)[:OUT]
            total = pltpu.roll(total * m, PAD - SHIFT, 1)
            res_ref[2 * half + r] = total[:, :COLS].astype(BF)
    copies = [
        pltpu.make_async_copy(res_ref.at[pl.ds(0, 2)], out_ref.at[pl.ds(0, 2)], sem.at[0]),
        pltpu.make_async_copy(res_ref.at[pl.ds(2, 2)], out_ref.at[pl.ds(ROWS - 2, 2)], sem.at[1]),
    ]
    for c in copies:
        c.start()
    for c in copies:
        c.wait()


def patch_rows(*args):
    smem = pl.BlockSpec(memory_space=pltpu.SMEM)
    vmem = pl.BlockSpec(memory_space=pltpu.VMEM)
    hbm = pl.BlockSpec(memory_space=pl.ANY)
    return pl.pallas_call(
        patch_kernel,
        out_shape=jax.ShapeDtypeStruct((ROWS, OUT, COLS), BF),
        in_specs=[smem, smem] + [vmem] * 11 + [hbm],
        out_specs=hbm,
        scratch_shapes=[
            pltpu.VMEM((15, 2 * FLD, PAD), F32),
            pltpu.VMEM((4, OUT, COLS), BF),
            pltpu.SemaphoreType.DMA((2,)),
        ],
        input_output_aliases={13: 0},
        compiler_params=pltpu.CompilerParams(vmem_limit_bytes=24 << 20),
        name="patch",
    )(*args)


def shift_gx(x, step):
    n = lax.axis_size("gx")
    return lax.ppermute(x, "gx", [(i, (i + step) % n) for i in range(n)])


def shift_gy(x, step):
    n = lax.axis_size("gy")
    return lax.ppermute(x, "gy", [(i, i + step) for i in range(n) if 0 <= i + step < n])


def per_device(
    ocean, atm, dest_tile, dest_row, live, land_mask, fold_pair, w1, b1, w2, b2
):
    edges = edge_columns(ocean, land_mask)
    west = shift_gx(edges[2:4], 1)
    east = shift_gx(edges[0:2], -1)

    tile = dest_tile[:, 0]
    same = tile[:, None] == tile[None, :]
    before = jnp.arange(HALF)[:, None] > jnp.arange(HALF)[None, :]
    rank = jnp.sum((same & before).astype(I32), axis=1)
    info = jnp.stack([tile * 4 + rank, jnp.where(live == 1, dest_row + 1, 0)])
    info = jnp.pad(info, ((0, 0), (0, 64)), constant_values=-1)
    outgoing = pack(info, atm.reshape(2 * HALF, 8, 128))
    outgoing, west, east = lax.optimization_barrier((outgoing, west, east))
    incoming = lax.all_to_all(
        outgoing.reshape(DEV, STEP, 8, 128), ("gy", "gx"), split_axis=0, concat_axis=0, tiled=True
    )
    b1c = b1[:, None]
    b2c = b2[:, None]
    part, m3, strip = ocean_part(ocean, land_mask, west, east, w1, b1c)

    coarse, ccols, cwest, ceast, low, mid, top, tops = coarse_sums(
        incoming.reshape(DEV * STEP, 8, 128), strip
    )
    south = shift_gy(top, 1)
    north = shift_gy(low, -1)
    tops = lax.all_to_all(tops, "gx", split_axis=0, concat_axis=0, tiled=True)
    out = main_conv(
        part, m3, coarse, edges, west, east, ccols, cwest, ceast, w1, b1c, w2, b2c,
    )
    pos = jnp.stack([lax.axis_index("gy"), lax.axis_index("gx")]).astype(I32)
    return patch_rows(
        pos, fold_pair, south, low, mid, top, north, tops, strip, w1, b1c, w2, b2c, out
    )


def solution(mesh):
    return jax.shard_map(
        per_device,
        mesh=mesh,
        in_specs=(
            P("gy", None, "gx"),
            P(("gy", "gx"), None, None),
            P(("gy", "gx"), None),
            P(("gy", "gx")),
            P(("gy", "gx")),
            P("gy", "gx"),
            P(),
            P(),
            P(),
            P(),
            P(),
        ),
        out_specs=P("gy", None, "gx"),
        check_vma=False,
    )
```

time: 163 us -> 94.8 us (0.58)
  Pallas kernels: 82.2 us -> 50.4 us
  starting transfers between devices: 53.1 us -> 28.1 us
  local copies, waits for them, and re-layouts: 16 us -> 8.42 us
  other arithmetic: 2.96 us -> 0.28 us
    pallas_call x1, Pallas kernels: 41.7 us -> 19.8 us  [main_conv(): pl.pallas_call(main_kernel, out_shape=jax.ShapeDtypeStruct((ROWS, OUT, CO...]
    pallas_call x1, Pallas kernels: 21.3 us -> 3.53 us  [edge_columns(): pl.pallas_call(edge_kernel, out_shape=jax.ShapeDtypeStruct((4, 2 * FLD, R...]
    all_to_all x4 -> x2, starting transfers between devices: 28.9 us -> 15.9 us  [the longest x1 10.3 us: per_device(): lax.all_to_all(outgoing.reshape(DEV, STEP, 8, 128), ('gy', 'gx'), split_a...]
    pallas_call x1 -> x2, Pallas kernels: 6.67 us -> 16.7 us  [the longest x1 12.2 us: ocean_part(): pl.pallas_call(ocean_kernel, out_shape=(jax.ShapeDtypeStruct((ROWS, HID,...]
    ppermute x4 -> x2, starting transfers between devices: 18.9 us -> 9.44 us  [shift_gy(): lax.ppermute(x, 'gy', [(i, i + step) for i in range(n) if 0 <= i + step <...]
    unnamed x37 -> x33, local copies, waits for them, and re-layouts: 3.49 us -> 7.65 us
    reshape x6 -> x0, local copies, waits for them, and re-layouts: 4.07 us -> none  [the longest x2 1.11 us: per_device(): w1b = w1b.reshape(192, 480)]
    slice x13 -> x1, local copies, waits for them, and re-layouts: 3.04 us -> 0.01 us  [per_device(): east = shift_gx(edges[0:2], -1)]
  transfers between devices with their start and end apart: 12 -> 6, of which waited for: 3 -> 1; matrix products, arithmetic and copies ran while one was open for 10% -> 2% of each run, Pallas kernels for 35% -> 39%
where the time goes in v2:
time: 94.8 us; the launch traced here: 94.3 us
  Pallas kernels  50.4 us (53%)
  starting transfers between devices  28.1 us (30%)
  local copies, waits for them, and re-layouts  8.42 us (9%)
  waiting for transfers between devices  6.97 us (7%)
    pallas_call x1, Pallas kernels, main_conv(): pl.pallas_call(main_kernel, out_shape=jax.ShapeDtypeStruct((ROWS, OUT, CO...  19.8 us
    pallas_call x1, Pallas kernels, ocean_part(): pl.pallas_call(ocean_kernel, out_shape=(jax.ShapeDtypeStruct((ROWS, HID,...  12.2 us
    all_to_all x1, starting transfers between devices, per_device(): lax.all_to_all(outgoing.reshape(DEV, STEP, 8, 128), ('gy', 'gx'), split_a...  10.3 us
    ppermute x2, starting transfers between devices, shift_gy(): lax.ppermute(x, 'gy', [(i, i + step) for i in range(n) if 0 <= i + step <...  9.44 us
    unnamed x33, local copies, waits for them, and re-layouts  7.65 us
    pallas_call x1, Pallas kernels, coarse_sums(): pl.pallas_call(coarse_kernel, out_shape=(jax.ShapeDtypeStruct((HALF, FLD,...  7.27 us
    all_to_all x1, waiting for transfers between devices, per_device(): lax.all_to_all(outgoing.reshape(DEV, STEP, 8, 128), ('gy', 'gx'), split_a...  6.96 us
    all_to_all x1, starting transfers between devices, per_device(): tops = lax.all_to_all(tops, 'gx', split_axis=0, concat_axis=0, tiled=True)  5.65 us
  transfers between devices with their start and end apart: 6, of which 1 were waited for; matrix products, arithmetic and copies ran while one was open for 2% of the time, Pallas kernels for 39%

profile of v2, /device:TPU:66, one launch (start us, length us, event | category | flops | bytes accessed | tf_op | source)
XLA Modules:
  0.0 94.3 jit_solution(1325005807543707836)
XLA Ops:
  0.0 1.9 %copy-done = bf16[384,16,256]{2,1,0:T(8,128)(2,1)S(1)} copy-done((bf16[384,16,256]{2,1,0:T(8,128)(2,1)S(1)}, bf16[384,16,256]{2,1,0:T(8,128)(2,1)}, u32[]{:S(2)}) %copy-start) | copy-done | bytes 3145752
  1.9 1.0 %copy-done.2 = s32[384,256]{1,0:T(8,128)S(1)} copy-done((s32[384,256]{1,0:T(8,128)S(1)}, s32[384,256]{1,0:T(8,128)}, u32[]{:S(2)}) %copy-start.2) | copy-done | bytes 393240
  2.9 3.5 %edges.1.own_ref = bf16[4,32,384]{2,1,0:T(8,128)(2,1)S(1)} custom-call(bf16[384,16,256]{2,1,0:T(8,128)(2,1)S(1)} %copy-done, s32[384,256]{1,0:T(8,128)S(1)} %copy-done.2), custom_call_target="tpu_custom_call" | custom-call | tf_op jit(solution)/shard_map/edges/pallas_call | solution.py:231
  6.4 0.1 collective-permute-start
  6.5 2.6 %collective-permute-start.1 = (bf16[2,32,384]{2,1,0:T(8,128)(2,1)S(1)}, bf16[2,32,384]{2,1,0:T(8,128)(2,1)S(1)}, u32[]{:S(2)}, u32[]{:S(2)}) collective-permute-start(bf16[2,32,384]{2,1,0:T(8,128)(2,1)S(1)} %get-tuple-element.33), channel_id=1, source_target_pairs={{0,15},{1,0},{2,1},{3,2},{4,3},{5,4},{6,5},{7,6},{8,7},{9,8},{10,9... | collective-permute-start | bytes 147464 | tf_op jit(solution)/shard_map/ppermute | solution.py:647
  9.2 0.2 convert_reduce_fusion
  9.4 0.6 pad.4.info_ref.row_ref
  10.0 4.5 %pack.1 = bf16[896,8,128]{2,1,0:T(8,128)(2,1)} custom-call(s32[2,256]{1,0:T(2,128)} %pad.4.info_ref.row_ref, s32[2,256]{1,0:T(2,128)} %pad.4.info_ref.row_ref, bf16[384,8,128]{2,1,0:T(8,128)(2,1)} %bitcast.13), custom_call_target="tpu_custom_call" | custom-call | tf_op jit(solution)/shard_map/pack/pallas_call | solution.py:88
  14.5 0.0 collective-permute-done.west_ref
  14.5 0.0 collective-permute-done.1.east_ref
  14.5 0.0 copy-start.1
  14.5 10.3 %all-to-all-start = ((bf16[128,7,8,128]{3,2,1,0:T(8,128)(2,1)}), bf16[128,7,8,128]{3,2,1,0:T(8,128)(2,1)}, u32[]{:S(2)}, u32[]{:S(2)}) async-start(bf16[128,7,8,128]{3,2,1,0:T(8,128)(2,1)} %bitcast.12), calls=%async_computation | async-start | bytes 3670016 | tf_op jit(solution)/shard_map/all_to_all | solution.py:670
  24.8 1.0 %copy.21.w_ref.w1_ref = bf16[3,3,64,32]{3,2,1,0:T(8,128)(2,1)S(1)} copy(bf16[3,3,64,32]{2,3,1,0:T(8,128)(2,1)} %param.18) | data formatting | bytes 73728 | tf_op args[7]
  25.8 0.1 copy.22.b_ref.b1_ref
  25.9 1.0 %copy-done.3 = s32[384,256]{1,0:T(8,128)S(1)} copy-done((s32[384,256]{1,0:T(8,128)S(1)}, s32[384,256]{1,0:T(8,128)}, u32[]{:S(2)}) %copy-start.3) | copy-done | bytes 393240
  26.9 12.2 %ocean.1 = (bf16[384,64,256]{2,1,0:T(8,128)(2,1)}, f32[3,384,256]{2,1,0:T(8,128)S(1)}, bf16[8,32,384]{2,1,0:T(8,128)(2,1)S(1)}) custom-call(bf16[384,16,256]{2,1,0:T(8,128)(2,1)S(1)} %copy-done.1, s32[384,256]{1,0:T(8,128)S(1)} %copy-done.3, bf16[2,32,384]{2,1,0:T(8,128)(2,1)S(1)} %collective-permute-done.west_ref, ...), custom_call_target="tpu_custom_call" | custom-call | tf_op jit(solution)/shard_map/ocean/pallas_call | solution.py:333
  39.1 0.0 copy-start.4
  39.1 1.0 %copy-done.4 = f32[3,384,256]{2,1,0:T(8,128)} copy-done((f32[3,384,256]{2,1,0:T(8,128)}, f32[3,384,256]{2,1,0:T(8,128)S(1)}, u32[]{:S(2)}) %copy-start.4) | copy-done | bytes 1179672
  40.1 0.7 copy-done.6
  40.8 7.0 %all-to-all-done = bf16[128,7,8,128]{3,2,1,0:T(8,128)(2,1)} async-done(((bf16[128,7,8,128]{3,2,1,0:T(8,128)(2,1)}), bf16[128,7,8,128]{3,2,1,0:T(8,128)(2,1)}, u32[]{:S(2)}, u32[]{:S(2)}) %all-to-all-start) | async-done | bytes 1835040 | tf_op jit(solution)/shard_map/all_to_all | solution.py:670
  47.8 1.0 %copy-done.7 = bf16[8,32,384]{2,1,0:T(8,128)(2,1)S(1)} copy-done((bf16[8,32,384]{2,1,0:T(8,128)(2,1)S(1)}, bf16[8,32,384]{2,1,0:T(8,128)(2,1)}, u32[]{:S(2)}) %copy-start.7) | copy-done | bytes 196632
  48.8 7.3 %coarse.1 = (bf16[192,16,128]{2,1,0:T(8,128)(2,1)S(1)}, bf16[2,16,256]{2,1,0:T(8,128)(2,1)S(1)}, bf16[16,256]{1,0:T(8,128)(2,1)S(1)}, bf16[16,256]{1,0:T(8,128)(...) custom-call(bf16[896,8,128]{2,1,0:T(8,128)(2,1)} %bitcast.8.inc_ref,, ...), custom_call_target="tpu_custom_call" | custom-call | tf_op jit(solution)/shard_map/coarse/pallas_call | solution.py:180
  56.1 5.6 %all-to-all-start.1 = ((bf16[16,2,32,256]{3,2,1,0:T(8,128)(2,1)}), bf16[16,2,32,256]{3,2,1,0:T(8,128)(2,1)S(1)}, u32[]{:S(2)}, u32[]{:S(2)}) async-start(bf16[16,2,32,256]{3,2,1,0:T(8,128)(2,1)} %get-tuple-element.26), calls=%async_computation.1 | async-start | bytes 1048576 | tf_op jit(solution)/shard_map/all_to_all | solution.py:682
  61.7 3.0 %collective-permute-start.2 = (bf16[2,32,384]{2,1,0:T(8,128)(2,1)S(1)}, bf16[2,32,384]{2,1,0:T(8,128)(2,1)S(1)}, u32[]{:S(2)}, u32[]{:S(2)}) collective-permute-start(bf16[2,32,384]{2,1,0:T(8,128)(2,1)S(1)} %get-tuple-element.23.top_ref), channel_id=1, source_target_pairs={{0,16},{16,32},{32,48},{48,64},{64,80},{80,96},{96,112},{1,17},{17... | collective-permute-start | bytes 147464 | tf_op jit(solution)/shard_map/ppermute | solution.py:652
  64.7 6.5 %collective-permute-start.3 = (bf16[2,32,384]{2,1,0:T(8,128)(2,1)S(1)}, bf16[2,32,384]{2,1,0:T(8,128)(2,1)S(1)}, u32[]{:S(2)}, u32[]{:S(2)}) collective-permute-start(bf16[2,32,384]{2,1,0:T(8,128)(2,1)S(1)} %get-tuple-element.24.low_ref), channel_id=1, source_target_pairs={{16,0},{32,16},{48,32},{64,48},{80,64},{96,80},{112,96},{17,1},{33... | collective-permute-start | bytes 147464 | tf_op jit(solution)/shard_map/ppermute | solution.py:652
  71.2 0.1 pad_add_fusion.1.pos_ref
  71.3 0.1 copy.28.b2_ref
  71.4 19.8 %convs.1.main_ref = bf16[384,8,256]{2,1,0:T(8,128)(2,1)} custom-call(bf16[384,64,256]{2,1,0:T(8,128)(2,1)} %get-tuple-element.27.part_ref, f32[3,384,256]{2,1,0:T(8,128)S(1)} %copy-done.5, bf16[192,16,128]{2,1,0:T(8,128)(2,1)S(1)} %get-tuple-element.29.coarse_ref, bf16[4,32,384]{2,1,0:T(8,128)(2,1)S(1)} %edges.1.own_ref, ...), custom_call_target="tpu_custom_call" | custom-call | tf_op jit(solution)/shard_map/convs/pallas_call | solution.py:491
  91.2 0.0 collective-permute-done.2.south_ref
  91.2 0.0 collective-permute-done.3.north_ref
  91.2 0.0 all-to-all-done.1.tops_ref
  91.2 3.1 %patch.1 = bf16[384,8,256]{2,1,0:T(8,128)(2,1)} custom-call(s32[2]{0:T(128)S(1)} %pad_add_fusion.1.pos_ref, s32[16]{0:T(128)S(1)} %copy-done.10, bf16[2,32,384]{2,1,0:T(8,128)(2,1)S(1)} %collective-permute-done.2.south_ref, bf16[2,32,384]{2,1,0:T(8,128)(2,1)S(1)} %get-tuple-element.24.low_ref, ...), custom_call_target="tpu_custom_call", output_to_operand_aliasing={{}: (13, {})} | custom-call | tf_op jit(solution)/shard_map/patch/pallas_call | solution.py:629
  (28 shorter events, 0.1 us)
Async XLA Ops:
  0.0 1.9 %copy-start = (bf16[384,16,256]{2,1,0:T(8,128)(2,1)S(1)}, bf16[384,16,256]{2,1,0:T(8,128)(2,1)}, u32[]{:S(2)}) copy-start(bf16[384,16,256]{2,1,0:T(8,128)(2,1)} %ocean_ref.3) | copy-start | bytes 9437188
  1.9 1.0 %copy-start.2 = (s32[384,256]{1,0:T(8,128)S(1)}, s32[384,256]{1,0:T(8,128)}, u32[]{:S(2)}) copy-start(s32[384,256]{1,0:T(8,128)} %mask_ref.3) | copy-start | bytes 1179652
  2.9 6.3 %copy-start.11 = (s32[192,1]{0,1:T(1,128)S(1)}, s32[192,1]{0,1:T(1,128)}, u32[]{:S(2)}) copy-start(s32[192,1]{0,1:T(1,128)} %param.13) | copy-start | bytes 2308
  2.9 6.5 %copy-start.12 = (s32[192]{0:T(256)S(1)}, s32[192]{0:T(256)}, u32[]{:S(2)}) copy-start(s32[192]{0:T(256)} %param.15) | copy-start | bytes 2308
  2.9 6.5 %copy-start.13 = (s32[192]{0:T(256)S(1)}, s32[192]{0:T(256)}, u32[]{:S(2)}) copy-start(s32[192]{0:T(256)} %param.14) | copy-start | bytes 2308
  6.4 8.1 %collective-permute-start = (bf16[2,32,384]{2,1,0:T(8,128)(2,1)S(1)}, bf16[2,32,384]{2,1,0:T(8,128)(2,1)S(1)}, u32[]{:S(2)}, u32[]{:S(2)}) collective-permute-start(bf16[2,32,384]{2,1,0:T(8,128)(2,1)S(1)} %get-tuple-element.34), channel_id=1, source_target_pairs={{0,1},{1,2},{2,3},{3,4},{4,5},{5,6},{6,7},{7,8},{8,9},{9,10},{10,1... | collective-permute-start | bytes 147464 | tf_op jit(solution)/shard_map/ppermute | solution.py:647
  6.5 8.0 %collective-permute-start.1 = (bf16[2,32,384]{2,1,0:T(8,128)(2,1)S(1)}, bf16[2,32,384]{2,1,0:T(8,128)(2,1)S(1)}, u32[]{:S(2)}, u32[]{:S(2)}) collective-permute-start(bf16[2,32,384]{2,1,0:T(8,128)(2,1)S(1)} %get-tuple-element.33), channel_id=1, source_target_pairs={{0,15},{1,0},{2,1},{3,2},{4,3},{5,4},{6,5},{7,6},{8,7},{9,8},{10,9... | collective-permute-start | bytes 147464 | tf_op jit(solution)/shard_map/ppermute | solution.py:647
  14.5 11.3 %copy-start.14 = (f32[64]{0:T(128)S(1)}, f32[64]{0:T(128)}, u32[]{:S(2)}) copy-start(f32[64]{0:T(128)} %param.19) | copy-start | bytes 772
  14.5 11.4 %copy-start.1 = (bf16[384,16,256]{2,1,0:T(8,128)(2,1)S(1)}, bf16[384,16,256]{2,1,0:T(8,128)(2,1)}, u32[]{:S(2)}) copy-start(bf16[384,16,256]{2,1,0:T(8,128)(2,1)} %ocean_ref.3) | copy-start | bytes 9437188
  14.5 33.3 %all-to-all-start = ((bf16[128,7,8,128]{3,2,1,0:T(8,128)(2,1)}), bf16[128,7,8,128]{3,2,1,0:T(8,128)(2,1)}, u32[]{:S(2)}, u32[]{:S(2)}) async-start(bf16[128,7,8,128]{3,2,1,0:T(8,128)(2,1)} %bitcast.12), calls=%async_computation | async-start | bytes 3670016 | tf_op jit(solution)/shard_map/all_to_all | solution.py:670
  25.9 1.0 %copy-start.3 = (s32[384,256]{1,0:T(8,128)S(1)}, s32[384,256]{1,0:T(8,128)}, u32[]{:S(2)}) copy-start(s32[384,256]{1,0:T(8,128)} %mask_ref.3) | copy-start | bytes 1179652
  26.9 44.3 %copy-start.15 = (f32[8]{0:T(128)S(1)}, f32[8]{0:T(128)}, u32[]{:S(2)}) copy-start(f32[8]{0:T(128)} %param.21) | copy-start | bytes 100
  26.9 44.4 %copy-start.9 = (bf16[3,3,8,64]{3,2,1,0:T(8,128)(2,1)S(1)}, bf16[3,3,8,64]{3,2,1,0:T(8,128)(2,1)}, u32[]{:S(2)}) copy-start(bf16[3,3,8,64]{3,2,1,0:T(8,128)(2,1)} %w2_ref.3) | copy-start | bytes 27652
  39.1 1.0 %copy-start.4 = (f32[3,384,256]{2,1,0:T(8,128)}, f32[3,384,256]{2,1,0:T(8,128)S(1)}, u32[]{:S(2)}) copy-start(f32[3,384,256]{2,1,0:T(8,128)S(1)} %get-tuple-element.28.m3_ref) | copy-start | bytes 3538948
  40.1 0.7 copy-start.6
  47.8 23.6 %copy-start.5 = (f32[3,384,256]{2,1,0:T(8,128)S(1)}, f32[3,384,256]{2,1,0:T(8,128)}, u32[]{:S(2)}) copy-start(f32[3,384,256]{2,1,0:T(8,128)} %copy-done.4) | copy-start | bytes 3538948
  47.8 1.0 %copy-start.7 = (bf16[8,32,384]{2,1,0:T(8,128)(2,1)S(1)}, bf16[8,32,384]{2,1,0:T(8,128)(2,1)}, u32[]{:S(2)}) copy-start(bf16[8,32,384]{2,1,0:T(8,128)(2,1)} %copy-done.6) | copy-start | bytes 589828
  56.1 35.1 %all-to-all-start.1 = ((bf16[16,2,32,256]{3,2,1,0:T(8,128)(2,1)}), bf16[16,2,32,256]{3,2,1,0:T(8,128)(2,1)S(1)}, u32[]{:S(2)}, u32[]{:S(2)}) async-start(bf16[16,2,32,256]{3,2,1,0:T(8,128)(2,1)} %get-tuple-element.26), calls=%async_computation.1 | async-start | bytes 1048576 | tf_op jit(solution)/shard_map/all_to_all | solution.py:682
  61.7 29.4 %collective-permute-start.2 = (bf16[2,32,384]{2,1,0:T(8,128)(2,1)S(1)}, bf16[2,32,384]{2,1,0:T(8,128)(2,1)S(1)}, u32[]{:S(2)}, u32[]{:S(2)}) collective-permute-start(bf16[2,32,384]{2,1,0:T(8,128)(2,1)S(1)} %get-tuple-element.23.top_ref), channel_id=1, source_target_pairs={{0,16},{16,32},{32,48},{48,64},{64,80},{80,96},{96,112},{1,17},{17... | collective-permute-start | bytes 147464 | tf_op jit(solution)/shard_map/ppermute | solution.py:652
  64.7 26.5 %collective-permute-start.3 = (bf16[2,32,384]{2,1,0:T(8,128)(2,1)S(1)}, bf16[2,32,384]{2,1,0:T(8,128)(2,1)S(1)}, u32[]{:S(2)}, u32[]{:S(2)}) collective-permute-start(bf16[2,32,384]{2,1,0:T(8,128)(2,1)S(1)} %get-tuple-element.24.low_ref), channel_id=1, source_target_pairs={{16,0},{32,16},{48,32},{64,48},{80,64},{96,80},{112,96},{17,1},{33... | collective-permute-start | bytes 147464 | tf_op jit(solution)/shard_map/ppermute | solution.py:652
  71.4 19.8 %copy-start.8 = (bf16[8,32,384]{2,1,0:T(8,128)(2,1)S(1)}, bf16[8,32,384]{2,1,0:T(8,128)(2,1)}, u32[]{:S(2)}) copy-start(bf16[8,32,384]{2,1,0:T(8,128)(2,1)} %copy-done.6) | copy-start | bytes 589828
  71.4 19.8 %copy-start.10 = (s32[16]{0:T(128)S(1)}, s32[16]{0:T(128)}, u32[]{:S(2)}) copy-start(s32[16]{0:T(128)} %fold_ref.1) | copy-start | bytes 196

commit v3 on v2

--- a/solution.py
+++ b/solution.py
@@ -34,7 +34,18 @@
 STEP = 2 * CAP + 1
 
 
-def pack_kernel(info_ref, row_ref, atm_ref, out_ref, q_ref):
+def pack_kernel(tile_ref, row_ref, live_ref, atm_ref, out_ref, q_ref, code_ref, info_ref, sem):
+    across = jnp.concatenate([tile_ref[...].astype(F32), jnp.full((1, 64), -1.0, F32)], axis=1)
+    column = jnp.broadcast_to(across, (128, 256))
+    column = jnp.concatenate([column[:, :128].T, column[:, 128:].T[:64]], axis=0)
+    earlier = (subs((HALF, 256)) < lanes((HALF, 256))) & (
+        jnp.concatenate([column, column], axis=1) == jnp.broadcast_to(across, (HALF, 256))
+    )
+    code = 4.0 * across + jnp.sum(earlier.astype(F32), axis=0, keepdims=True)
+    code_ref[...] = code.astype(I32)
+    copy = pltpu.make_async_copy(code_ref, info_ref, sem)
+    copy.start()
+    copy.wait()
     lane = lanes((FLD, 128))
     first, last = [], []
     for chunk, count in ((0, 128), (128, 64)):
@@ -56,8 +67,9 @@
         first.append(c0)
         last.append(c1)
     values = [jnp.concatenate(last, axis=1), jnp.concatenate(first, axis=1)]
-    code = jnp.broadcast_to(row_ref[0:1, :], (DEV, 256))
-    row = row_ref[1:2, :].astype(F32).astype(BF)
+    code = jnp.broadcast_to(code_ref[...], (DEV, 256))
+    row = jnp.where(live_ref[...] == 1, row_ref[...] + 1, 0).astype(F32)
+    row = jnp.concatenate([row, jnp.zeros((1, 64), F32)], axis=1).astype(BF)
     total = jnp.zeros((DEV, 128), F32)
     tile = subs((DEV, 256))
     none = jnp.zeros((FLD, 256), BF)
@@ -84,19 +96,18 @@
     lax.fori_loop(0, DEV, head, 0, unroll=16)
 
 
-def pack(info, atm):
+def pack(tile, row, live, atm):
     return pl.pallas_call(
         pack_kernel,
         out_shape=jax.ShapeDtypeStruct((DEV * STEP, 8, 128), BF),
-        in_specs=[
-            pl.BlockSpec(memory_space=pltpu.SMEM),
-            pl.BlockSpec(memory_space=pltpu.VMEM),
-            pl.BlockSpec(memory_space=pltpu.VMEM),
+        scratch_shapes=[
+            pltpu.VMEM((DEV, 128), F32),
+            pltpu.VMEM((1, 256), I32),
+            pltpu.SMEM((1, 256), I32),
+            pltpu.SemaphoreType.DMA,
         ],
-        out_specs=pl.BlockSpec(memory_space=pltpu.VMEM),
-        scratch_shapes=[pltpu.VMEM((DEV, 128), F32)],
         name="pack",
-    )(info, info, atm)
+    )(tile, row, live, atm)
 
 
 def coarse_kernel(
@@ -196,12 +207,12 @@
             pltpu.SMEM((4, 8, 128), I32),
             pltpu.SemaphoreType.DMA,
         ],
-        compiler_params=pltpu.CompilerParams(vmem_limit_bytes=24 << 20),
+        compiler_params=pltpu.CompilerParams(vmem_limit_bytes=12 << 20),
         name="coarse",
     )(incoming, strip)
 
 
-def edge_kernel(ocean_ref, mask_ref, out_ref):
+def edge_kernel(ocean_ref, mask_ref, first_ref, last_ref):
     lane = lanes((FLD, 128))
     for chunk in range(3):
         block = mask_ref[chunk * 128 : chunk * 128 + 128, :].astype(F32)
@@ -224,13 +235,14 @@
         rows = (m_left[0:1], m_left[1:2], m_right[126:127], m_right[127:128])
         for k in range(4):
             m = jnp.broadcast_to(rows[k], (FLD, 128)).astype(BF)
-            out_ref[k, :, chunk * 128 : chunk * 128 + 128] = jnp.concatenate([got[k] * m, m], axis=0)
+            ref = last_ref if k >= 2 else first_ref
+            ref[k % 2, :, chunk * 128 : chunk * 128 + 128] = jnp.concatenate([got[k] * m, m], axis=0)
 
 
 def edge_columns(ocean, mask):
     return pl.pallas_call(
         edge_kernel,
-        out_shape=jax.ShapeDtypeStruct((4, 2 * FLD, ROWS), BF),
+        out_shape=(jax.ShapeDtypeStruct((2, 2 * FLD, ROWS), BF),) * 2,
         compiler_params=pltpu.CompilerParams(vmem_limit_bytes=24 << 20),
         name="edges",
     )(ocean, mask)
@@ -249,11 +261,84 @@
 
 
 def ocean_kernel(
-    ocean_ref, mask_ref, west_ref, east_ref, w_ref, b_ref, part_ref, m3_ref, strip_ref,
-    xs_ref, h_ref, band_ref, sem,
+    ocean_ref, mask_ref, wt_ref, b1_ref, b2_ref, part_ref, strip_ref, w_ref, b1c_ref, b2c_ref, xs_ref, band_ref, h_ref, sem,
 ):
+    for u in range(3):
+        for v in range(3):
+            w_ref[u, v] = wt_ref[u, v].astype(F32).T.astype(BF)
+    b1c_ref[...] = jnp.broadcast_to(b1_ref[...], (128, HID)).T
+    b2c_ref[...] = jnp.broadcast_to(b2_ref[...], (128, OUT)).T
     banded(w_ref, band_ref, 0)
-    bias = jnp.concatenate([b_ref[...]] * 3, axis=0)
+    bias = jnp.concatenate([b1c_ref[:, 0:1]] * 3, axis=0)
+    lane16 = lanes((FLD, 128))
+    zero = jnp.zeros((48, COLS), BF)
+    xs_ref[0] = zero
+    xs_ref[ROWS + 1] = zero
+    nothing = jnp.zeros((FLD, 128), BF)
+
+    def build(y):
+        m = jnp.broadcast_to(mask_ref[pl.ds(y, 1), :].astype(F32), (FLD, COLS)).astype(BF)
+        x = ocean_ref[y] * m
+        up, down = pltpu.roll(x, 1, 1), pltpu.roll(x, COLS - 1, 1)
+        xs_ref[y + 1, 0:16, 0:128] = jnp.where(lane16 == 0, nothing, up[:, :128])
+        xs_ref[y + 1, 0:16, 128:256] = up[:, 128:]
+        xs_ref[y + 1, 16:32, :] = x
+        xs_ref[y + 1, 32:48, 0:128] = down[:, :128]
+        xs_ref[y + 1, 32:48, 128:256] = jnp.where(lane16 == 127, nothing, down[:, 128:])
+
+    for n, y in enumerate((0, 1, 2, 3, ROWS - 4, ROWS - 3, ROWS - 2, ROWS - 1)):
+        m = jnp.broadcast_to(mask_ref[y : y + 1, :].astype(F32), (FLD, COLS))
+        x = jnp.concatenate([ocean_ref[y].astype(F32) * m, m], axis=0)
+        x = jnp.concatenate([x, jnp.zeros((2 * FLD, 128), F32)], axis=1)
+        strip_ref[n] = pltpu.roll(x, SHIFT, 1).astype(BF)
+
+    def first(i, carry):
+        build(i)
+        return carry
+
+    lax.fori_loop(0, 24, first, 0, unroll=8)
+
+    def conv(block, carry):
+        for k in range(8):
+            g = block * 8 + k
+            for r in range(3):
+                build(jnp.minimum(3 * g + 24 + r, ROWS - 1))
+            x = xs_ref[pl.ds(3 * g, 5)].reshape(240, COLS)
+            t = jnp.dot(band_ref[...], x, preferred_element_type=F32) + bias
+            h_ref[pl.ds(3 * g, 3)] = t.astype(BF).reshape(3, HID, COLS)
+        at = pl.ds(block * 24, 24)
+        pltpu.make_async_copy(h_ref.at[at], part_ref.at[at], sem.at[block]).start()
+        return carry
+
+    lax.fori_loop(0, BLOCKS, conv, 0)
+    for block in range(BLOCKS):
+        at = pl.ds(block * 24, 24)
+        pltpu.make_async_copy(h_ref.at[at], part_ref.at[at], sem.at[block]).wait()
+
+
+def ocean_part(*args):
+    return pl.pallas_call(
+        ocean_kernel,
+        out_shape=(
+            jax.ShapeDtypeStruct((ROWS, HID, COLS), BF),
+            jax.ShapeDtypeStruct((8, 2 * FLD, PAD), BF),
+            jax.ShapeDtypeStruct((3, 3, HID, 2 * FLD), BF),
+            jax.ShapeDtypeStruct((HID, 128), F32),
+            jax.ShapeDtypeStruct((OUT, 128), F32),
+        ),
+        out_specs=(pl.BlockSpec(memory_space=pl.ANY),) + (pl.BlockSpec(memory_space=pltpu.VMEM),) * 4,
+        scratch_shapes=[
+            pltpu.VMEM((ROWS + 2, 48, COLS), BF),
+            pltpu.VMEM((192, 240), BF),
+            pltpu.VMEM((ROWS, HID, COLS), BF),
+            pltpu.SemaphoreType.DMA((BLOCKS,)),
+        ],
+        compiler_params=pltpu.CompilerParams(vmem_limit_bytes=40 << 20),
+        name="ocean",
+    )(*args)
+
+
+def margin_kernel(mask_ref, west_ref, east_ref, rows_ref, m3_ref, strip_ref):
     lane = lanes((128, 128))
     for chunk in range(3):
         at = slice(chunk * 128, chunk * 128 + 128)
@@ -266,33 +351,10 @@
         m3_ref[1, at, :] = m
         m3_ref[2, at, 0:128] = down[:, :128]
         m3_ref[2, at, 128:256] = jnp.where(lane == 127, east, down[:, 128:])
-
-    lane16 = lanes((FLD, 128))
-    zero = jnp.zeros((48, COLS), BF)
-    xs_ref[0] = zero
-    xs_ref[ROWS + 1] = zero
-
-    def build(y):
-        base = pl.multiple_of((y // 128) * 128, 128)
-        i = y % 128
-        m = jnp.broadcast_to(m3_ref[1, pl.ds(y, 1), :], (FLD, COLS)).astype(BF)
-        x = ocean_ref[y] * m
-        west = pltpu.roll(west_ref[1, 0:FLD, pl.ds(base, 128)], 128 - i, 1)
-        east = pltpu.roll(east_ref[0, 0:FLD, pl.ds(base, 128)], 127 - i, 1)
-        up, down = pltpu.roll(x, 1, 1), pltpu.roll(x, COLS - 1, 1)
-        xs_ref[y + 1, 0:16, 0:128] = jnp.where(lane16 == 0, west, up[:, :128])
-        xs_ref[y + 1, 0:16, 128:256] = up[:, 128:]
-        xs_ref[y + 1, 16:32, :] = x
-        xs_ref[y + 1, 32:48, 0:128] = down[:, :128]
-        xs_ref[y + 1, 32:48, 128:256] = jnp.where(lane16 == 127, east, down[:, 128:])
-
     wide_lane = lanes((2 * FLD, 128))
     for n, y in enumerate((0, 1, 2, 3, ROWS - 4, ROWS - 3, ROWS - 2, ROWS - 1)):
         base, i = (y // 128) * 128, y % 128
-        m = jnp.broadcast_to(m3_ref[1, y : y + 1, :], (FLD, COLS))
-        x = jnp.concatenate([ocean_ref[y].astype(F32) * m, m], axis=0)
-        x = jnp.concatenate([x, jnp.zeros((2 * FLD, 128), F32)], axis=1)
-        x = pltpu.roll(x, SHIFT, 1)
+        x = rows_ref[n].astype(F32)
 
         def beside(ref, k, lane_at):
             return pltpu.roll(ref[k, :, base : base + 128].astype(F32), (128 + lane_at - i) % 128, 1)
@@ -305,63 +367,26 @@
         strip_ref[n, :, 128:256] = x[:, 128:256].astype(BF)
         strip_ref[n, :, 256:384] = hi.astype(BF)
 
-    def first(i, carry):
-        build(i)
-        return carry
-
-    lax.fori_loop(0, 24, first, 0, unroll=8)
-
-    def conv(block, carry):
-        for k in range(8):
-            g = block * 8 + k
-            for r in range(3):
-                build(jnp.minimum(3 * g + 24 + r, ROWS - 1))
-            x = xs_ref[pl.ds(3 * g, 5)].reshape(240, COLS)
-            t = jnp.dot(band_ref[...], x, preferred_element_type=F32) + bias
-            h_ref[pl.ds(3 * g, 3)] = t.astype(BF).reshape(3, HID, COLS)
-        at = pl.ds(block * 24, 24)
-        pltpu.make_async_copy(h_ref.at[at], part_ref.at[at], sem.at[block]).start()
-        return carry
-
-    lax.fori_loop(0, BLOCKS, conv, 0)
-    for block in range(BLOCKS):
-        at = pl.ds(block * 24, 24)
-        pltpu.make_async_copy(h_ref.at[at], part_ref.at[at], sem.at[block]).wait()
-
-
-def ocean_part(ocean, mask, west, east, w1, b1):
+def margins(*args):
     return pl.pallas_call(
-        ocean_kernel,
+        margin_kernel,
         out_shape=(
-            jax.ShapeDtypeStruct((ROWS, HID, COLS), BF),
             jax.ShapeDtypeStruct((3, ROWS, COLS), F32),
             jax.ShapeDtypeStruct((8, 2 * FLD, PAD), BF),
         ),
-        out_specs=(
-            pl.BlockSpec(memory_space=pl.ANY),
-            pl.BlockSpec(memory_space=pltpu.VMEM),
-            pl.BlockSpec(memory_space=pltpu.VMEM),
-        ),
-        scratch_shapes=[
-            pltpu.VMEM((ROWS + 2, 48, COLS), BF),
-            pltpu.VMEM((ROWS, HID, COLS), BF),
-            pltpu.VMEM((192, 240), BF),
-            pltpu.SemaphoreType.DMA((BLOCKS,)),
-        ],
-        compiler_params=pltpu.CompilerParams(vmem_limit_bytes=44 << 20),
-        name="ocean",
-    )(ocean, mask, west, east, w1, b1)
+        compiler_params=pltpu.CompilerParams(vmem_limit_bytes=24 << 20),
+        name="margins",
+    )(*args)
 
 
 def main_kernel(
-    part_ref, m3_ref, coarse_ref, own_ref, west_ref, east_ref, cown_ref, cwest_ref, ceast_ref,
+    part_ref, m3_ref, coarse_ref, first_ref, last_ref, west_ref, east_ref, cown_ref, cwest_ref, ceast_ref,
     w1_ref, b1_ref, w2_ref, b2_ref, out_ref,
-    cx_ref, fine_ref, p_ref, h_ref, add_ref, band1_ref, band2_ref, side1_ref, side2_ref, sem,
+    cx_ref, fine_ref, p_ref, h_ref, add_ref, band1_ref, band2_ref, side1_ref, side2_ref, pair_ref, sem,
 ):
     def fetch(block):
-        return pltpu.make_async_copy(
-            part_ref.at[pl.ds(block * 24, 24)], p_ref.at[pl.ds(block * 24, 24)], sem.at[block]
-        )
+        at = pl.ds(block * 24, 24)
+        return pltpu.make_async_copy(part_ref.at[at], p_ref.at[at], sem.at[block])
 
     for block in range(BLOCKS):
         fetch(block).start()
@@ -377,8 +402,13 @@
             w1 = w1_ref[u, v]
             at = (u * 3 + v) * 2 * FLD
             side1_ref[:, at : at + 2 * FLD] = w1
-        side2_ref[0, :, u * HID : u * HID + HID] = w2_ref[u, 0]
-        side2_ref[1, :, u * HID : u * HID + HID] = w2_ref[u, 2]
+        for side in range(2):
+            at = u * HID
+            side2_ref[side, 0:OUT, at : at + HID] = w2_ref[u, 2 * side]
+            side2_ref[side, OUT : 2 * OUT, at : at + HID] = jnp.zeros((OUT, HID), BF)
+            at = (3 + u) * HID
+            side2_ref[side, 0:OUT, at : at + HID] = w2_ref[u, 1]
+            side2_ref[side, OUT : 2 * OUT, at : at + HID] = w2_ref[u, 2 * side]
 
     rep = (subs((256, ROWS)) == lanes((256, ROWS)) // 2).astype(BF)
 
@@ -388,28 +418,49 @@
 
     w2c = column(cwest_ref[...], west_ref[0])
     w1c = column(cwest_ref[...], west_ref[1])
-    o0c = column(cown_ref[0], own_ref[0])
-    o255c = column(cown_ref[1], own_ref[3])
+    o0c = column(cown_ref[0], first_ref[0])
+    o1c = column(cown_ref[0], first_ref[1])
+    o254c = column(cown_ref[1], last_ref[0])
+    o255c = column(cown_ref[1], last_ref[1])
     e1c = column(ceast_ref[...], east_ref[0])
     e2c = column(ceast_ref[...], east_ref[1])
-    for side, cols in ((0, (w2c, w1c, o0c)), (1, (o255c, e1c, e2c))):
-        x = jnp.concatenate(cols, axis=0)
-        xt = jnp.concatenate([pltpu.roll(x, 1, 1), x, pltpu.roll(x, ROWS - 1, 1)], axis=0)
-        hid = jnp.dot(side1_ref[...], xt, preferred_element_type=F32)
-        hid = jnp.maximum(hid + b1_ref[...], 0.0).astype(BF)
-        ht = jnp.concatenate([pltpu.roll(hid, 1, 1), hid, pltpu.roll(hid, ROWS - 1, 1)], axis=0)
-        add_ref[side] = jnp.dot(side2_ref[side], ht, preferred_element_type=F32)
+
+    def around(x):
+        return jnp.concatenate([pltpu.roll(x, 1, 1), x, pltpu.roll(x, ROWS - 1, 1)], axis=0)
+
+    ends = []
+    for side, outer, inner in (
+        (0, (w2c, w1c, o0c), (w1c, o0c, o1c)),
+        (1, (o255c, e1c, e2c), (o254c, o255c, e1c)),
+    ):
+        hidden = []
+        for cols in (outer, inner):
+            xt = around(jnp.concatenate(cols, axis=0))
+            hid = jnp.dot(side1_ref[...], xt, preferred_element_type=F32)
+            hidden.append(around(jnp.maximum(hid + b1_ref[:, 0:1], 0.0).astype(BF)))
+        ends.append(jnp.dot(side2_ref[side], jnp.concatenate(hidden, axis=0), preferred_element_type=F32))
+    phase = lanes((OUT, 128)) & 3
+    for chunk in range(3):
+        at = slice(chunk * 128, chunk * 128 + 128)
+        c0 = ends[0][0:OUT, at]
+        c1 = pltpu.roll(ends[0][OUT:, at], 1, 1)
+        c254 = pltpu.roll(ends[1][OUT:, at], 126, 1)
+        c255 = pltpu.roll(ends[1][0:OUT, at], 127, 1)
+        for q in range(4):
+            z = jnp.where(phase == q, c0, jnp.where(phase == (q + 1) % 4, c1, c255))
+            add_ref[q, chunk] = jnp.where(phase == (q + 2) % 4, c254, z)
 
     lane = lanes((FLD, 128))
     for chunk, count in ((0, 128), (128, 64)):
+        west = cwest_ref[:, chunk : chunk + 128]
+        east = pltpu.roll(ceast_ref[:, chunk : chunk + 128], 1, 1)
+        for q in range(2):
+            pair_ref[q] = jnp.where((lane & 1) == q, west, east)
 
         def extend(i, carry):
             r = chunk + i
-            west = pltpu.roll(cwest_ref[:, chunk : chunk + 128], 128 - i, 1)
-            east = pltpu.roll(ceast_ref[:, chunk : chunk + 128], 129 - i, 1)
             cx_ref[r, :, 0:128] = coarse_ref[r]
-            both = jnp.where(lane == 0, west, jnp.where(lane == 1, east, jnp.zeros_like(east)))
-            cx_ref[r, :, 128:256] = both
+            cx_ref[r, :, 128:256] = pltpu.roll(pair_ref[i & 1], 128 - i, 1)
             return carry
 
         lax.fori_loop(0, count, extend, 0, unroll=16)
@@ -436,7 +487,7 @@
     h_ref[0] = hzero
     h_ref[ROWS + 1] = hzero
 
-    def conv1(block):
+    def conv1(block, carry):
         fetch(block).wait()
         for j in range(4):
             y0 = block * 24 + j * 6
@@ -453,37 +504,34 @@
                 t = jnp.dot(band1_ref[...], x, preferred_element_type=F32)
                 t = t + p_ref[pl.ds(y0 + 3 * k, 3)].reshape(192, COLS).astype(F32)
                 h_ref[pl.ds(y0 + 3 * k + 1, 3)] = jnp.maximum(t, 0.0).astype(BF).reshape(3, HID, COLS)
-
-    b2 = b2_ref[...]
+        return carry
+
+    lax.fori_loop(0, BLOCKS, conv1, 0)
+
+    b2 = b2_ref[:, 0:1]
     lane8 = lanes((OUT, 128))
 
-    def conv2(first, count):
-        for k in range(count):
-            j = jnp.maximum(first + k, 0)
+    def conv2(block, carry):
+        for k in range(8):
+            j = block * 8 + k
             x = h_ref[pl.ds(6 * j, 8)].reshape(512, COLS)
             t = jnp.dot(band2_ref[...], x, preferred_element_type=F32).reshape(6, 3, OUT, COLS)
             for r in range(6):
                 y = 6 * j + r
-                base = pl.multiple_of((y // 128) * 128, 128)
-                i = y % 128
-                west = pltpu.roll(add_ref[0, :, pl.ds(base, 128)], 128 - i, 1)
-                east = pltpu.roll(add_ref[1, :, pl.ds(base, 128)], 127 - i, 1)
+                ends = pltpu.roll(add_ref[y & 3, y >> 7], 128 - (y & 127), 1)
                 up = pltpu.roll(t[r, 0], 1, 1)
                 down = pltpu.roll(t[r, 2], COLS - 1, 1)
-                mid = t[r, 1] + b2
                 m = m3_ref[1, pl.ds(y, 1), :]
-                lo = mid[:, :128] + jnp.where(lane8 == 0, west, up[:, :128]) + down[:, :128]
-                hi = mid[:, 128:] + up[:, 128:] + jnp.where(lane8 == 127, east, down[:, 128:])
+                lo = jnp.where(lane8 == 0, 0.0, t[r, 1, :, :128]) + b2
+                lo = lo + jnp.where(lane8 < 2, ends, up[:, :128]) + down[:, :128]
+                hi = jnp.where(lane8 == 127, 0.0, t[r, 1, :, 128:]) + b2
+                hi = hi + up[:, 128:] + jnp.where(lane8 > 125, ends, down[:, 128:])
                 out_ref[y, :, 0:128] = (lo * m[:, :128]).astype(BF)
                 out_ref[y, :, 128:256] = (hi * m[:, 128:]).astype(BF)
 
-    def both(block, carry):
-        conv2(4 * block - 5, 4)
-        conv1(block)
         return carry
 
-    lax.fori_loop(0, BLOCKS, both, 0)
-    conv2(4 * BLOCKS - 5, 5)
+    lax.fori_loop(0, 8, conv2, 0)
 
 
 def main_conv(*args):
@@ -491,17 +539,18 @@
     return pl.pallas_call(
         main_kernel,
         out_shape=jax.ShapeDtypeStruct((ROWS, OUT, COLS), BF),
-        in_specs=[pl.BlockSpec(memory_space=pl.ANY)] + [vmem] * 12,
+        in_specs=[pl.BlockSpec(memory_space=pl.ANY)] + [vmem] * 13,
         scratch_shapes=[
             pltpu.VMEM((HALF, FLD, COLS), BF),
             pltpu.VMEM((HALF + 2, 48, COLS), BF),
             pltpu.VMEM((ROWS, HID, COLS), BF),
             pltpu.VMEM((ROWS + 2, HID, COLS), BF),
-            pltpu.VMEM((2, OUT, ROWS), F32),
+            pltpu.VMEM((4, 3, OUT, 128), F32),
             pltpu.VMEM((192, 240), BF),
             pltpu.VMEM((144, 512), BF),
             pltpu.VMEM((HID, 288), BF),
-            pltpu.VMEM((2, OUT, 192), BF),
+            pltpu.VMEM((2, 2 * OUT, 384), BF),
+            pltpu.VMEM((2, FLD, 128), BF),
             pltpu.SemaphoreType.DMA((BLOCKS,)),
         ],
         compiler_params=pltpu.CompilerParams(vmem_limit_bytes=44 << 20),
@@ -519,10 +568,10 @@
 
 
 def patch_kernel(
-    pos_ref, fold_ref, south_ref, low_ref, mid_ref, top_ref, north_ref, tops_ref, strip_ref,
+    fold_ref, south_ref, low_ref, mid_ref, top_ref, north_ref, tops_ref, strip_ref,
     w1_ref, b1_ref, w2_ref, b2_ref, main_ref, out_ref, in_ref, res_ref, sem,
 ):
-    gy, gx = pos_ref[0], pos_ref[1]
+    gy, gx = lax.axis_index("gy"), lax.axis_index("gx")
     signs = jnp.where(
         (subs((2 * FLD, PAD)) < 8) | (subs((2 * FLD, PAD)) == 16) | (subs((2 * FLD, PAD)) == 17), -1.0, 1.0
     )
@@ -579,7 +628,7 @@
         in_ref[14] = last * signs
 
     def hidden(rows, flip):
-        total = jnp.broadcast_to(b1_ref[...], (HID, PAD))
+        total = jnp.broadcast_to(b1_ref[:, 0:1], (HID, PAD))
         for u in range(3):
             x = in_ref[rows + u]
             for v in range(3):
@@ -603,7 +652,7 @@
         else:
             hid[3] = jnp.where(gy == 7, virtual, hid[3])
         for r in range(2):
-            total = jnp.broadcast_to(b2_ref[...], (OUT, PAD))
+            total = jnp.broadcast_to(b2_ref[:, 0:1], (OUT, PAD))
             for u in range(3):
                 x = hid[r + u]
                 for v in range(3):
@@ -629,14 +678,14 @@
     return pl.pallas_call(
         patch_kernel,
         out_shape=jax.ShapeDtypeStruct((ROWS, OUT, COLS), BF),
-        in_specs=[smem, smem] + [vmem] * 11 + [hbm],
+        in_specs=[smem] + [vmem] * 11 + [hbm],
         out_specs=hbm,
         scratch_shapes=[
             pltpu.VMEM((15, 2 * FLD, PAD), F32),
             pltpu.VMEM((4, OUT, COLS), BF),
             pltpu.SemaphoreType.DMA((2,)),
         ],
-        input_output_aliases={13: 0},
+        input_output_aliases={12: 0},
         compiler_params=pltpu.CompilerParams(vmem_limit_bytes=24 << 20),
         name="patch",
     )(*args)
@@ -655,24 +704,20 @@
 def per_device(
     ocean, atm, dest_tile, dest_row, live, land_mask, fold_pair, w1, b1, w2, b2
 ):
-    edges = edge_columns(ocean, land_mask)
-    west = shift_gx(edges[2:4], 1)
-    east = shift_gx(edges[0:2], -1)
-
-    tile = dest_tile[:, 0]
-    same = tile[:, None] == tile[None, :]
-    before = jnp.arange(HALF)[:, None] > jnp.arange(HALF)[None, :]
-    rank = jnp.sum((same & before).astype(I32), axis=1)
-    info = jnp.stack([tile * 4 + rank, jnp.where(live == 1, dest_row + 1, 0)])
-    info = jnp.pad(info, ((0, 0), (0, 64)), constant_values=-1)
-    outgoing = pack(info, atm.reshape(2 * HALF, 8, 128))
-    outgoing, west, east = lax.optimization_barrier((outgoing, west, east))
+    outgoing = pack(
+        dest_tile.reshape(1, HALF), dest_row.reshape(1, HALF), live.reshape(1, HALF), atm.reshape(2 * HALF, 8, 128)
+    )
     incoming = lax.all_to_all(
         outgoing.reshape(DEV, STEP, 8, 128), ("gy", "gx"), split_axis=0, concat_axis=0, tiled=True
     )
-    b1c = b1[:, None]
-    b2c = b2[:, None]
-    part, m3, strip = ocean_part(ocean, land_mask, west, east, w1, b1c)
+    ocean, land_mask, _ = lax.optimization_barrier((ocean, land_mask, outgoing))
+    first, last = edge_columns(ocean, land_mask)
+    west = shift_gx(last, 1)
+    east = shift_gx(first, -1)
+    part, rows, w1, b1c, b2c = ocean_part(
+        ocean, land_mask, w1.swapaxes(2, 3), b1.reshape(1, HID), b2.reshape(1, OUT)
+    )
+    m3, strip = margins(land_mask, west, east, rows)
 
     coarse, ccols, cwest, ceast, low, mid, top, tops = coarse_sums(
         incoming.reshape(DEV * STEP, 8, 128), strip
@@ -681,11 +726,10 @@
     north = shift_gy(low, -1)
     tops = lax.all_to_all(tops, "gx", split_axis=0, concat_axis=0, tiled=True)
     out = main_conv(
-        part, m3, coarse, edges, west, east, ccols, cwest, ceast, w1, b1c, w2, b2c,
-    )
-    pos = jnp.stack([lax.axis_index("gy"), lax.axis_index("gx")]).astype(I32)
+        part, m3, coarse, first, last, west, east, ccols, cwest, ceast, w1, b1c, w2, b2c,
+    )
     return patch_rows(
-        pos, fold_pair, south, low, mid, top, north, tops, strip, w1, b1c, w2, b2c, out
+        fold_pair, south, low, mid, top, north, tops, strip, w1, b1c, w2, b2c, out
     )
 
 

time: 94.8 us -> 82.3 us (0.87)
  local copies, waits for them, and re-layouts: 8.42 us -> 2.57 us
  Pallas kernels: 50.4 us -> 46.4 us
  waiting for transfers between devices: 6.97 us -> 4.65 us
    all_to_all x1, waiting for transfers between devices: 6.96 us -> 0.01 us  [per_device(): lax.all_to_all(outgoing.reshape(DEV, STEP, 8, 128), ('gy', 'gx'), split_a...]
    unnamed x33 -> x38, local copies, waits for them, and re-layouts: 7.65 us -> 2.57 us
    ppermute x2, waiting for transfers between devices: 0.01 us -> 4.64 us  [shift_gx(): return lax.ppermute(x, 'gx', [(i, (i + step) % n) for i in range(n)])]
    pallas_call x1, Pallas kernels: 19.8 us -> 16.8 us  [main_conv(): pl.pallas_call(main_kernel, out_shape=jax.ShapeDtypeStruct((ROWS, OUT, CO...]
    pallas_call x1, Pallas kernels: 12.2 us -> 10.1 us  [ocean_part(): pl.pallas_call(ocean_kernel, out_shape=(jax.ShapeDtypeStruct((ROWS, HID,...]
    pallas_call x1 -> x2, Pallas kernels: 3.53 us -> 4.06 us  [the longest x1 3.61 us: edge_columns(): pl.pallas_call(edge_kernel, out_shape=(jax.ShapeDtypeStruct((2, 2 * FLD,...]
  transfers between devices with their start and end apart: 6 -> 6, of which waited for: 1 -> 1; matrix products, arithmetic and copies ran while one was open for 2% -> 0% of each run, Pallas kernels for 39% -> 38%
where the time goes in v3:
time: 82.3 us; the launch traced here: 82 us
  Pallas kernels  46.4 us (56%)
  starting transfers between devices  28 us (34%)
  waiting for transfers between devices  4.65 us (6%)
  local copies, waits for them, and re-layouts  2.57 us (3%)
    pallas_call x1, Pallas kernels, main_conv(): pl.pallas_call(main_kernel, out_shape=jax.ShapeDtypeStruct((ROWS, OUT, CO...  16.8 us
    all_to_all x1, starting transfers between devices, per_device(): lax.all_to_all(outgoing.reshape(DEV, STEP, 8, 128), ('gy', 'gx'), split_a...  10.4 us
    pallas_call x1, Pallas kernels, ocean_part(): pl.pallas_call(ocean_kernel, out_shape=(jax.ShapeDtypeStruct((ROWS, HID,...  10.1 us
    ppermute x2, starting transfers between devices, shift_gy(): lax.ppermute(x, 'gy', [(i, i + step) for i in range(n) if 0 <= i + step <...  9.44 us
    pallas_call x1, Pallas kernels, coarse_sums(): pl.pallas_call(coarse_kernel, out_shape=(jax.ShapeDtypeStruct((HALF, FLD,...  7.28 us
    all_to_all x1, starting transfers between devices, per_device(): tops = lax.all_to_all(tops, 'gx', split_axis=0, concat_axis=0, tiled=True)  5.44 us
    pallas_call x1, Pallas kernels, pack(): pl.pallas_call(pack_kernel, out_shape=jax.ShapeDtypeStruct((DEV * STEP, 8...  5.08 us
    ppermute x2, waiting for transfers between devices, shift_gx(): return lax.ppermute(x, 'gx', [(i, (i + step) % n) for i in range(n)])  4.64 us
  transfers between devices with their start and end apart: 6, of which 1 were waited for; matrix products, arithmetic and copies ran while one was open for 0% of the time, Pallas kernels for 38%

profile of v3, /device:TPU:66, one launch (start us, length us, event | category | flops | bytes accessed | tf_op | source)
XLA Modules:
  0.0 82.0 jit_solution(9055360910386669908)
XLA Ops:
  0.0 5.1 %pack.1 = bf16[896,8,128]{2,1,0:T(8,128)(2,1)} custom-call(s32[1,192]{1,0:T(1,128)} %bitcast.14, s32[1,192]{1,0:T(1,128)} %bitcast.15, s32[1,192]{1,0:T(1,128)} %bitcast.16, bf16[384,8,128]{2,1,0:T(8,128)(2,1)} %bitcast.13), custom_call_target="tpu_custom_call" | custom-call | tf_op jit(solution)/shard_map/pack/pallas_call | solution.py:100
  5.1 0.0 copy-start
  5.1 0.0 copy-start.1
  5.1 10.4 %all-to-all-start = ((bf16[128,7,8,128]{3,2,1,0:T(8,128)(2,1)}), bf16[128,7,8,128]{3,2,1,0:T(8,128)(2,1)}, u32[]{:S(2)}, u32[]{:S(2)}) async-start(bf16[128,7,8,128]{3,2,1,0:T(8,128)(2,1)} %bitcast.12), calls=%async_computation | async-start | bytes 3670016 | tf_op jit(solution)/shard_map/all_to_all | solution.py:710
  15.6 0.0 copy-done
  15.6 0.0 copy-start.11
  15.6 0.0 copy-start.16
  15.6 0.0 copy-start.17
  15.6 3.6 %edges.1 = (bf16[2,32,384]{2,1,0:T(8,128)(2,1)S(1)}, bf16[2,32,384]{2,1,0:T(8,128)(2,1)S(1)}) custom-call(bf16[384,16,256]{2,1,0:T(8,128)(2,1)S(1)} %copy-done, s32[384,256]{1,0:T(8,128)S(1)} %copy-done.1), custom_call_target="tpu_custom_call" | custom-call | tf_op jit(solution)/shard_map/edges/pallas_call | solution.py:243
  19.2 0.2 collective-permute-start
  19.5 2.5 %collective-permute-start.1 = (bf16[2,32,384]{2,1,0:T(8,128)(2,1)S(1)}, bf16[2,32,384]{2,1,0:T(8,128)(2,1)S(1)}, u32[]{:S(2)}, u32[]{:S(2)}) collective-permute-start(bf16[2,32,384]{2,1,0:T(8,128)(2,1)S(1)} %get-tuple-element.27.first_ref), channel_id=1, source_target_pairs={{0,15},{1,0},{2,1},{3,2},{4,3},{5,4},{6,5},{7,6},{8,7},{9,8},{10,9... | collective-permute-start | bytes 147464 | tf_op jit(solution)/shard_map/ppermute | solution.py:696
  22.0 10.1 %ocean.1 = (bf16[384,64,256]{2,1,0:T(8,128)(2,1)}, bf16[8,32,384]{2,1,0:T(8,128)(2,1)S(1)}, bf16[3,3,64,32]{3,2,1,0:T(8,128)(2,1)S(1)}, f32[64,128]{1,0:T(8,128)S(1)}, f32[8,128]{1,0:T(8,128)S(1)}) custom-call(bf16[384,16,256]{2,1,0:T(8,128)(2,1)S(1)} %copy-done, s32[384,256]{1,0:T(8,128)S(1)} %copy-done.1, bf16[3,3,32,64]{3,2,1,0:T(8,128)(2,1)S(1)} %bitcast.9, ...), custom_call_target="tpu_custom_call" | custom-call | tf_op jit(solution)/shard_map/ocean/pallas_call | solution.py:320
  32.0 0.0 copy-start.2
  32.1 0.7 copy-done.2
  32.7 0.6 copy-done.8
  33.3 4.6 %collective-permute-done.west_ref = bf16[2,32,384]{2,1,0:T(8,128)(2,1)S(1)} collective-permute-done((bf16[2,32,384]{2,1,0:T(8,128)(2,1)S(1)}, bf16[2,32,384]{2,1,0:T(8,128)(2,1)S(1)}, u32[]{:S(2)}, u32[]{:S(2)}) %collective-permute-start) | collective-permute-done | bytes 49184 | tf_op jit(solution)/shard_map/ppermute | solution.py:696
  38.0 0.0 collective-permute-done.1.east_ref
  38.0 0.0 copy-start.10
  38.0 0.5 margins.1
  38.5 0.6 copy-done.4
  39.1 0.6 copy-done.6
  39.7 0.0 all-to-all-done
  39.7 7.3 %coarse.1 = (bf16[192,16,128]{2,1,0:T(8,128)(2,1)S(1)}, bf16[2,16,256]{2,1,0:T(8,128)(2,1)S(1)}, bf16[16,256]{1,0:T(8,128)(2,1)S(1)}, bf16[16,256]{1,0:T(8,128)(...) custom-call(bf16[896,8,128]{2,1,0:T(8,128)(2,1)} %bitcast.5.inc_ref,, ...), custom_call_target="tpu_custom_call" | custom-call | tf_op jit(solution)/shard_map/coarse/pallas_call | solution.py:191
  47.0 5.4 %all-to-all-start.1 = ((bf16[16,2,32,256]{3,2,1,0:T(8,128)(2,1)}), bf16[16,2,32,256]{3,2,1,0:T(8,128)(2,1)S(1)}, u32[]{:S(2)}, u32[]{:S(2)}) async-start(bf16[16,2,32,256]{3,2,1,0:T(8,128)(2,1)} %get-tuple-element.33), calls=%async_computation.1 | async-start | bytes 1048576 | tf_op jit(solution)/shard_map/all_to_all | solution.py:727
  52.5 3.3 %collective-permute-start.2 = (bf16[2,32,384]{2,1,0:T(8,128)(2,1)S(1)}, bf16[2,32,384]{2,1,0:T(8,128)(2,1)S(1)}, u32[]{:S(2)}, u32[]{:S(2)}) collective-permute-start(bf16[2,32,384]{2,1,0:T(8,128)(2,1)S(1)} %get-tuple-element.30.top_ref), channel_id=1, source_target_pairs={{0,16},{16,32},{32,48},{48,64},{64,80},{80,96},{96,112},{1,17},{17... | collective-permute-start | bytes 147464 | tf_op jit(solution)/shard_map/ppermute | solution.py:701
  55.7 6.2 %collective-permute-start.3 = (bf16[2,32,384]{2,1,0:T(8,128)(2,1)S(1)}, bf16[2,32,384]{2,1,0:T(8,128)(2,1)S(1)}, u32[]{:S(2)}, u32[]{:S(2)}) collective-permute-start(bf16[2,32,384]{2,1,0:T(8,128)(2,1)S(1)} %get-tuple-element.31.low_ref), channel_id=1, source_target_pairs={{16,0},{32,16},{48,32},{64,48},{80,64},{96,80},{112,96},{17,1},{33... | collective-permute-start | bytes 147464 | tf_op jit(solution)/shard_map/ppermute | solution.py:701
  62.0 0.0 copy-start.18
  62.0 16.8 %convs.1.main_ref = bf16[384,8,256]{2,1,0:T(8,128)(2,1)} custom-call(bf16[384,64,256]{2,1,0:T(8,128)(2,1)} %get-tuple-element.37.part_ref, f32[3,384,256]{2,1,0:T(8,128)S(1)} %get-tuple-element.38.m3_ref, bf16[192,16,128]{2,1,0:T(8,128)(2,1)S(1)} %get-tuple-element.39.coarse_ref, bf16[2,32,384]{2,1,0:T(8,128)(2,1)S(1)} %copy-done.13, ...), custom_call_target="tpu_custom_call" | custom-call | tf_op jit(solution)/shard_map/convs/pallas_call | solution.py:539
  78.8 0.0 collective-permute-done.2.south_ref
  78.9 0.0 collective-permute-done.3.north_ref
  78.9 0.0 all-to-all-done.1.tops_ref
  78.9 3.1 %patch.1 = bf16[384,8,256]{2,1,0:T(8,128)(2,1)} custom-call(s32[16]{0:T(128)S(1)} %copy-done.18, bf16[2,32,384]{2,1,0:T(8,128)(2,1)S(1)} %collective-permute-done.2.south_ref, bf16[2,32,384]{2,1,0:T(8,128)(2,1)S(1)} %get-tuple-element.31.low_ref, bf16[4,32,384]{2,1,0:T(8,128)(2,1)S(1)} %get-tuple-element.32.mid_ref, ...), custom_call_target="tpu_custom_call", output_to_operand_aliasing={{}: (12, {})} | custom-call | tf_op jit(solution)/shard_map/patch/pallas_call | solution.py:678
  (25 shorter events, 0.0 us)
Async XLA Ops:
  5.1 10.5 %copy-start = (bf16[384,16,256]{2,1,0:T(8,128)(2,1)S(1)}, bf16[384,16,256]{2,1,0:T(8,128)(2,1)}, u32[]{:S(2)}) copy-start(bf16[384,16,256]{2,1,0:T(8,128)(2,1)} %ocean_ref.1) | copy-start | bytes 9437188
  5.1 10.5 %copy-start.1 = (s32[384,256]{1,0:T(8,128)S(1)}, s32[384,256]{1,0:T(8,128)}, u32[]{:S(2)}) copy-start(s32[384,256]{1,0:T(8,128)} %mask_ref.2) | copy-start | bytes 1179652
  5.1 34.6 %all-to-all-start = ((bf16[128,7,8,128]{3,2,1,0:T(8,128)(2,1)}), bf16[128,7,8,128]{3,2,1,0:T(8,128)(2,1)}, u32[]{:S(2)}, u32[]{:S(2)}) async-start(bf16[128,7,8,128]{3,2,1,0:T(8,128)(2,1)} %bitcast.12), calls=%async_computation | async-start | bytes 3670016 | tf_op jit(solution)/shard_map/all_to_all | solution.py:710
  15.6 6.4 %copy-start.11 = (bf16[3,3,64,32]{2,3,1,0:T(8,128)(2,1)S(1)}, bf16[3,3,64,32]{2,3,1,0:T(8,128)(2,1)}, u32[]{:S(2)}) copy-start(bf16[3,3,64,32]{2,3,1,0:T(8,128)(2,1)} %param.18) | copy-start | bytes 110596
  15.6 6.4 %copy-start.16 = (f32[64]{0:T(128)S(1)}, f32[64]{0:T(128)}, u32[]{:S(2)}) copy-start(f32[64]{0:T(128)} %param.19) | copy-start | bytes 772
  15.6 6.4 %copy-start.17 = (f32[8]{0:T(128)S(1)}, f32[8]{0:T(128)}, u32[]{:S(2)}) copy-start(f32[8]{0:T(128)} %param.21) | copy-start | bytes 100
  19.2 18.8 %copy-start.12 = (bf16[2,32,384]{2,1,0:T(8,128)(2,1)}, bf16[2,32,384]{2,1,0:T(8,128)(2,1)S(1)}, u32[]{:S(2)}) copy-start(bf16[2,32,384]{2,1,0:T(8,128)(2,1)S(1)} %get-tuple-element.27.first_ref) | copy-start | bytes 147460
  19.2 18.8 %copy-start.14 = (bf16[2,32,384]{2,1,0:T(8,128)(2,1)}, bf16[2,32,384]{2,1,0:T(8,128)(2,1)S(1)}, u32[]{:S(2)}) copy-start(bf16[2,32,384]{2,1,0:T(8,128)(2,1)S(1)} %get-tuple-element.26.last_ref) | copy-start | bytes 147460
  19.2 18.7 %collective-permute-start = (bf16[2,32,384]{2,1,0:T(8,128)(2,1)S(1)}, bf16[2,32,384]{2,1,0:T(8,128)(2,1)S(1)}, u32[]{:S(2)}, u32[]{:S(2)}) collective-permute-start(bf16[2,32,384]{2,1,0:T(8,128)(2,1)S(1)} %get-tuple-element.26.last_ref), channel_id=1, source_target_pairs={{0,1},{1,2},{2,3},{3,4},{4,5},{5,6},{6,7},{7,8},{8,9},{9,10},{10,1... | collective-permute-start | bytes 147464 | tf_op jit(solution)/shard_map/ppermute | solution.py:696
  19.5 18.5 %collective-permute-start.1 = (bf16[2,32,384]{2,1,0:T(8,128)(2,1)S(1)}, bf16[2,32,384]{2,1,0:T(8,128)(2,1)S(1)}, u32[]{:S(2)}, u32[]{:S(2)}) collective-permute-start(bf16[2,32,384]{2,1,0:T(8,128)(2,1)S(1)} %get-tuple-element.27.first_ref), channel_id=1, source_target_pairs={{0,15},{1,0},{2,1},{3,2},{4,3},{5,4},{6,5},{7,6},{8,7},{9,8},{10,9... | collective-permute-start | bytes 147464 | tf_op jit(solution)/shard_map/ppermute | solution.py:696
  32.0 0.7 copy-start.2
  32.7 0.6 copy-start.8
  38.0 23.9 %copy-start.3 = (bf16[3,3,64,32]{3,2,1,0:T(8,128)(2,1)S(1)}, bf16[3,3,64,32]{3,2,1,0:T(8,128)(2,1)}, u32[]{:S(2)}) copy-start(bf16[3,3,64,32]{3,2,1,0:T(8,128)(2,1)} %copy-done.2) | copy-start | bytes 110596
  38.0 23.9 %copy-start.9 = (f32[64,128]{1,0:T(8,128)S(1)}, f32[64,128]{1,0:T(8,128)}, u32[]{:S(2)}) copy-start(f32[64,128]{1,0:T(8,128)} %copy-done.8) | copy-start | bytes 98308
  38.0 23.9 %copy-start.10 = (bf16[3,3,8,64]{3,2,1,0:T(8,128)(2,1)S(1)}, bf16[3,3,8,64]{3,2,1,0:T(8,128)(2,1)}, u32[]{:S(2)}) copy-start(bf16[3,3,8,64]{3,2,1,0:T(8,128)(2,1)} %w2_ref.3) | copy-start | bytes 27652
  38.0 23.9 %copy-start.13 = (bf16[2,32,384]{2,1,0:T(8,128)(2,1)S(1)}, bf16[2,32,384]{2,1,0:T(8,128)(2,1)}, u32[]{:S(2)}) copy-start(bf16[2,32,384]{2,1,0:T(8,128)(2,1)} %copy-done.12) | copy-start | bytes 147460
  38.5 0.6 copy-start.4
  39.1 0.6 copy-start.6
  39.7 22.2 %copy-start.15 = (bf16[2,32,384]{2,1,0:T(8,128)(2,1)S(1)}, bf16[2,32,384]{2,1,0:T(8,128)(2,1)}, u32[]{:S(2)}) copy-start(bf16[2,32,384]{2,1,0:T(8,128)(2,1)} %copy-done.14) | copy-start | bytes 147460
  39.7 22.2 %copy-start.5 = (bf16[2,32,384]{2,1,0:T(8,128)(2,1)S(1)}, bf16[2,32,384]{2,1,0:T(8,128)(2,1)}, u32[]{:S(2)}) copy-start(bf16[2,32,384]{2,1,0:T(8,128)(2,1)} %copy-done.4) | copy-start | bytes 147460
  39.7 22.3 %copy-start.7 = (bf16[2,32,384]{2,1,0:T(8,128)(2,1)S(1)}, bf16[2,32,384]{2,1,0:T(8,128)(2,1)}, u32[]{:S(2)}) copy-start(bf16[2,32,384]{2,1,0:T(8,128)(2,1)} %copy-done.6) | copy-start | bytes 147460
  47.0 31.8 %all-to-all-start.1 = ((bf16[16,2,32,256]{3,2,1,0:T(8,128)(2,1)}), bf16[16,2,32,256]{3,2,1,0:T(8,128)(2,1)S(1)}, u32[]{:S(2)}, u32[]{:S(2)}) async-start(bf16[16,2,32,256]{3,2,1,0:T(8,128)(2,1)} %get-tuple-element.33), calls=%async_computation.1 | async-start | bytes 1048576 | tf_op jit(solution)/shard_map/all_to_all | solution.py:727
  52.5 26.4 %collective-permute-start.2 = (bf16[2,32,384]{2,1,0:T(8,128)(2,1)S(1)}, bf16[2,32,384]{2,1,0:T(8,128)(2,1)S(1)}, u32[]{:S(2)}, u32[]{:S(2)}) collective-permute-start(bf16[2,32,384]{2,1,0:T(8,128)(2,1)S(1)} %get-tuple-element.30.top_ref), channel_id=1, source_target_pairs={{0,16},{16,32},{32,48},{48,64},{64,80},{80,96},{96,112},{1,17},{17... | collective-permute-start | bytes 147464 | tf_op jit(solution)/shard_map/ppermute | solution.py:701
  55.7 23.1 %collective-permute-start.3 = (bf16[2,32,384]{2,1,0:T(8,128)(2,1)S(1)}, bf16[2,32,384]{2,1,0:T(8,128)(2,1)S(1)}, u32[]{:S(2)}, u32[]{:S(2)}) collective-permute-start(bf16[2,32,384]{2,1,0:T(8,128)(2,1)S(1)} %get-tuple-element.31.low_ref), channel_id=1, source_target_pairs={{16,0},{32,16},{48,32},{64,48},{80,64},{96,80},{112,96},{17,1},{33... | collective-permute-start | bytes 147464 | tf_op jit(solution)/shard_map/ppermute | solution.py:701
  62.0 16.9 %copy-start.18 = (s32[16]{0:T(128)S(1)}, s32[16]{0:T(128)}, u32[]{:S(2)}) copy-start(s32[16]{0:T(128)} %fold_ref.1) | copy-start | bytes 196

commit v4 on v3

--- a/solution.py
+++ b/solution.py
@@ -34,7 +34,20 @@
 STEP = 2 * CAP + 1
 
 
-def pack_kernel(tile_ref, row_ref, live_ref, atm_ref, out_ref, q_ref, code_ref, info_ref, sem):
+PIECES = 8
+
+
+def pack_kernel(
+    tile_ref, row_ref, live_ref, atm_hbm, out_hbm, atm_ref, out_ref, q_ref, code_ref, info_ref,
+    sem, in_sem, out_sem,
+):
+    loads, stores = [], []
+    for c in range(PIECES):
+        at = pl.ds(c * (2 * HALF // PIECES), 2 * HALF // PIECES)
+        loads.append(pltpu.make_async_copy(atm_hbm.at[at], atm_ref.at[at], in_sem.at[c]))
+        at = pl.ds(c * (DEV * STEP // PIECES), DEV * STEP // PIECES)
+        stores.append(pltpu.make_async_copy(out_ref.at[at], out_hbm.at[at], out_sem.at[c]))
+        loads[c].start()
     across = jnp.concatenate([tile_ref[...].astype(F32), jnp.full((1, 64), -1.0, F32)], axis=1)
     column = jnp.broadcast_to(across, (128, 256))
     column = jnp.concatenate([column[:, :128].T, column[:, 128:].T[:64]], axis=0)
@@ -45,25 +58,22 @@
     code_ref[...] = code.astype(I32)
     copy = pltpu.make_async_copy(code_ref, info_ref, sem)
     copy.start()
-    copy.wait()
+    for load in loads:
+        load.wait()
     lane = lanes((FLD, 128))
     first, last = [], []
     for chunk, count in ((0, 128), (128, 64)):
 
-        def place(i, carry):
+        def ends(i, carry):
             c0, c1 = carry
-            n = chunk + i
-            code = info_ref[0, n]
-            block = atm_ref[pl.ds(2 * n, 2)]
-            out_ref[pl.ds(STEP * (code >> 2) + 2 * (code & 3), 2)] = block
-            block = block.reshape(FLD, 128)
+            block = atm_ref[pl.ds(2 * (chunk + i), 2)].reshape(FLD, 128)
             here = lane == i
             c0 = jnp.where(here, pltpu.roll(block, i, 1), c0)
             c1 = jnp.where(here, pltpu.roll(block, i + 1, 1), c1)
             return c0, c1
 
         zero = jnp.zeros((FLD, 128), BF)
-        c0, c1 = lax.fori_loop(0, count, place, (zero, zero), unroll=16)
+        c0, c1 = lax.fori_loop(0, count, ends, (zero, zero), unroll=32)
         first.append(c0)
         last.append(c1)
     values = [jnp.concatenate(last, axis=1), jnp.concatenate(first, axis=1)]
@@ -82,86 +92,122 @@
             hit, jnp.concatenate(parts, axis=0), (((1,), (1,)), ((), ())), preferred_element_type=F32
         )
     q_ref[...] = total
+    copy.wait()
+
+    def place(n, carry):
+        code = info_ref[0, n]
+        out_ref[pl.ds(STEP * (code >> 2) + 2 * (code & 3), 2)] = atm_ref[pl.ds(2 * n, 2)]
+        return carry
+
+    lax.fori_loop(0, HALF, place, 0, unroll=32)
     sub = subs((8, 128))
-
-    def head(t, carry):
-        near = (t & -16) + ((t + 15) & 15)
-        far = (t & -16) + ((t + 1) & 15)
-        own, west, east = [
-            jnp.broadcast_to(q_ref[pl.ds(i, 1), :], (8, 128)) for i in (t, near, far)
-        ]
-        out_ref[STEP * t + STEP - 1] = jnp.where(sub == 0, own, jnp.where(sub == 1, west, east)).astype(BF)
-        return carry
-
-    lax.fori_loop(0, DEV, head, 0, unroll=16)
+    for c in range(PIECES):
+        for t in range(c * DEV // PIECES, (c + 1) * DEV // PIECES):
+            near = (t & -16) + ((t + 15) & 15)
+            far = (t & -16) + ((t + 1) & 15)
+            own, west, east = [
+                jnp.broadcast_to(q_ref[i : i + 1, :], (8, 128)) for i in (t, near, far)
+            ]
+            head = jnp.where(sub == 0, own, jnp.where(sub == 1, west, east))
+            out_ref[STEP * t + STEP - 1] = head.astype(BF)
+        stores[c].start()
+    for store in stores:
+        store.wait()
 
 
 def pack(tile, row, live, atm):
+    vmem = pl.BlockSpec(memory_space=pltpu.VMEM)
+    hbm = pl.BlockSpec(memory_space=pl.ANY)
     return pl.pallas_call(
         pack_kernel,
         out_shape=jax.ShapeDtypeStruct((DEV * STEP, 8, 128), BF),
+        in_specs=[vmem, vmem, vmem, hbm],
+        out_specs=hbm,
         scratch_shapes=[
+            pltpu.VMEM((2 * HALF, 8, 128), BF),
+            pltpu.VMEM((DEV * STEP, 8, 128), BF),
             pltpu.VMEM((DEV, 128), F32),
             pltpu.VMEM((1, 256), I32),
             pltpu.SMEM((1, 256), I32),
             pltpu.SemaphoreType.DMA,
+            pltpu.SemaphoreType.DMA((PIECES,)),
+            pltpu.SemaphoreType.DMA((PIECES,)),
         ],
+        compiler_params=pltpu.CompilerParams(vmem_limit_bytes=56 << 20),
         name="pack",
     )(tile, row, live, atm)
 
 
 def coarse_kernel(
-    inc_ref, strip_ref, out_ref, cols_ref, west_ref, east_ref, low_ref, mid_ref, top_ref, tops_ref,
-    acc_ref, head_ref, idx_ref, where_ref, sem,
+    inc_hbm, strip_ref, out_ref, cols_ref, west_ref, east_ref, low_ref, mid_ref, top_ref, tops_ref,
+    inc_ref, raw_ref, acc_ref, head_ref, idx_ref, where_ref, sem, raw_sem, in_sem,
 ):
+    raw = pltpu.make_async_copy(inc_hbm.at[:, STEP - 1], raw_ref, raw_sem)
+    raw.start()
+    loads = []
+    for c in range(PIECES):
+        at = pl.ds(c * DEV // PIECES, DEV // PIECES)
+        loads.append(pltpu.make_async_copy(inc_hbm.at[at], inc_ref.at[at], in_sem.at[c]))
+        loads[c].start()
+    acc_ref[...] = jnp.zeros_like(acc_ref)
+    raw.wait()
     few = lanes((8, 128)) < CAP
     for g in range(4):
 
         def gather(s, total):
-            head = inc_ref[STEP * (32 * g + s) + STEP - 1].astype(F32)
+            head = raw_ref[32 * g + s].astype(F32)
             head_ref[32 * g + s] = head
             return total + pltpu.roll(jnp.where(few, head, 0.0), 4 * s, 1)
 
         idx_ref[g] = lax.fori_loop(0, 32, gather, jnp.zeros((8, 128), F32), unroll=32).astype(I32)
     copy = pltpu.make_async_copy(idx_ref, where_ref, sem)
     copy.start()
-    acc_ref[...] = jnp.zeros_like(acc_ref)
-    copy.wait()
-    for g in range(4):
-
-        def add(s, carry):
-            for k in range(CAP):
-                r = where_ref[g, 0, 4 * s + k]
-                block = inc_ref[pl.ds(STEP * (32 * g + s) + 2 * k, 2)]
-                acc_ref[k, r] = acc_ref[k, r] + block.astype(F32)
-            return carry
-
-        lax.fori_loop(0, 32, add, 0, unroll=8)
-    lane = lanes((FLD, 128))
-
-    def finish(r, carry):
-        total = acc_ref[0, r + 1] + acc_ref[1, r + 1] + acc_ref[2, r + 1]
-        out_ref[r] = total.reshape(FLD, 128).astype(BF)
-        return carry
-
-    lax.fori_loop(0, HALF, finish, 0, unroll=16)
-    target = (lanes((DEV, 256)) + 1).astype(F32)
+    target = (subs((256, DEV)) + 1).astype(F32)
     for j, wanted in (
         (0, ((4 * FLD, cols_ref.at[0]), (FLD, cols_ref.at[1]))),
         (1, ((FLD, west_ref),)),
         (2, ((4 * FLD, east_ref),)),
     ):
-        heads = head_ref[:, j, :]
-        turned = heads.T.astype(BF)
-        hits = [
-            (jnp.broadcast_to(heads[:, k : k + 1], (DEV, 256)) == target).astype(BF) for k in range(CAP)
-        ]
-        for first, ref in wanted:
-            total = jnp.zeros((FLD, 256), F32)
+        turned = head_ref[:, j, :].T
+        values = turned.astype(BF)
+        hits = jnp.concatenate(
+            [
+                (jnp.broadcast_to(turned[k : k + 1], (256, DEV)) == target).astype(BF)
+                for k in range(CAP)
+            ],
+            axis=1,
+        )
+        blocks = jnp.concatenate(
+            [
+                jnp.concatenate([values[at + FLD * k : at + FLD * k + FLD] for k in range(CAP)], axis=1)
+                for at, _ in wanted
+            ],
+            axis=0,
+        )
+        total = lax.dot_general(blocks, hits, (((1,), (1,)), ((), ())), preferred_element_type=F32)
+        for n, (_, ref) in enumerate(wanted):
+            ref[...] = total[n * FLD : n * FLD + FLD].astype(BF)
+    copy.wait()
+    for c in range(PIECES):
+        loads[c].wait()
+        count = DEV // PIECES
+
+        def add(i, carry):
             for k in range(CAP):
-                at = first + FLD * k
-                total = total + jnp.dot(turned[at : at + FLD], hits[k], preferred_element_type=F32)
-            ref[...] = total.astype(BF)
+                r = where_ref[c * count // 32, 0, 4 * (c * count % 32 + i) + k]
+                block = inc_ref[c * count + i, 2 * k : 2 * k + 2]
+                acc_ref[k, r] = acc_ref[k, r] + block.astype(F32)
+            return carry
+
+        lax.fori_loop(0, count, add, 0, unroll=16)
+    lane = lanes((FLD, 128))
+
+    def finish(r, carry):
+        total = acc_ref[0, r + 1] + acc_ref[1, r + 1] + acc_ref[2, r + 1]
+        out_ref[r] = total.reshape(FLD, 128).astype(BF)
+        return carry
+
+    lax.fori_loop(0, HALF, finish, 0, unroll=16)
     spread = (subs((256, PAD)) == lanes((256, PAD)) // 2).astype(BF)
     for k, r in enumerate((0, 1, HALF - 2, HALF - 1)):
         chunk, i = (r // 128) * 128, r % 128
@@ -200,14 +246,19 @@
             jax.ShapeDtypeStruct((2, 2 * FLD, PAD), BF),
             jax.ShapeDtypeStruct((16, 2, 2 * FLD, COLS), BF),
         ),
+        in_specs=[pl.BlockSpec(memory_space=pl.ANY), pl.BlockSpec(memory_space=pltpu.VMEM)],
         scratch_shapes=[
+            pltpu.VMEM((DEV, STEP, 8, 128), BF),
+            pltpu.VMEM((DEV, 8, 128), BF),
             pltpu.VMEM((CAP, HALF + 1, 2, 8, 128), F32),
             pltpu.VMEM((DEV, 8, 128), F32),
             pltpu.VMEM((4, 8, 128), I32),
             pltpu.SMEM((4, 8, 128), I32),
             pltpu.SemaphoreType.DMA,
+            pltpu.SemaphoreType.DMA,
+            pltpu.SemaphoreType.DMA((PIECES,)),
         ],
-        compiler_params=pltpu.CompilerParams(vmem_limit_bytes=12 << 20),
+        compiler_params=pltpu.CompilerParams(vmem_limit_bytes=20 << 20),
         name="coarse",
     )(incoming, strip)
 
@@ -382,7 +433,7 @@
 def main_kernel(
     part_ref, m3_ref, coarse_ref, first_ref, last_ref, west_ref, east_ref, cown_ref, cwest_ref, ceast_ref,
     w1_ref, b1_ref, w2_ref, b2_ref, out_ref,
-    cx_ref, fine_ref, p_ref, h_ref, add_ref, band1_ref, band2_ref, side1_ref, side2_ref, pair_ref, sem,
+    fine_ref, p_ref, h_ref, add_ref, band1_ref, band2_ref, side1_ref, side2_ref, pair_ref, sem,
 ):
     def fetch(block):
         at = pl.ds(block * 24, 24)
@@ -451,37 +502,31 @@
             add_ref[q, chunk] = jnp.where(phase == (q + 2) % 4, c254, z)
 
     lane = lanes((FLD, 128))
-    for chunk, count in ((0, 128), (128, 64)):
+    spread = (subs((128, COLS)) == lanes((128, COLS)) // 2).astype(BF)
+    fine_ref[0] = jnp.zeros((48, COLS), BF)
+    fine_ref[HALF + 1] = jnp.zeros((48, COLS), BF)
+    for chunk, count in ((0, 8), (128, 4)):
         west = cwest_ref[:, chunk : chunk + 128]
-        east = pltpu.roll(ceast_ref[:, chunk : chunk + 128], 1, 1)
+        east = pltpu.roll(ceast_ref[:, chunk : chunk + 128], 127, 1)
         for q in range(2):
             pair_ref[q] = jnp.where((lane & 1) == q, west, east)
 
-        def extend(i, carry):
-            r = chunk + i
-            cx_ref[r, :, 0:128] = coarse_ref[r]
-            cx_ref[r, :, 128:256] = pltpu.roll(pair_ref[i & 1], 128 - i, 1)
+        def widen(k, carry):
+            r0 = chunk + 16 * k
+            part = coarse_ref[pl.ds(r0, 16)].reshape(256, 128)
+            fine = jnp.dot(part, spread, preferred_element_type=F32).astype(BF).reshape(16, FLD, COLS)
+            for i in range(16):
+                x = fine[i]
+                beside = pltpu.roll(pair_ref[i & 1], 128 - (16 * k + i), 1)
+                up, down = pltpu.roll(x, 1, 1), pltpu.roll(x, COLS - 1, 1)
+                fine_ref[r0 + i + 1, 0:16, 0:128] = jnp.where(lane == 0, beside, up[:, :128])
+                fine_ref[r0 + i + 1, 0:16, 128:256] = up[:, 128:]
+                fine_ref[r0 + i + 1, 16:32, :] = x
+                fine_ref[r0 + i + 1, 32:48, 0:128] = down[:, :128]
+                fine_ref[r0 + i + 1, 32:48, 128:256] = jnp.where(lane == 127, beside, down[:, 128:])
             return carry
 
-        lax.fori_loop(0, count, extend, 0, unroll=16)
-
-    src, dst = subs((256, COLS)), lanes((256, COLS))
-    spread = [
-        (src == jnp.where(dst == 0, 128, (dst - 1) // 2)).astype(BF),
-        (src == dst // 2).astype(BF),
-        (src == jnp.where(dst == COLS - 1, 129, (dst + 1) // 2)).astype(BF),
-    ]
-    fine_ref[0] = jnp.zeros((48, COLS), BF)
-    fine_ref[HALF + 1] = jnp.zeros((48, COLS), BF)
-
-    def widen(k, carry):
-        part = cx_ref[pl.ds(k * 16, 16)].reshape(256, 256)
-        for v in range(3):
-            fine = jnp.dot(part, spread[v], preferred_element_type=F32).astype(BF)
-            fine_ref[pl.ds(k * 16 + 1, 16), 16 * v : 16 * v + 16, :] = fine.reshape(16, FLD, COLS)
-        return carry
-
-    lax.fori_loop(0, 12, widen, 0, unroll=2)
+        lax.fori_loop(0, count, widen, 0, unroll=2)
 
     hzero = jnp.zeros((HID, COLS), BF)
     h_ref[0] = hzero
@@ -541,7 +586,6 @@
         out_shape=jax.ShapeDtypeStruct((ROWS, OUT, COLS), BF),
         in_specs=[pl.BlockSpec(memory_space=pl.ANY)] + [vmem] * 13,
         scratch_shapes=[
-            pltpu.VMEM((HALF, FLD, COLS), BF),
             pltpu.VMEM((HALF + 2, 48, COLS), BF),
             pltpu.VMEM((ROWS, HID, COLS), BF),
             pltpu.VMEM((ROWS + 2, HID, COLS), BF),
@@ -627,16 +671,19 @@
         last = last + move(tops_ref[fold_ref[wrap(b + 1)], 1], put(COLS - 1, 272))
         in_ref[14] = last * signs
 
+    def shifted(x):
+        return [pltpu.roll(x, 1, 1).astype(BF), x.astype(BF), pltpu.roll(x, PAD - 1, 1).astype(BF)]
+
+    inputs = [shifted(in_ref[k]) for k in range(15)]
+    weights = [
+        jnp.concatenate([w1_ref[u, 2 - v if flip else v] for u in range(3) for v in range(3)], axis=1)
+        for flip in (False, True)
+    ]
+
     def hidden(rows, flip):
-        total = jnp.broadcast_to(b1_ref[:, 0:1], (HID, PAD))
-        for u in range(3):
-            x = in_ref[rows + u]
-            for v in range(3):
-                shifted = pltpu.roll(x, (1 - v) % PAD, 1) if v != 1 else x
-                total = total + jnp.dot(
-                    w1_ref[u, 2 - v if flip else v], shifted.astype(BF), preferred_element_type=F32
-                )
-        return jnp.maximum(total, 0.0).astype(BF)
+        x = jnp.concatenate(inputs[rows] + inputs[rows + 1] + inputs[rows + 2], axis=0)
+        total = jnp.dot(weights[flip], x, preferred_element_type=F32)
+        return jnp.maximum(total + b1_ref[:, 0:1], 0.0).astype(BF)
 
     virtual = hidden(12, True).astype(F32)
     lane = lanes((HID, PAD))
@@ -645,19 +692,17 @@
         pltpu.roll(virtual, (SHIFT - 1 - 265) % PAD, 1),
         jnp.where(lane == SHIFT + 256, pltpu.roll(virtual, (SHIFT + 256 - 273) % PAD, 1), virtual),
     )
+    second = jnp.concatenate([w2_ref[u, v] for u in range(3) for v in range(3)], axis=1)
     for half in range(2):
         hid = [hidden(6 * half + k, False).astype(F32) for k in range(4)]
         if half == 0:
             hid[0] = jnp.where(gy == 0, jnp.zeros_like(hid[0]), hid[0])
         else:
             hid[3] = jnp.where(gy == 7, virtual, hid[3])
+        around = [shifted(x) for x in hid]
         for r in range(2):
-            total = jnp.broadcast_to(b2_ref[:, 0:1], (OUT, PAD))
-            for u in range(3):
-                x = hid[r + u]
-                for v in range(3):
-                    shifted = pltpu.roll(x, (1 - v) % PAD, 1) if v != 1 else x
-                    total = total + jnp.dot(w2_ref[u, v], shifted.astype(BF), preferred_element_type=F32)
+            x = jnp.concatenate(around[r] + around[r + 1] + around[r + 2], axis=0)
+            total = jnp.dot(second, x, preferred_element_type=F32) + b2_ref[:, 0:1]
             m = strip_ref[6 * half + r, FLD : 2 * FLD, :].astype(F32)[:OUT]
             total = pltpu.roll(total * m, PAD - SHIFT, 1)
             res_ref[2 * half + r] = total[:, :COLS].astype(BF)
@@ -720,7 +765,7 @@
     m3, strip = margins(land_mask, west, east, rows)
 
     coarse, ccols, cwest, ceast, low, mid, top, tops = coarse_sums(
-        incoming.reshape(DEV * STEP, 8, 128), strip
+        incoming, strip
     )
     south = shift_gy(top, 1)
     north = shift_gy(low, -1)

time: 82.3 us -> 78.2 us (0.950)
  Pallas kernels: 46.4 us -> 42.3 us
    pallas_call x1, Pallas kernels: 7.28 us -> 5.38 us  [coarse_sums(): pl.pallas_call(coarse_kernel, out_shape=(jax.ShapeDtypeStruct((HALF, FLD,...]
    pallas_call x1, Pallas kernels: 16.8 us -> 15.4 us  [main_conv(): pl.pallas_call(main_kernel, out_shape=jax.ShapeDtypeStruct((ROWS, OUT, CO...]
where the time goes in v4:
time: 78.2 us; the launch traced here: 77.8 us
  Pallas kernels  42.3 us (54%)
  starting transfers between devices  28 us (36%)
  waiting for transfers between devices  4.65 us (6%)
  local copies, waits for them, and re-layouts  2.57 us (3%)
    pallas_call x1, Pallas kernels, main_conv(): pl.pallas_call(main_kernel, out_shape=jax.ShapeDtypeStruct((ROWS, OUT, CO...  15.4 us
    all_to_all x1, starting transfers between devices, per_device(): lax.all_to_all(outgoing.reshape(DEV, STEP, 8, 128), ('gy', 'gx'), split_a...  10.4 us
    pallas_call x1, Pallas kernels, ocean_part(): pl.pallas_call(ocean_kernel, out_shape=(jax.ShapeDtypeStruct((ROWS, HID,...  10.1 us
    ppermute x2, starting transfers between devices, shift_gy(): lax.ppermute(x, 'gy', [(i, i + step) for i in range(n) if 0 <= i + step <...  9.44 us
    all_to_all x1, starting transfers between devices, per_device(): tops = lax.all_to_all(tops, 'gx', split_axis=0, concat_axis=0, tiled=True)  5.44 us
    pallas_call x1, Pallas kernels, coarse_sums(): pl.pallas_call(coarse_kernel, out_shape=(jax.ShapeDtypeStruct((HALF, FLD,...  5.38 us
    pallas_call x1, Pallas kernels, pack(): pl.pallas_call(pack_kernel, out_shape=jax.ShapeDtypeStruct((DEV * STEP, 8...  4.85 us
    ppermute x2, waiting for transfers between devices, shift_gx(): return lax.ppermute(x, 'gx', [(i, (i + step) % n) for i in range(n)])  4.64 us
  transfers between devices with their start and end apart: 6, of which 1 were waited for; matrix products, arithmetic and copies ran while one was open for 0% of the time, Pallas kernels for 38%

profile of v4, /device:TPU:66, one launch (start us, length us, event | category | flops | bytes accessed | tf_op | source)
XLA Modules:
  0.0 77.8 jit_solution(16195118804475188238)
XLA Ops:
  0.0 4.9 %pack.1 = bf16[896,8,128]{2,1,0:T(8,128)(2,1)} custom-call(s32[1,192]{1,0:T(1,128)} %bitcast.13, s32[1,192]{1,0:T(1,128)} %bitcast.14, s32[1,192]{1,0:T(1,128)} %bitcast.15, bf16[384,8,128]{2,1,0:T(8,128)(2,1)} %bitcast.12), custom_call_target="tpu_custom_call" | custom-call | tf_op jit(solution)/shard_map/pack/pallas_call | solution.py:121
  4.9 0.0 copy-start
  4.9 0.0 copy-start.1
  4.9 10.4 %all-to-all-start = ((bf16[128,7,8,128]{3,2,1,0:T(8,128)(2,1)}), bf16[128,7,8,128]{3,2,1,0:T(8,128)(2,1)}, u32[]{:S(2)}, u32[]{:S(2)}) async-start(bf16[128,7,8,128]{3,2,1,0:T(8,128)(2,1)} %bitcast.11), calls=%async_computation | async-start | bytes 3670016 | tf_op jit(solution)/shard_map/all_to_all | solution.py:755
  15.3 0.0 copy-start.11
  15.4 0.0 copy-start.16
  15.4 0.0 copy-start.17
  15.4 3.6 %edges.1 = (bf16[2,32,384]{2,1,0:T(8,128)(2,1)S(1)}, bf16[2,32,384]{2,1,0:T(8,128)(2,1)S(1)}) custom-call(bf16[384,16,256]{2,1,0:T(8,128)(2,1)S(1)} %copy-done, s32[384,256]{1,0:T(8,128)S(1)} %copy-done.1), custom_call_target="tpu_custom_call" | custom-call | tf_op jit(solution)/shard_map/edges/pallas_call | solution.py:294
  19.0 0.2 collective-permute-start
  19.2 2.5 %collective-permute-start.1 = (bf16[2,32,384]{2,1,0:T(8,128)(2,1)S(1)}, bf16[2,32,384]{2,1,0:T(8,128)(2,1)S(1)}, u32[]{:S(2)}, u32[]{:S(2)}) collective-permute-start(bf16[2,32,384]{2,1,0:T(8,128)(2,1)S(1)} %get-tuple-element.27.first_ref), channel_id=1, source_target_pairs={{0,15},{1,0},{2,1},{3,2},{4,3},{5,4},{6,5},{7,6},{8,7},{9,8},{10,9... | collective-permute-start | bytes 147464 | tf_op jit(solution)/shard_map/ppermute | solution.py:741
  21.7 0.0 copy-done.11
  21.7 10.1 %ocean.1 = (bf16[384,64,256]{2,1,0:T(8,128)(2,1)}, bf16[8,32,384]{2,1,0:T(8,128)(2,1)S(1)}, bf16[3,3,64,32]{3,2,1,0:T(8,128)(2,1)S(1)}, f32[64,128]{1,0:T(8,128)S(1)}, f32[8,128]{1,0:T(8,128)S(1)}) custom-call(bf16[384,16,256]{2,1,0:T(8,128)(2,1)S(1)} %copy-done, s32[384,256]{1,0:T(8,128)S(1)} %copy-done.1, bf16[3,3,32,64]{3,2,1,0:T(8,128)(2,1)S(1)} %bitcast.8, ...), custom_call_target="tpu_custom_call" | custom-call | tf_op jit(solution)/shard_map/ocean/pallas_call | solution.py:371
  31.8 0.0 copy-start.2
  31.8 0.7 copy-done.2
  32.5 0.6 copy-done.8
  33.1 4.6 %collective-permute-done.west_ref = bf16[2,32,384]{2,1,0:T(8,128)(2,1)S(1)} collective-permute-done((bf16[2,32,384]{2,1,0:T(8,128)(2,1)S(1)}, bf16[2,32,384]{2,1,0:T(8,128)(2,1)S(1)}, u32[]{:S(2)}, u32[]{:S(2)}) %collective-permute-start) | collective-permute-done | bytes 49184 | tf_op jit(solution)/shard_map/ppermute | solution.py:741
  37.7 0.0 collective-permute-done.1.east_ref
  37.8 0.0 copy-start.10
  37.8 0.5 margins.1
  38.3 0.6 copy-done.4
  38.9 0.6 copy-done.6
  39.5 0.0 all-to-all-done.inc_hbm
  39.5 5.4 %coarse.1 = (bf16[192,16,128]{2,1,0:T(8,128)(2,1)S(1)}, bf16[2,16,256]{2,1,0:T(8,128)(2,1)S(1)}, bf16[16,256]{1,0:T(8,128)(2,1)S(1)}, bf16[16,256]{1,0:T(8,128)(...) custom-call(bf16[128,7,8,128]{3,2,1,0:T(8,128)(2,1)} %all-to-all-don, ...), custom_call_target="tpu_custom_call" | custom-call | tf_op jit(solution)/shard_map/coarse/pallas_call | solution.py:237
  44.9 5.4 %all-to-all-start.1 = ((bf16[16,2,32,256]{3,2,1,0:T(8,128)(2,1)}), bf16[16,2,32,256]{3,2,1,0:T(8,128)(2,1)S(1)}, u32[]{:S(2)}, u32[]{:S(2)}) async-start(bf16[16,2,32,256]{3,2,1,0:T(8,128)(2,1)} %get-tuple-element.33), calls=%async_computation.1 | async-start | bytes 1048576 | tf_op jit(solution)/shard_map/all_to_all | solution.py:772
  50.3 3.3 %collective-permute-start.2 = (bf16[2,32,384]{2,1,0:T(8,128)(2,1)S(1)}, bf16[2,32,384]{2,1,0:T(8,128)(2,1)S(1)}, u32[]{:S(2)}, u32[]{:S(2)}) collective-permute-start(bf16[2,32,384]{2,1,0:T(8,128)(2,1)S(1)} %get-tuple-element.30.top_ref), channel_id=1, source_target_pairs={{0,16},{16,32},{32,48},{48,64},{64,80},{80,96},{96,112},{1,17},{17... | collective-permute-start | bytes 147464 | tf_op jit(solution)/shard_map/ppermute | solution.py:746
  53.6 6.2 %collective-permute-start.3 = (bf16[2,32,384]{2,1,0:T(8,128)(2,1)S(1)}, bf16[2,32,384]{2,1,0:T(8,128)(2,1)S(1)}, u32[]{:S(2)}, u32[]{:S(2)}) collective-permute-start(bf16[2,32,384]{2,1,0:T(8,128)(2,1)S(1)} %get-tuple-element.31.low_ref), channel_id=1, source_target_pairs={{16,0},{32,16},{48,32},{64,48},{80,64},{96,80},{112,96},{17,1},{33... | collective-permute-start | bytes 147464 | tf_op jit(solution)/shard_map/ppermute | solution.py:746
  59.9 0.0 copy-start.18
  59.9 15.4 %convs.1.main_ref = bf16[384,8,256]{2,1,0:T(8,128)(2,1)} custom-call(bf16[384,64,256]{2,1,0:T(8,128)(2,1)} %get-tuple-element.37.part_ref, f32[3,384,256]{2,1,0:T(8,128)S(1)} %get-tuple-element.38.m3_ref, bf16[192,16,128]{2,1,0:T(8,128)(2,1)S(1)} %get-tuple-element.39.coarse_ref, bf16[2,32,384]{2,1,0:T(8,128)(2,1)S(1)} %copy-done.13, ...), custom_call_target="tpu_custom_call" | custom-call | tf_op jit(solution)/shard_map/convs/pallas_call | solution.py:584
  75.3 0.0 collective-permute-done.2.south_ref
  75.3 0.0 collective-permute-done.3.north_ref
  75.3 0.0 all-to-all-done.1.tops_ref
  75.4 2.5 %patch.1 = bf16[384,8,256]{2,1,0:T(8,128)(2,1)} custom-call(s32[16]{0:T(128)S(1)} %copy-done.18, bf16[2,32,384]{2,1,0:T(8,128)(2,1)S(1)} %collective-permute-done.2.south_ref, bf16[2,32,384]{2,1,0:T(8,128)(2,1)S(1)} %get-tuple-element.31.low_ref, bf16[4,32,384]{2,1,0:T(8,128)(2,1)S(1)} %get-tuple-element.32.mid_ref, ...), custom_call_target="tpu_custom_call", output_to_operand_aliasing={{}: (12, {})} | custom-call | tf_op jit(solution)/shard_map/patch/pallas_call | solution.py:723
  (25 shorter events, 0.0 us)
Async XLA Ops:
  4.9 10.5 %copy-start = (bf16[384,16,256]{2,1,0:T(8,128)(2,1)S(1)}, bf16[384,16,256]{2,1,0:T(8,128)(2,1)}, u32[]{:S(2)}) copy-start(bf16[384,16,256]{2,1,0:T(8,128)(2,1)} %ocean_ref.1) | copy-start | bytes 9437188
  4.9 10.5 %copy-start.1 = (s32[384,256]{1,0:T(8,128)S(1)}, s32[384,256]{1,0:T(8,128)}, u32[]{:S(2)}) copy-start(s32[384,256]{1,0:T(8,128)} %mask_ref.2) | copy-start | bytes 1179652
  4.9 34.6 %all-to-all-start = ((bf16[128,7,8,128]{3,2,1,0:T(8,128)(2,1)}), bf16[128,7,8,128]{3,2,1,0:T(8,128)(2,1)}, u32[]{:S(2)}, u32[]{:S(2)}) async-start(bf16[128,7,8,128]{3,2,1,0:T(8,128)(2,1)} %bitcast.11), calls=%async_computation | async-start | bytes 3670016 | tf_op jit(solution)/shard_map/all_to_all | solution.py:755
  15.3 6.4 %copy-start.11 = (bf16[3,3,64,32]{2,3,1,0:T(8,128)(2,1)S(1)}, bf16[3,3,64,32]{2,3,1,0:T(8,128)(2,1)}, u32[]{:S(2)}) copy-start(bf16[3,3,64,32]{2,3,1,0:T(8,128)(2,1)} %param.18) | copy-start | bytes 110596
  15.4 6.4 %copy-start.16 = (f32[64]{0:T(128)S(1)}, f32[64]{0:T(128)}, u32[]{:S(2)}) copy-start(f32[64]{0:T(128)} %param.19) | copy-start | bytes 772
  15.4 6.4 %copy-start.17 = (f32[8]{0:T(128)S(1)}, f32[8]{0:T(128)}, u32[]{:S(2)}) copy-start(f32[8]{0:T(128)} %param.21) | copy-start | bytes 100
  19.0 18.8 %copy-start.12 = (bf16[2,32,384]{2,1,0:T(8,128)(2,1)}, bf16[2,32,384]{2,1,0:T(8,128)(2,1)S(1)}, u32[]{:S(2)}) copy-start(bf16[2,32,384]{2,1,0:T(8,128)(2,1)S(1)} %get-tuple-element.27.first_ref) | copy-start | bytes 147460
  19.0 18.8 %copy-start.14 = (bf16[2,32,384]{2,1,0:T(8,128)(2,1)}, bf16[2,32,384]{2,1,0:T(8,128)(2,1)S(1)}, u32[]{:S(2)}) copy-start(bf16[2,32,384]{2,1,0:T(8,128)(2,1)S(1)} %get-tuple-element.26.last_ref) | copy-start | bytes 147460
  19.0 18.7 %collective-permute-start = (bf16[2,32,384]{2,1,0:T(8,128)(2,1)S(1)}, bf16[2,32,384]{2,1,0:T(8,128)(2,1)S(1)}, u32[]{:S(2)}, u32[]{:S(2)}) collective-permute-start(bf16[2,32,384]{2,1,0:T(8,128)(2,1)S(1)} %get-tuple-element.26.last_ref), channel_id=1, source_target_pairs={{0,1},{1,2},{2,3},{3,4},{4,5},{5,6},{6,7},{7,8},{8,9},{9,10},{10,1... | collective-permute-start | bytes 147464 | tf_op jit(solution)/shard_map/ppermute | solution.py:741
  19.2 18.5 %collective-permute-start.1 = (bf16[2,32,384]{2,1,0:T(8,128)(2,1)S(1)}, bf16[2,32,384]{2,1,0:T(8,128)(2,1)S(1)}, u32[]{:S(2)}, u32[]{:S(2)}) collective-permute-start(bf16[2,32,384]{2,1,0:T(8,128)(2,1)S(1)} %get-tuple-element.27.first_ref), channel_id=1, source_target_pairs={{0,15},{1,0},{2,1},{3,2},{4,3},{5,4},{6,5},{7,6},{8,7},{9,8},{10,9... | collective-permute-start | bytes 147464 | tf_op jit(solution)/shard_map/ppermute | solution.py:741
  31.8 0.7 copy-start.2
  32.5 0.6 copy-start.8
  37.8 22.0 %copy-start.3 = (bf16[3,3,64,32]{3,2,1,0:T(8,128)(2,1)S(1)}, bf16[3,3,64,32]{3,2,1,0:T(8,128)(2,1)}, u32[]{:S(2)}) copy-start(bf16[3,3,64,32]{3,2,1,0:T(8,128)(2,1)} %copy-done.2) | copy-start | bytes 110596
  37.8 22.0 %copy-start.9 = (f32[64,128]{1,0:T(8,128)S(1)}, f32[64,128]{1,0:T(8,128)}, u32[]{:S(2)}) copy-start(f32[64,128]{1,0:T(8,128)} %copy-done.8) | copy-start | bytes 98308
  37.8 22.0 %copy-start.10 = (bf16[3,3,8,64]{3,2,1,0:T(8,128)(2,1)S(1)}, bf16[3,3,8,64]{3,2,1,0:T(8,128)(2,1)}, u32[]{:S(2)}) copy-start(bf16[3,3,8,64]{3,2,1,0:T(8,128)(2,1)} %w2_ref.3) | copy-start | bytes 27652
  37.8 22.0 %copy-start.13 = (bf16[2,32,384]{2,1,0:T(8,128)(2,1)S(1)}, bf16[2,32,384]{2,1,0:T(8,128)(2,1)}, u32[]{:S(2)}) copy-start(bf16[2,32,384]{2,1,0:T(8,128)(2,1)} %copy-done.12) | copy-start | bytes 147460
  38.3 0.6 copy-start.4
  38.9 0.6 copy-start.6
  39.5 20.3 %copy-start.15 = (bf16[2,32,384]{2,1,0:T(8,128)(2,1)S(1)}, bf16[2,32,384]{2,1,0:T(8,128)(2,1)}, u32[]{:S(2)}) copy-start(bf16[2,32,384]{2,1,0:T(8,128)(2,1)} %copy-done.14) | copy-start | bytes 147460
  39.5 20.3 %copy-start.5 = (bf16[2,32,384]{2,1,0:T(8,128)(2,1)S(1)}, bf16[2,32,384]{2,1,0:T(8,128)(2,1)}, u32[]{:S(2)}) copy-start(bf16[2,32,384]{2,1,0:T(8,128)(2,1)} %copy-done.4) | copy-start | bytes 147460
  39.5 20.3 %copy-start.7 = (bf16[2,32,384]{2,1,0:T(8,128)(2,1)S(1)}, bf16[2,32,384]{2,1,0:T(8,128)(2,1)}, u32[]{:S(2)}) copy-start(bf16[2,32,384]{2,1,0:T(8,128)(2,1)} %copy-done.6) | copy-start | bytes 147460
  44.9 30.5 %all-to-all-start.1 = ((bf16[16,2,32,256]{3,2,1,0:T(8,128)(2,1)}), bf16[16,2,32,256]{3,2,1,0:T(8,128)(2,1)S(1)}, u32[]{:S(2)}, u32[]{:S(2)}) async-start(bf16[16,2,32,256]{3,2,1,0:T(8,128)(2,1)} %get-tuple-element.33), calls=%async_computation.1 | async-start | bytes 1048576 | tf_op jit(solution)/shard_map/all_to_all | solution.py:772
  50.3 25.0 %collective-permute-start.2 = (bf16[2,32,384]{2,1,0:T(8,128)(2,1)S(1)}, bf16[2,32,384]{2,1,0:T(8,128)(2,1)S(1)}, u32[]{:S(2)}, u32[]{:S(2)}) collective-permute-start(bf16[2,32,384]{2,1,0:T(8,128)(2,1)S(1)} %get-tuple-element.30.top_ref), channel_id=1, source_target_pairs={{0,16},{16,32},{32,48},{48,64},{64,80},{80,96},{96,112},{1,17},{17... | collective-permute-start | bytes 147464 | tf_op jit(solution)/shard_map/ppermute | solution.py:746
  53.6 21.7 %collective-permute-start.3 = (bf16[2,32,384]{2,1,0:T(8,128)(2,1)S(1)}, bf16[2,32,384]{2,1,0:T(8,128)(2,1)S(1)}, u32[]{:S(2)}, u32[]{:S(2)}) collective-permute-start(bf16[2,32,384]{2,1,0:T(8,128)(2,1)S(1)} %get-tuple-element.31.low_ref), channel_id=1, source_target_pairs={{16,0},{32,16},{48,32},{64,48},{80,64},{96,80},{112,96},{17,1},{33... | collective-permute-start | bytes 147464 | tf_op jit(solution)/shard_map/ppermute | solution.py:746
  59.9 15.5 %copy-start.18 = (s32[16]{0:T(128)S(1)}, s32[16]{0:T(128)}, u32[]{:S(2)}) copy-start(s32[16]{0:T(128)} %fold_ref.1) | copy-start | bytes 196

commit v5 on v4

--- a/solution.py
+++ b/solution.py
@@ -58,11 +58,11 @@
     code_ref[...] = code.astype(I32)
     copy = pltpu.make_async_copy(code_ref, info_ref, sem)
     copy.start()
-    for load in loads:
-        load.wait()
     lane = lanes((FLD, 128))
     first, last = [], []
-    for chunk, count in ((0, 128), (128, 64)):
+    for chunk, count, need in ((0, 128, loads[:6]), (128, 64, loads[6:])):
+        for load in need:
+            load.wait()
 
         def ends(i, carry):
             c0, c1 = carry
@@ -80,17 +80,21 @@
     code = jnp.broadcast_to(code_ref[...], (DEV, 256))
     row = jnp.where(live_ref[...] == 1, row_ref[...] + 1, 0).astype(F32)
     row = jnp.concatenate([row, jnp.zeros((1, 64), F32)], axis=1).astype(BF)
-    total = jnp.zeros((DEV, 128), F32)
+    hits, columns = [], []
     tile = subs((DEV, 256))
     none = jnp.zeros((FLD, 256), BF)
     for k in range(CAP):
-        hit = (code == 4 * tile + k).astype(BF)
+        hits.append((code == 4 * tile + k).astype(BF))
         rows = jnp.where(subs((FLD, 256)) == k, jnp.broadcast_to(row, (FLD, 256)), none)
         parts = [rows] + [values[0] if i == k else none for i in range(3)]
         parts = parts + [values[1] if i == k else none for i in range(3)] + [none]
-        total = total + lax.dot_general(
-            hit, jnp.concatenate(parts, axis=0), (((1,), (1,)), ((), ())), preferred_element_type=F32
-        )
+        columns.append(jnp.concatenate(parts, axis=0))
+    total = lax.dot_general(
+        jnp.concatenate(hits, axis=1),
+        jnp.concatenate(columns, axis=1),
+        (((1,), (1,)), ((), ())),
+        preferred_element_type=F32,
+    )
     q_ref[...] = total
     copy.wait()
 
@@ -202,26 +206,31 @@
         lax.fori_loop(0, count, add, 0, unroll=16)
     lane = lanes((FLD, 128))
 
+    def summed(r):
+        total = acc_ref[0, r + 1] + acc_ref[1, r + 1] + acc_ref[2, r + 1]
+        return total.reshape(FLD, 128).astype(BF)
+
     def finish(r, carry):
-        total = acc_ref[0, r + 1] + acc_ref[1, r + 1] + acc_ref[2, r + 1]
-        out_ref[r] = total.reshape(FLD, 128).astype(BF)
+        out_ref[r] = summed(r)
         return carry
 
-    lax.fori_loop(0, HALF, finish, 0, unroll=16)
     spread = (subs((256, PAD)) == lanes((256, PAD)) // 2).astype(BF)
-    for k, r in enumerate((0, 1, HALF - 2, HALF - 1)):
+    wides = []
+    for r in (0, 1, HALF - 2, HALF - 1):
         chunk, i = (r // 128) * 128, r % 128
         west = pltpu.roll(west_ref[:, chunk : chunk + 128].astype(F32), (128 - i) % 128, 1)
         east = pltpu.roll(east_ref[:, chunk : chunk + 128].astype(F32), (129 - i) % 128, 1)
-        row = pltpu.roll(out_ref[r].astype(F32), 1, 1)
-        wide = jnp.concatenate(
+        row = pltpu.roll(summed(r).astype(F32), 1, 1)
+        wides.append(jnp.concatenate(
             [
                 jnp.where(lane == 0, west, row),
                 jnp.where(lane == 0, row, jnp.where(lane == 1, east, 0.0)),
             ],
             axis=1,
-        ).astype(BF)
-        fine = jnp.dot(wide, spread, preferred_element_type=F32).astype(BF)
+        ).astype(BF))
+    fines = jnp.dot(jnp.concatenate(wides, axis=0), spread, preferred_element_type=F32).astype(BF)
+    for k in range(4):
+        fine = fines[k * FLD : k * FLD + FLD]
         for h in range(2):
             n = 2 * k + h
             ref, at = ((low_ref, n), (mid_ref, n - 2), (mid_ref, n - 2), (top_ref, n - 6))[k]
@@ -231,6 +240,7 @@
         row = pltpu.roll(top_ref[h].astype(F32), PAD - SHIFT, 1)[:, :COLS].astype(BF)
         for t in range(16):
             tops_ref[t, h] = row
+    lax.fori_loop(0, HALF, finish, 0, unroll=16)
 
 
 def coarse_sums(incoming, strip):
@@ -433,7 +443,7 @@
 def main_kernel(
     part_ref, m3_ref, coarse_ref, first_ref, last_ref, west_ref, east_ref, cown_ref, cwest_ref, ceast_ref,
     w1_ref, b1_ref, w2_ref, b2_ref, out_ref,
-    fine_ref, p_ref, h_ref, add_ref, band1_ref, band2_ref, side1_ref, side2_ref, pair_ref, sem,
+    fine_ref, p_ref, h_ref, add_ref, band1_ref, band2_ref, side1_ref, side2_ref, pair_ref, res_ref, sem, out_sem,
 ):
     def fetch(block):
         at = pl.ds(block * 24, 24)
@@ -447,9 +457,9 @@
     for u in range(3):
         for v in range(3):
             w = w2_ref[u, v]
-            for r in range(6):
-                at = (r * 3 + v) * OUT
-                band2_ref[at : at + OUT, (r + u) * HID : (r + u) * HID + HID] = w
+            for i in range(4):
+                at = ((i + 2 - u) * 3 + v) * OUT
+                band2_ref[at : at + OUT, i * HID : i * HID + HID] = w
             w1 = w1_ref[u, v]
             at = (u * 3 + v) * 2 * FLD
             side1_ref[:, at : at + 2 * FLD] = w1
@@ -479,17 +489,19 @@
     def around(x):
         return jnp.concatenate([pltpu.roll(x, 1, 1), x, pltpu.roll(x, ROWS - 1, 1)], axis=0)
 
-    ends = []
-    for side, outer, inner in (
-        (0, (w2c, w1c, o0c), (w1c, o0c, o1c)),
-        (1, (o255c, e1c, e2c), (o254c, o255c, e1c)),
-    ):
-        hidden = []
-        for cols in (outer, inner):
-            xt = around(jnp.concatenate(cols, axis=0))
-            hid = jnp.dot(side1_ref[...], xt, preferred_element_type=F32)
-            hidden.append(around(jnp.maximum(hid + b1_ref[:, 0:1], 0.0).astype(BF)))
-        ends.append(jnp.dot(side2_ref[side], jnp.concatenate(hidden, axis=0), preferred_element_type=F32))
+    groups = ((w2c, w1c, o0c), (w1c, o0c, o1c), (o255c, e1c, e2c), (o254c, o255c, e1c))
+    xt = jnp.concatenate([around(jnp.concatenate(cols, axis=0)) for cols in groups], axis=1)
+    hid = jnp.dot(side1_ref[...], xt, preferred_element_type=F32)
+    hid = jnp.maximum(hid + b1_ref[:, 0:1], 0.0).astype(BF)
+    hid = [around(hid[:, k * ROWS : k * ROWS + ROWS]) for k in range(4)]
+    ends = [
+        jnp.dot(
+            side2_ref[side],
+            jnp.concatenate(hid[2 * side : 2 * side + 2], axis=0),
+            preferred_element_type=F32,
+        )
+        for side in range(2)
+    ]
     phase = lanes((OUT, 128)) & 3
     for chunk in range(3):
         at = slice(chunk * 128, chunk * 128 + 128)
@@ -556,27 +568,44 @@
     b2 = b2_ref[:, 0:1]
     lane8 = lanes((OUT, 128))
 
+    def emit(y, t):
+        ends = pltpu.roll(add_ref[y & 3, y >> 7], 128 - (y & 127), 1)
+        up = pltpu.roll(t[0], 1, 1)
+        down = pltpu.roll(t[2], COLS - 1, 1)
+        m = m3_ref[1, pl.ds(y, 1), :]
+        lo = jnp.where(lane8 == 0, 0.0, t[1, :, :128]) + b2
+        lo = lo + jnp.where(lane8 < 2, ends, up[:, :128]) + down[:, :128]
+        hi = jnp.where(lane8 == 127, 0.0, t[1, :, 128:]) + b2
+        hi = hi + up[:, 128:] + jnp.where(lane8 > 125, ends, down[:, 128:])
+        res_ref[y, :, 0:128] = (lo * m[:, :128]).astype(BF)
+        res_ref[y, :, 128:256] = (hi * m[:, 128:]).astype(BF)
+
+    def store(block):
+        at = pl.ds(block * 48, 48)
+        return pltpu.make_async_copy(res_ref.at[at], out_ref.at[at], out_sem.at[block])
+
     def conv2(block, carry):
-        for k in range(8):
-            j = block * 8 + k
-            x = h_ref[pl.ds(6 * j, 8)].reshape(512, COLS)
+        for k in range(12):
+            g = block * 12 + k
+            x = h_ref[pl.ds(4 * g + 1, 4)].reshape(256, COLS)
             t = jnp.dot(band2_ref[...], x, preferred_element_type=F32).reshape(6, 3, OUT, COLS)
-            for r in range(6):
-                y = 6 * j + r
-                ends = pltpu.roll(add_ref[y & 3, y >> 7], 128 - (y & 127), 1)
-                up = pltpu.roll(t[r, 0], 1, 1)
-                down = pltpu.roll(t[r, 2], COLS - 1, 1)
-                m = m3_ref[1, pl.ds(y, 1), :]
-                lo = jnp.where(lane8 == 0, 0.0, t[r, 1, :, :128]) + b2
-                lo = lo + jnp.where(lane8 < 2, ends, up[:, :128]) + down[:, :128]
-                hi = jnp.where(lane8 == 127, 0.0, t[r, 1, :, 128:]) + b2
-                hi = hi + up[:, 128:] + jnp.where(lane8 > 125, ends, down[:, 128:])
-                out_ref[y, :, 0:128] = (lo * m[:, :128]).astype(BF)
-                out_ref[y, :, 128:256] = (hi * m[:, 128:]).astype(BF)
+            emit(jnp.maximum(4 * g - 1, 0), t[0] + carry[0])
+            emit(4 * g, t[1] + carry[1])
+            emit(4 * g + 1, t[2])
+            emit(4 * g + 2, t[3])
+            carry = (t[4], t[5])
+
+        @pl.when(block > 0)
+        def _():
+            store(block - 1).start()
 
         return carry
 
-    lax.fori_loop(0, 8, conv2, 0)
+    none = jnp.zeros((3, OUT, COLS), F32)
+    lax.fori_loop(0, 8, conv2, (none, none))
+    store(7).start()
+    for block in range(8):
+        store(block).wait()
 
 
 def main_conv(*args):
@@ -585,17 +614,20 @@
         main_kernel,
         out_shape=jax.ShapeDtypeStruct((ROWS, OUT, COLS), BF),
         in_specs=[pl.BlockSpec(memory_space=pl.ANY)] + [vmem] * 13,
+        out_specs=pl.BlockSpec(memory_space=pl.ANY),
         scratch_shapes=[
             pltpu.VMEM((HALF + 2, 48, COLS), BF),
             pltpu.VMEM((ROWS, HID, COLS), BF),
             pltpu.VMEM((ROWS + 2, HID, COLS), BF),
             pltpu.VMEM((4, 3, OUT, 128), F32),
             pltpu.VMEM((192, 240), BF),
-            pltpu.VMEM((144, 512), BF),
+            pltpu.VMEM((144, 256), BF),
             pltpu.VMEM((HID, 288), BF),
             pltpu.VMEM((2, 2 * OUT, 384), BF),
             pltpu.VMEM((2, FLD, 128), BF),
+            pltpu.VMEM((ROWS, OUT, COLS), BF),
             pltpu.SemaphoreType.DMA((BLOCKS,)),
+            pltpu.SemaphoreType.DMA((8,)),
         ],
         compiler_params=pltpu.CompilerParams(vmem_limit_bytes=44 << 20),
         name="convs",

time: 78.2 us -> 76.8 us (0.982)
  Pallas kernels: 42.3 us -> 40.9 us
    pallas_call x1, Pallas kernels: 15.4 us -> 14.2 us  [main_conv(): pl.pallas_call(main_kernel, out_shape=jax.ShapeDtypeStruct((ROWS, OUT, CO...]
  transfers between devices with their start and end apart: 6 -> 6, of which waited for: 1 -> 1; matrix products, arithmetic and copies ran while one was open for 0% -> 0% of each run, Pallas kernels for 38% -> 37%
where the time goes in v5:
time: 76.8 us; the launch traced here: 76.5 us
  Pallas kernels  40.9 us (53%)
  starting transfers between devices  28 us (36%)
  waiting for transfers between devices  4.65 us (6%)
  local copies, waits for them, and re-layouts  2.57 us (3%)
    pallas_call x1, Pallas kernels, main_conv(): pl.pallas_call(main_kernel, out_shape=jax.ShapeDtypeStruct((ROWS, OUT, CO...  14.2 us
    all_to_all x1, starting transfers between devices, per_device(): lax.all_to_all(outgoing.reshape(DEV, STEP, 8, 128), ('gy', 'gx'), split_a...  10.4 us
    pallas_call x1, Pallas kernels, ocean_part(): pl.pallas_call(ocean_kernel, out_shape=(jax.ShapeDtypeStruct((ROWS, HID,...  10.1 us
    ppermute x2, starting transfers between devices, shift_gy(): lax.ppermute(x, 'gy', [(i, i + step) for i in range(n) if 0 <= i + step <...  9.44 us
    all_to_all x1, starting transfers between devices, per_device(): tops = lax.all_to_all(tops, 'gx', split_axis=0, concat_axis=0, tiled=True)  5.44 us
    pallas_call x1, Pallas kernels, coarse_sums(): pl.pallas_call(coarse_kernel, out_shape=(jax.ShapeDtypeStruct((HALF, FLD,...  5.28 us
    pallas_call x1, Pallas kernels, pack(): pl.pallas_call(pack_kernel, out_shape=jax.ShapeDtypeStruct((DEV * STEP, 8...  4.77 us
    ppermute x2, waiting for transfers between devices, shift_gx(): return lax.ppermute(x, 'gx', [(i, (i + step) % n) for i in range(n)])  4.64 us
  transfers between devices with their start and end apart: 6, of which 1 were waited for; matrix products, arithmetic and copies ran while one was open for 0% of the time, Pallas kernels for 37%

profile of v5, /device:TPU:66, one launch (start us, length us, event | category | flops | bytes accessed | tf_op | source)
XLA Modules:
  0.0 76.5 jit_solution(7298679502900670336)
XLA Ops:
  0.0 4.8 %pack.1 = bf16[896,8,128]{2,1,0:T(8,128)(2,1)} custom-call(s32[1,192]{1,0:T(1,128)} %bitcast.13, s32[1,192]{1,0:T(1,128)} %bitcast.14, s32[1,192]{1,0:T(1,128)} %bitcast.15, bf16[384,8,128]{2,1,0:T(8,128)(2,1)} %bitcast.12), custom_call_target="tpu_custom_call" | custom-call | tf_op jit(solution)/shard_map/pack/pallas_call | solution.py:125
  4.8 0.0 copy-start
  4.8 0.0 copy-start.1
  4.8 10.4 %all-to-all-start = ((bf16[128,7,8,128]{3,2,1,0:T(8,128)(2,1)}), bf16[128,7,8,128]{3,2,1,0:T(8,128)(2,1)}, u32[]{:S(2)}, u32[]{:S(2)}) async-start(bf16[128,7,8,128]{3,2,1,0:T(8,128)(2,1)} %bitcast.11), calls=%async_computation | async-start | bytes 3670016 | tf_op jit(solution)/shard_map/all_to_all | solution.py:787
  15.3 0.0 copy-start.11
  15.3 0.0 copy-start.16
  15.3 0.0 copy-start.17
  15.3 3.6 %edges.1 = (bf16[2,32,384]{2,1,0:T(8,128)(2,1)S(1)}, bf16[2,32,384]{2,1,0:T(8,128)(2,1)S(1)}) custom-call(bf16[384,16,256]{2,1,0:T(8,128)(2,1)S(1)} %copy-done, s32[384,256]{1,0:T(8,128)S(1)} %copy-done.1), custom_call_target="tpu_custom_call" | custom-call | tf_op jit(solution)/shard_map/edges/pallas_call | solution.py:304
  18.9 0.2 collective-permute-start
  19.2 2.5 %collective-permute-start.1 = (bf16[2,32,384]{2,1,0:T(8,128)(2,1)S(1)}, bf16[2,32,384]{2,1,0:T(8,128)(2,1)S(1)}, u32[]{:S(2)}, u32[]{:S(2)}) collective-permute-start(bf16[2,32,384]{2,1,0:T(8,128)(2,1)S(1)} %get-tuple-element.27.first_ref), channel_id=1, source_target_pairs={{0,15},{1,0},{2,1},{3,2},{4,3},{5,4},{6,5},{7,6},{8,7},{9,8},{10,9... | collective-permute-start | bytes 147464 | tf_op jit(solution)/shard_map/ppermute | solution.py:773
  21.7 10.1 %ocean.1 = (bf16[384,64,256]{2,1,0:T(8,128)(2,1)}, bf16[8,32,384]{2,1,0:T(8,128)(2,1)S(1)}, bf16[3,3,64,32]{3,2,1,0:T(8,128)(2,1)S(1)}, f32[64,128]{1,0:T(8,128)S(1)}, f32[8,128]{1,0:T(8,128)S(1)}) custom-call(bf16[384,16,256]{2,1,0:T(8,128)(2,1)S(1)} %copy-done, s32[384,256]{1,0:T(8,128)S(1)} %copy-done.1, bf16[3,3,32,64]{3,2,1,0:T(8,128)(2,1)S(1)} %bitcast.8, ...), custom_call_target="tpu_custom_call" | custom-call | tf_op jit(solution)/shard_map/ocean/pallas_call | solution.py:381
  31.7 0.0 copy-start.2
  31.8 0.7 copy-done.2
  32.4 0.6 copy-done.8
  33.0 4.6 %collective-permute-done.west_ref = bf16[2,32,384]{2,1,0:T(8,128)(2,1)S(1)} collective-permute-done((bf16[2,32,384]{2,1,0:T(8,128)(2,1)S(1)}, bf16[2,32,384]{2,1,0:T(8,128)(2,1)S(1)}, u32[]{:S(2)}, u32[]{:S(2)}) %collective-permute-start) | collective-permute-done | bytes 49184 | tf_op jit(solution)/shard_map/ppermute | solution.py:773
  37.7 0.0 collective-permute-done.1.east_ref
  37.7 0.0 copy-done.14
  37.7 0.0 copy-start.10
  37.7 0.5 margins.1
  38.2 0.6 copy-done.4
  38.8 0.6 copy-done.6
  39.4 0.0 all-to-all-done.inc_hbm
  39.4 5.3 %coarse.1 = (bf16[192,16,128]{2,1,0:T(8,128)(2,1)S(1)}, bf16[2,16,256]{2,1,0:T(8,128)(2,1)S(1)}, bf16[16,256]{1,0:T(8,128)(2,1)S(1)}, bf16[16,256]{1,0:T(8,128)(...) custom-call(bf16[128,7,8,128]{3,2,1,0:T(8,128)(2,1)} %all-to-all-don, ...), custom_call_target="tpu_custom_call" | custom-call | tf_op jit(solution)/shard_map/coarse/pallas_call | solution.py:247
  44.7 5.4 %all-to-all-start.1 = ((bf16[16,2,32,256]{3,2,1,0:T(8,128)(2,1)}), bf16[16,2,32,256]{3,2,1,0:T(8,128)(2,1)S(1)}, u32[]{:S(2)}, u32[]{:S(2)}) async-start(bf16[16,2,32,256]{3,2,1,0:T(8,128)(2,1)} %get-tuple-element.33), calls=%async_computation.1 | async-start | bytes 1048576 | tf_op jit(solution)/shard_map/all_to_all | solution.py:804
  50.1 3.3 %collective-permute-start.2 = (bf16[2,32,384]{2,1,0:T(8,128)(2,1)S(1)}, bf16[2,32,384]{2,1,0:T(8,128)(2,1)S(1)}, u32[]{:S(2)}, u32[]{:S(2)}) collective-permute-start(bf16[2,32,384]{2,1,0:T(8,128)(2,1)S(1)} %get-tuple-element.30.top_ref), channel_id=1, source_target_pairs={{0,16},{16,32},{32,48},{48,64},{64,80},{80,96},{96,112},{1,17},{17... | collective-permute-start | bytes 147464 | tf_op jit(solution)/shard_map/ppermute | solution.py:778
  53.4 6.2 %collective-permute-start.3 = (bf16[2,32,384]{2,1,0:T(8,128)(2,1)S(1)}, bf16[2,32,384]{2,1,0:T(8,128)(2,1)S(1)}, u32[]{:S(2)}, u32[]{:S(2)}) collective-permute-start(bf16[2,32,384]{2,1,0:T(8,128)(2,1)S(1)} %get-tuple-element.31.low_ref), channel_id=1, source_target_pairs={{16,0},{32,16},{48,32},{64,48},{80,64},{96,80},{112,96},{17,1},{33... | collective-permute-start | bytes 147464 | tf_op jit(solution)/shard_map/ppermute | solution.py:778
  59.7 0.0 copy-start.18
  59.7 14.2 %convs.1.main_ref = bf16[384,8,256]{2,1,0:T(8,128)(2,1)} custom-call(bf16[384,64,256]{2,1,0:T(8,128)(2,1)} %get-tuple-element.37.part_ref, f32[3,384,256]{2,1,0:T(8,128)S(1)} %get-tuple-element.38.m3_ref, bf16[192,16,128]{2,1,0:T(8,128)(2,1)S(1)} %get-tuple-element.39.coarse_ref, bf16[2,32,384]{2,1,0:T(8,128)(2,1)S(1)} %copy-done.13, ...), custom_call_target="tpu_custom_call" | custom-call | tf_op jit(solution)/shard_map/convs/pallas_call | solution.py:613
  73.9 0.0 collective-permute-done.2.south_ref
  73.9 0.0 collective-permute-done.3.north_ref
  73.9 0.0 all-to-all-done.1.tops_ref
  74.0 2.5 %patch.1 = bf16[384,8,256]{2,1,0:T(8,128)(2,1)} custom-call(s32[16]{0:T(128)S(1)} %copy-done.18, bf16[2,32,384]{2,1,0:T(8,128)(2,1)S(1)} %collective-permute-done.2.south_ref, bf16[2,32,384]{2,1,0:T(8,128)(2,1)S(1)} %get-tuple-element.31.low_ref, bf16[4,32,384]{2,1,0:T(8,128)(2,1)S(1)} %get-tuple-element.32.mid_ref, ...), custom_call_target="tpu_custom_call", output_to_operand_aliasing={{}: (12, {})} | custom-call | tf_op jit(solution)/shard_map/patch/pallas_call | solution.py:755
  (25 shorter events, 0.0 us)
Async XLA Ops:
  4.8 10.5 %copy-start = (bf16[384,16,256]{2,1,0:T(8,128)(2,1)S(1)}, bf16[384,16,256]{2,1,0:T(8,128)(2,1)}, u32[]{:S(2)}) copy-start(bf16[384,16,256]{2,1,0:T(8,128)(2,1)} %ocean_ref.1) | copy-start | bytes 9437188
  4.8 10.5 %copy-start.1 = (s32[384,256]{1,0:T(8,128)S(1)}, s32[384,256]{1,0:T(8,128)}, u32[]{:S(2)}) copy-start(s32[384,256]{1,0:T(8,128)} %mask_ref.2) | copy-start | bytes 1179652
  4.8 34.6 %all-to-all-start = ((bf16[128,7,8,128]{3,2,1,0:T(8,128)(2,1)}), bf16[128,7,8,128]{3,2,1,0:T(8,128)(2,1)}, u32[]{:S(2)}, u32[]{:S(2)}) async-start(bf16[128,7,8,128]{3,2,1,0:T(8,128)(2,1)} %bitcast.11), calls=%async_computation | async-start | bytes 3670016 | tf_op jit(solution)/shard_map/all_to_all | solution.py:787
  15.3 6.4 %copy-start.11 = (bf16[3,3,64,32]{2,3,1,0:T(8,128)(2,1)S(1)}, bf16[3,3,64,32]{2,3,1,0:T(8,128)(2,1)}, u32[]{:S(2)}) copy-start(bf16[3,3,64,32]{2,3,1,0:T(8,128)(2,1)} %param.18) | copy-start | bytes 110596
  15.3 6.4 %copy-start.16 = (f32[64]{0:T(128)S(1)}, f32[64]{0:T(128)}, u32[]{:S(2)}) copy-start(f32[64]{0:T(128)} %param.19) | copy-start | bytes 772
  15.3 6.4 %copy-start.17 = (f32[8]{0:T(128)S(1)}, f32[8]{0:T(128)}, u32[]{:S(2)}) copy-start(f32[8]{0:T(128)} %param.21) | copy-start | bytes 100
  18.9 18.8 %copy-start.12 = (bf16[2,32,384]{2,1,0:T(8,128)(2,1)}, bf16[2,32,384]{2,1,0:T(8,128)(2,1)S(1)}, u32[]{:S(2)}) copy-start(bf16[2,32,384]{2,1,0:T(8,128)(2,1)S(1)} %get-tuple-element.27.first_ref) | copy-start | bytes 147460
  18.9 18.8 %copy-start.14 = (bf16[2,32,384]{2,1,0:T(8,128)(2,1)}, bf16[2,32,384]{2,1,0:T(8,128)(2,1)S(1)}, u32[]{:S(2)}) copy-start(bf16[2,32,384]{2,1,0:T(8,128)(2,1)S(1)} %get-tuple-element.26.last_ref) | copy-start | bytes 147460
  18.9 18.7 %collective-permute-start = (bf16[2,32,384]{2,1,0:T(8,128)(2,1)S(1)}, bf16[2,32,384]{2,1,0:T(8,128)(2,1)S(1)}, u32[]{:S(2)}, u32[]{:S(2)}) collective-permute-start(bf16[2,32,384]{2,1,0:T(8,128)(2,1)S(1)} %get-tuple-element.26.last_ref), channel_id=1, source_target_pairs={{0,1},{1,2},{2,3},{3,4},{4,5},{5,6},{6,7},{7,8},{8,9},{9,10},{10,1... | collective-permute-start | bytes 147464 | tf_op jit(solution)/shard_map/ppermute | solution.py:773
  19.2 18.5 %collective-permute-start.1 = (bf16[2,32,384]{2,1,0:T(8,128)(2,1)S(1)}, bf16[2,32,384]{2,1,0:T(8,128)(2,1)S(1)}, u32[]{:S(2)}, u32[]{:S(2)}) collective-permute-start(bf16[2,32,384]{2,1,0:T(8,128)(2,1)S(1)} %get-tuple-element.27.first_ref), channel_id=1, source_target_pairs={{0,15},{1,0},{2,1},{3,2},{4,3},{5,4},{6,5},{7,6},{8,7},{9,8},{10,9... | collective-permute-start | bytes 147464 | tf_op jit(solution)/shard_map/ppermute | solution.py:773
  31.7 0.7 copy-start.2
  32.4 0.6 copy-start.8
  37.7 21.9 %copy-start.3 = (bf16[3,3,64,32]{3,2,1,0:T(8,128)(2,1)S(1)}, bf16[3,3,64,32]{3,2,1,0:T(8,128)(2,1)}, u32[]{:S(2)}) copy-start(bf16[3,3,64,32]{3,2,1,0:T(8,128)(2,1)} %copy-done.2) | copy-start | bytes 110596
  37.7 21.9 %copy-start.9 = (f32[64,128]{1,0:T(8,128)S(1)}, f32[64,128]{1,0:T(8,128)}, u32[]{:S(2)}) copy-start(f32[64,128]{1,0:T(8,128)} %copy-done.8) | copy-start | bytes 98308
  37.7 21.9 %copy-start.10 = (bf16[3,3,8,64]{3,2,1,0:T(8,128)(2,1)S(1)}, bf16[3,3,8,64]{3,2,1,0:T(8,128)(2,1)}, u32[]{:S(2)}) copy-start(bf16[3,3,8,64]{3,2,1,0:T(8,128)(2,1)} %w2_ref.3) | copy-start | bytes 27652
  37.7 21.9 %copy-start.13 = (bf16[2,32,384]{2,1,0:T(8,128)(2,1)S(1)}, bf16[2,32,384]{2,1,0:T(8,128)(2,1)}, u32[]{:S(2)}) copy-start(bf16[2,32,384]{2,1,0:T(8,128)(2,1)} %copy-done.12) | copy-start | bytes 147460
  38.2 0.6 copy-start.4
  38.8 0.6 copy-start.6
  39.4 20.2 %copy-start.15 = (bf16[2,32,384]{2,1,0:T(8,128)(2,1)S(1)}, bf16[2,32,384]{2,1,0:T(8,128)(2,1)}, u32[]{:S(2)}) copy-start(bf16[2,32,384]{2,1,0:T(8,128)(2,1)} %copy-done.14) | copy-start | bytes 147460
  39.4 20.2 %copy-start.5 = (bf16[2,32,384]{2,1,0:T(8,128)(2,1)S(1)}, bf16[2,32,384]{2,1,0:T(8,128)(2,1)}, u32[]{:S(2)}) copy-start(bf16[2,32,384]{2,1,0:T(8,128)(2,1)} %copy-done.4) | copy-start | bytes 147460
  39.4 20.3 %copy-start.7 = (bf16[2,32,384]{2,1,0:T(8,128)(2,1)S(1)}, bf16[2,32,384]{2,1,0:T(8,128)(2,1)}, u32[]{:S(2)}) copy-start(bf16[2,32,384]{2,1,0:T(8,128)(2,1)} %copy-done.6) | copy-start | bytes 147460
  44.7 29.2 %all-to-all-start.1 = ((bf16[16,2,32,256]{3,2,1,0:T(8,128)(2,1)}), bf16[16,2,32,256]{3,2,1,0:T(8,128)(2,1)S(1)}, u32[]{:S(2)}, u32[]{:S(2)}) async-start(bf16[16,2,32,256]{3,2,1,0:T(8,128)(2,1)} %get-tuple-element.33), calls=%async_computation.1 | async-start | bytes 1048576 | tf_op jit(solution)/shard_map/all_to_all | solution.py:804
  50.1 23.8 %collective-permute-start.2 = (bf16[2,32,384]{2,1,0:T(8,128)(2,1)S(1)}, bf16[2,32,384]{2,1,0:T(8,128)(2,1)S(1)}, u32[]{:S(2)}, u32[]{:S(2)}) collective-permute-start(bf16[2,32,384]{2,1,0:T(8,128)(2,1)S(1)} %get-tuple-element.30.top_ref), channel_id=1, source_target_pairs={{0,16},{16,32},{32,48},{48,64},{64,80},{80,96},{96,112},{1,17},{17... | collective-permute-start | bytes 147464 | tf_op jit(solution)/shard_map/ppermute | solution.py:778
  53.4 20.5 %collective-permute-start.3 = (bf16[2,32,384]{2,1,0:T(8,128)(2,1)S(1)}, bf16[2,32,384]{2,1,0:T(8,128)(2,1)S(1)}, u32[]{:S(2)}, u32[]{:S(2)}) collective-permute-start(bf16[2,32,384]{2,1,0:T(8,128)(2,1)S(1)} %get-tuple-element.31.low_ref), channel_id=1, source_target_pairs={{16,0},{32,16},{48,32},{64,48},{80,64},{96,80},{112,96},{17,1},{33... | collective-permute-start | bytes 147464 | tf_op jit(solution)/shard_map/ppermute | solution.py:778
  59.7 14.3 %copy-start.18 = (s32[16]{0:T(128)S(1)}, s32[16]{0:T(128)}, u32[]{:S(2)}) copy-start(s32[16]{0:T(128)} %fold_ref.1) | copy-start | bytes 196

commit v6 on v5

--- a/solution.py
+++ b/solution.py
@@ -38,15 +38,17 @@
 
 
 def pack_kernel(
-    tile_ref, row_ref, live_ref, atm_hbm, out_hbm, atm_ref, out_ref, q_ref, code_ref, info_ref,
-    sem, in_sem, out_sem,
+    tile_ref, row_ref, live_ref, atm_hbm, out_hbm, atm_ref, out_ref, head_ref, q_ref, code_ref,
+    info_ref, sem, in_sem, out_sem, head_sem,
 ):
     loads, stores = [], []
     for c in range(PIECES):
         at = pl.ds(c * (2 * HALF // PIECES), 2 * HALF // PIECES)
         loads.append(pltpu.make_async_copy(atm_hbm.at[at], atm_ref.at[at], in_sem.at[c]))
-        at = pl.ds(c * (DEV * STEP // PIECES), DEV * STEP // PIECES)
-        stores.append(pltpu.make_async_copy(out_ref.at[at], out_hbm.at[at], out_sem.at[c]))
+        at = pl.ds(c * (DEV // PIECES), DEV // PIECES)
+        stores.append(
+            pltpu.make_async_copy(out_ref.at[at], out_hbm.at[at, pl.ds(0, STEP - 1)], out_sem.at[c])
+        )
         loads[c].start()
     across = jnp.concatenate([tile_ref[...].astype(F32), jnp.full((1, 64), -1.0, F32)], axis=1)
     column = jnp.broadcast_to(across, (128, 256))
@@ -76,6 +78,16 @@
         c0, c1 = lax.fori_loop(0, count, ends, (zero, zero), unroll=32)
         first.append(c0)
         last.append(c1)
+    copy.wait()
+
+    def place(n, carry):
+        code = info_ref[0, n]
+        out_ref[code >> 2, pl.ds(2 * (code & 3), 2)] = atm_ref[pl.ds(2 * n, 2)]
+        return carry
+
+    lax.fori_loop(0, HALF, place, 0, unroll=32)
+    for store in stores:
+        store.start()
     values = [jnp.concatenate(last, axis=1), jnp.concatenate(first, axis=1)]
     code = jnp.broadcast_to(code_ref[...], (DEV, 256))
     row = jnp.where(live_ref[...] == 1, row_ref[...] + 1, 0).astype(F32)
@@ -96,27 +108,17 @@
         preferred_element_type=F32,
     )
     q_ref[...] = total
-    copy.wait()
-
-    def place(n, carry):
-        code = info_ref[0, n]
-        out_ref[pl.ds(STEP * (code >> 2) + 2 * (code & 3), 2)] = atm_ref[pl.ds(2 * n, 2)]
-        return carry
-
-    lax.fori_loop(0, HALF, place, 0, unroll=32)
     sub = subs((8, 128))
-    for c in range(PIECES):
-        for t in range(c * DEV // PIECES, (c + 1) * DEV // PIECES):
-            near = (t & -16) + ((t + 15) & 15)
-            far = (t & -16) + ((t + 1) & 15)
-            own, west, east = [
-                jnp.broadcast_to(q_ref[i : i + 1, :], (8, 128)) for i in (t, near, far)
-            ]
-            head = jnp.where(sub == 0, own, jnp.where(sub == 1, west, east))
-            out_ref[STEP * t + STEP - 1] = head.astype(BF)
-        stores[c].start()
+    for t in range(DEV):
+        near = (t & -16) + ((t + 15) & 15)
+        far = (t & -16) + ((t + 1) & 15)
+        own, west, east = [jnp.broadcast_to(q_ref[i : i + 1, :], (8, 128)) for i in (t, near, far)]
+        head_ref[t] = jnp.where(sub == 0, own, jnp.where(sub == 1, west, east)).astype(BF)
+    heads = pltpu.make_async_copy(head_ref, out_hbm.at[:, STEP - 1], head_sem)
+    heads.start()
     for store in stores:
         store.wait()
+    heads.wait()
 
 
 def pack(tile, row, live, atm):
@@ -124,18 +126,20 @@
     hbm = pl.BlockSpec(memory_space=pl.ANY)
     return pl.pallas_call(
         pack_kernel,
-        out_shape=jax.ShapeDtypeStruct((DEV * STEP, 8, 128), BF),
+        out_shape=jax.ShapeDtypeStruct((DEV, STEP, 8, 128), BF),
         in_specs=[vmem, vmem, vmem, hbm],
         out_specs=hbm,
         scratch_shapes=[
             pltpu.VMEM((2 * HALF, 8, 128), BF),
-            pltpu.VMEM((DEV * STEP, 8, 128), BF),
+            pltpu.VMEM((DEV, STEP - 1, 8, 128), BF),
+            pltpu.VMEM((DEV, 8, 128), BF),
             pltpu.VMEM((DEV, 128), F32),
             pltpu.VMEM((1, 256), I32),
             pltpu.SMEM((1, 256), I32),
             pltpu.SemaphoreType.DMA,
             pltpu.SemaphoreType.DMA((PIECES,)),
             pltpu.SemaphoreType.DMA((PIECES,)),
+            pltpu.SemaphoreType.DMA,
         ],
         compiler_params=pltpu.CompilerParams(vmem_limit_bytes=56 << 20),
         name="pack",
@@ -785,7 +789,7 @@
         dest_tile.reshape(1, HALF), dest_row.reshape(1, HALF), live.reshape(1, HALF), atm.reshape(2 * HALF, 8, 128)
     )
     incoming = lax.all_to_all(
-        outgoing.reshape(DEV, STEP, 8, 128), ("gy", "gx"), split_axis=0, concat_axis=0, tiled=True
+        outgoing, ("gy", "gx"), split_axis=0, concat_axis=0, tiled=True
     )
     ocean, land_mask, _ = lax.optimization_barrier((ocean, land_mask, outgoing))
     first, last = edge_columns(ocean, land_mask)

time: 76.8 us -> 76.6 us (level)
  no operation moved by 1% of the time
where the time goes in v6:
time: 76.6 us; the launch traced here: 76.3 us
  Pallas kernels  40.7 us (53%)
  starting transfers between devices  28 us (37%)
  waiting for transfers between devices  4.65 us (6%)
  local copies, waits for them, and re-layouts  2.57 us (3%)
    pallas_call x1, Pallas kernels, main_conv(): pl.pallas_call(main_kernel, out_shape=jax.ShapeDtypeStruct((ROWS, OUT, CO...  14.2 us
    all_to_all x1, starting transfers between devices, per_device(): lax.all_to_all(outgoing, ('gy', 'gx'), split_axis=0, concat_axis=0, tiled...  10.4 us
    pallas_call x1, Pallas kernels, ocean_part(): pl.pallas_call(ocean_kernel, out_shape=(jax.ShapeDtypeStruct((ROWS, HID,...  10.1 us
    ppermute x2, starting transfers between devices, shift_gy(): lax.ppermute(x, 'gy', [(i, i + step) for i in range(n) if 0 <= i + step <...  9.44 us
    all_to_all x1, starting transfers between devices, per_device(): tops = lax.all_to_all(tops, 'gx', split_axis=0, concat_axis=0, tiled=True)  5.44 us
    pallas_call x1, Pallas kernels, coarse_sums(): pl.pallas_call(coarse_kernel, out_shape=(jax.ShapeDtypeStruct((HALF, FLD,...  5.28 us
    ppermute x2, waiting for transfers between devices, shift_gx(): return lax.ppermute(x, 'gx', [(i, (i + step) % n) for i in range(n)])  4.64 us
    pallas_call x1, Pallas kernels, pack(): pl.pallas_call(pack_kernel, out_shape=jax.ShapeDtypeStruct((DEV, STEP, 8,...  4.61 us
  transfers between devices with their start and end apart: 6, of which 1 were waited for; matrix products, arithmetic and copies ran while one was open for 0% of the time, Pallas kernels for 37%

profile of v6, /device:TPU:66, one launch (start us, length us, event | category | flops | bytes accessed | tf_op | source)
XLA Modules:
  0.0 76.3 jit_solution(1771654349404921427)
XLA Ops:
  0.0 4.6 %pack.1 = bf16[128,7,8,128]{3,2,1,0:T(8,128)(2,1)} custom-call(s32[1,192]{1,0:T(1,128)} %bitcast.11, s32[1,192]{1,0:T(1,128)} %bitcast.12, s32[1,192]{1,0:T(1,128)} %bitcast.13, bf16[384,8,128]{2,1,0:T(8,128)(2,1)} %bitcast.10), custom_call_target="tpu_custom_call" | custom-call | tf_op jit(solution)/shard_map/pack/pallas_call | solution.py:127
  4.6 0.0 copy-start
  4.6 0.0 copy-start.1
  4.6 10.4 %all-to-all-start = ((bf16[128,7,8,128]{3,2,1,0:T(8,128)(2,1)}), bf16[128,7,8,128]{3,2,1,0:T(8,128)(2,1)}, u32[]{:S(2)}, u32[]{:S(2)}) async-start(bf16[128,7,8,128]{3,2,1,0:T(8,128)(2,1)} %pack.1), calls=%async_computation | async-start | bytes 3670016 | tf_op jit(solution)/shard_map/all_to_all | solution.py:791
  15.1 0.0 copy-start.11
  15.1 0.0 copy-start.16
  15.1 0.0 copy-start.17
  15.1 3.6 %edges.1 = (bf16[2,32,384]{2,1,0:T(8,128)(2,1)S(1)}, bf16[2,32,384]{2,1,0:T(8,128)(2,1)S(1)}) custom-call(bf16[384,16,256]{2,1,0:T(8,128)(2,1)S(1)} %copy-done, s32[384,256]{1,0:T(8,128)S(1)} %copy-done.1), custom_call_target="tpu_custom_call" | custom-call | tf_op jit(solution)/shard_map/edges/pallas_call | solution.py:308
  18.8 0.2 collective-permute-start
  19.0 2.5 %collective-permute-start.1 = (bf16[2,32,384]{2,1,0:T(8,128)(2,1)S(1)}, bf16[2,32,384]{2,1,0:T(8,128)(2,1)S(1)}, u32[]{:S(2)}, u32[]{:S(2)}) collective-permute-start(bf16[2,32,384]{2,1,0:T(8,128)(2,1)S(1)} %get-tuple-element.27.first_ref), channel_id=1, source_target_pairs={{0,15},{1,0},{2,1},{3,2},{4,3},{5,4},{6,5},{7,6},{8,7},{9,8},{10,9... | collective-permute-start | bytes 147464 | tf_op jit(solution)/shard_map/ppermute | solution.py:777
  21.5 10.1 %ocean.1 = (bf16[384,64,256]{2,1,0:T(8,128)(2,1)}, bf16[8,32,384]{2,1,0:T(8,128)(2,1)S(1)}, bf16[3,3,64,32]{3,2,1,0:T(8,128)(2,1)S(1)}, f32[64,128]{1,0:T(8,128)S(1)}, f32[8,128]{1,0:T(8,128)S(1)}) custom-call(bf16[384,16,256]{2,1,0:T(8,128)(2,1)S(1)} %copy-done, s32[384,256]{1,0:T(8,128)S(1)} %copy-done.1, bf16[3,3,32,64]{3,2,1,0:T(8,128)(2,1)S(1)} %bitcast.7, ...), custom_call_target="tpu_custom_call" | custom-call | tf_op jit(solution)/shard_map/ocean/pallas_call | solution.py:385
  31.6 0.0 copy-start.2
  31.6 0.7 copy-done.2
  32.2 0.6 copy-done.8
  32.9 4.6 %collective-permute-done.west_ref = bf16[2,32,384]{2,1,0:T(8,128)(2,1)S(1)} collective-permute-done((bf16[2,32,384]{2,1,0:T(8,128)(2,1)S(1)}, bf16[2,32,384]{2,1,0:T(8,128)(2,1)S(1)}, u32[]{:S(2)}, u32[]{:S(2)}) %collective-permute-start) | collective-permute-done | bytes 49184 | tf_op jit(solution)/shard_map/ppermute | solution.py:777
  37.5 0.0 collective-permute-done.1.east_ref
  37.5 0.0 copy-done.14
  37.5 0.0 copy-start.10
  37.6 0.5 margins.1
  38.0 0.6 copy-done.4
  38.6 0.6 copy-done.6
  39.2 0.0 all-to-all-done.inc_hbm
  39.3 5.3 %coarse.1 = (bf16[192,16,128]{2,1,0:T(8,128)(2,1)S(1)}, bf16[2,16,256]{2,1,0:T(8,128)(2,1)S(1)}, bf16[16,256]{1,0:T(8,128)(2,1)S(1)}, bf16[16,256]{1,0:T(8,128)(...) custom-call(bf16[128,7,8,128]{3,2,1,0:T(8,128)(2,1)} %all-to-all-don, ...), custom_call_target="tpu_custom_call" | custom-call | tf_op jit(solution)/shard_map/coarse/pallas_call | solution.py:251
  44.5 5.4 %all-to-all-start.1 = ((bf16[16,2,32,256]{3,2,1,0:T(8,128)(2,1)}), bf16[16,2,32,256]{3,2,1,0:T(8,128)(2,1)S(1)}, u32[]{:S(2)}, u32[]{:S(2)}) async-start(bf16[16,2,32,256]{3,2,1,0:T(8,128)(2,1)} %get-tuple-element.33), calls=%async_computation.1 | async-start | bytes 1048576 | tf_op jit(solution)/shard_map/all_to_all | solution.py:808
  50.0 3.3 %collective-permute-start.2 = (bf16[2,32,384]{2,1,0:T(8,128)(2,1)S(1)}, bf16[2,32,384]{2,1,0:T(8,128)(2,1)S(1)}, u32[]{:S(2)}, u32[]{:S(2)}) collective-permute-start(bf16[2,32,384]{2,1,0:T(8,128)(2,1)S(1)} %get-tuple-element.30.top_ref), channel_id=1, source_target_pairs={{0,16},{16,32},{32,48},{48,64},{64,80},{80,96},{96,112},{1,17},{17... | collective-permute-start | bytes 147464 | tf_op jit(solution)/shard_map/ppermute | solution.py:782
  53.3 6.2 %collective-permute-start.3 = (bf16[2,32,384]{2,1,0:T(8,128)(2,1)S(1)}, bf16[2,32,384]{2,1,0:T(8,128)(2,1)S(1)}, u32[]{:S(2)}, u32[]{:S(2)}) collective-permute-start(bf16[2,32,384]{2,1,0:T(8,128)(2,1)S(1)} %get-tuple-element.31.low_ref), channel_id=1, source_target_pairs={{16,0},{32,16},{48,32},{64,48},{80,64},{96,80},{112,96},{17,1},{33... | collective-permute-start | bytes 147464 | tf_op jit(solution)/shard_map/ppermute | solution.py:782
  59.5 0.0 copy-start.18
  59.5 14.2 %convs.1.main_ref = bf16[384,8,256]{2,1,0:T(8,128)(2,1)} custom-call(bf16[384,64,256]{2,1,0:T(8,128)(2,1)} %get-tuple-element.37.part_ref, f32[3,384,256]{2,1,0:T(8,128)S(1)} %get-tuple-element.38.m3_ref, bf16[192,16,128]{2,1,0:T(8,128)(2,1)S(1)} %get-tuple-element.39.coarse_ref, bf16[2,32,384]{2,1,0:T(8,128)(2,1)S(1)} %copy-done.13, ...), custom_call_target="tpu_custom_call" | custom-call | tf_op jit(solution)/shard_map/convs/pallas_call | solution.py:617
  73.8 0.0 collective-permute-done.2.south_ref
  73.8 0.0 collective-permute-done.3.north_ref
  73.8 0.0 all-to-all-done.1.tops_ref
  73.8 2.5 %patch.1 = bf16[384,8,256]{2,1,0:T(8,128)(2,1)} custom-call(s32[16]{0:T(128)S(1)} %copy-done.18, bf16[2,32,384]{2,1,0:T(8,128)(2,1)S(1)} %collective-permute-done.2.south_ref, bf16[2,32,384]{2,1,0:T(8,128)(2,1)S(1)} %get-tuple-element.31.low_ref, bf16[4,32,384]{2,1,0:T(8,128)(2,1)S(1)} %get-tuple-element.32.mid_ref, ...), custom_call_target="tpu_custom_call", output_to_operand_aliasing={{}: (12, {})} | custom-call | tf_op jit(solution)/shard_map/patch/pallas_call | solution.py:759
  (25 shorter events, 0.0 us)
Async XLA Ops:
  4.6 10.5 %copy-start = (bf16[384,16,256]{2,1,0:T(8,128)(2,1)S(1)}, bf16[384,16,256]{2,1,0:T(8,128)(2,1)}, u32[]{:S(2)}) copy-start(bf16[384,16,256]{2,1,0:T(8,128)(2,1)} %ocean_ref.1) | copy-start | bytes 9437188
  4.6 10.5 %copy-start.1 = (s32[384,256]{1,0:T(8,128)S(1)}, s32[384,256]{1,0:T(8,128)}, u32[]{:S(2)}) copy-start(s32[384,256]{1,0:T(8,128)} %mask_ref.2) | copy-start | bytes 1179652
  4.6 34.6 %all-to-all-start = ((bf16[128,7,8,128]{3,2,1,0:T(8,128)(2,1)}), bf16[128,7,8,128]{3,2,1,0:T(8,128)(2,1)}, u32[]{:S(2)}, u32[]{:S(2)}) async-start(bf16[128,7,8,128]{3,2,1,0:T(8,128)(2,1)} %pack.1), calls=%async_computation | async-start | bytes 3670016 | tf_op jit(solution)/shard_map/all_to_all | solution.py:791
  15.1 6.4 %copy-start.11 = (bf16[3,3,64,32]{2,3,1,0:T(8,128)(2,1)S(1)}, bf16[3,3,64,32]{2,3,1,0:T(8,128)(2,1)}, u32[]{:S(2)}) copy-start(bf16[3,3,64,32]{2,3,1,0:T(8,128)(2,1)} %param.18) | copy-start | bytes 110596
  15.1 6.4 %copy-start.16 = (f32[64]{0:T(128)S(1)}, f32[64]{0:T(128)}, u32[]{:S(2)}) copy-start(f32[64]{0:T(128)} %param.19) | copy-start | bytes 772
  15.1 6.4 %copy-start.17 = (f32[8]{0:T(128)S(1)}, f32[8]{0:T(128)}, u32[]{:S(2)}) copy-start(f32[8]{0:T(128)} %param.21) | copy-start | bytes 100
  18.8 18.8 %copy-start.12 = (bf16[2,32,384]{2,1,0:T(8,128)(2,1)}, bf16[2,32,384]{2,1,0:T(8,128)(2,1)S(1)}, u32[]{:S(2)}) copy-start(bf16[2,32,384]{2,1,0:T(8,128)(2,1)S(1)} %get-tuple-element.27.first_ref) | copy-start | bytes 147460
  18.8 18.8 %copy-start.14 = (bf16[2,32,384]{2,1,0:T(8,128)(2,1)}, bf16[2,32,384]{2,1,0:T(8,128)(2,1)S(1)}, u32[]{:S(2)}) copy-start(bf16[2,32,384]{2,1,0:T(8,128)(2,1)S(1)} %get-tuple-element.26.last_ref) | copy-start | bytes 147460
  18.8 18.7 %collective-permute-start = (bf16[2,32,384]{2,1,0:T(8,128)(2,1)S(1)}, bf16[2,32,384]{2,1,0:T(8,128)(2,1)S(1)}, u32[]{:S(2)}, u32[]{:S(2)}) collective-permute-start(bf16[2,32,384]{2,1,0:T(8,128)(2,1)S(1)} %get-tuple-element.26.last_ref), channel_id=1, source_target_pairs={{0,1},{1,2},{2,3},{3,4},{4,5},{5,6},{6,7},{7,8},{8,9},{9,10},{10,1... | collective-permute-start | bytes 147464 | tf_op jit(solution)/shard_map/ppermute | solution.py:777
  19.0 18.5 %collective-permute-start.1 = (bf16[2,32,384]{2,1,0:T(8,128)(2,1)S(1)}, bf16[2,32,384]{2,1,0:T(8,128)(2,1)S(1)}, u32[]{:S(2)}, u32[]{:S(2)}) collective-permute-start(bf16[2,32,384]{2,1,0:T(8,128)(2,1)S(1)} %get-tuple-element.27.first_ref), channel_id=1, source_target_pairs={{0,15},{1,0},{2,1},{3,2},{4,3},{5,4},{6,5},{7,6},{8,7},{9,8},{10,9... | collective-permute-start | bytes 147464 | tf_op jit(solution)/shard_map/ppermute | solution.py:777
  31.6 0.7 copy-start.2
  32.2 0.6 copy-start.8
  37.5 21.9 %copy-start.3 = (bf16[3,3,64,32]{3,2,1,0:T(8,128)(2,1)S(1)}, bf16[3,3,64,32]{3,2,1,0:T(8,128)(2,1)}, u32[]{:S(2)}) copy-start(bf16[3,3,64,32]{3,2,1,0:T(8,128)(2,1)} %copy-done.2) | copy-start | bytes 110596
  37.5 21.9 %copy-start.9 = (f32[64,128]{1,0:T(8,128)S(1)}, f32[64,128]{1,0:T(8,128)}, u32[]{:S(2)}) copy-start(f32[64,128]{1,0:T(8,128)} %copy-done.8) | copy-start | bytes 98308
  37.5 21.9 %copy-start.10 = (bf16[3,3,8,64]{3,2,1,0:T(8,128)(2,1)S(1)}, bf16[3,3,8,64]{3,2,1,0:T(8,128)(2,1)}, u32[]{:S(2)}) copy-start(bf16[3,3,8,64]{3,2,1,0:T(8,128)(2,1)} %w2_ref.3) | copy-start | bytes 27652
  37.5 21.9 %copy-start.13 = (bf16[2,32,384]{2,1,0:T(8,128)(2,1)S(1)}, bf16[2,32,384]{2,1,0:T(8,128)(2,1)}, u32[]{:S(2)}) copy-start(bf16[2,32,384]{2,1,0:T(8,128)(2,1)} %copy-done.12) | copy-start | bytes 147460
  38.0 0.6 copy-start.4
  38.6 0.6 copy-start.6
  39.2 20.2 %copy-start.15 = (bf16[2,32,384]{2,1,0:T(8,128)(2,1)S(1)}, bf16[2,32,384]{2,1,0:T(8,128)(2,1)}, u32[]{:S(2)}) copy-start(bf16[2,32,384]{2,1,0:T(8,128)(2,1)} %copy-done.14) | copy-start | bytes 147460
  39.3 20.2 %copy-start.5 = (bf16[2,32,384]{2,1,0:T(8,128)(2,1)S(1)}, bf16[2,32,384]{2,1,0:T(8,128)(2,1)}, u32[]{:S(2)}) copy-start(bf16[2,32,384]{2,1,0:T(8,128)(2,1)} %copy-done.4) | copy-start | bytes 147460
  39.3 20.3 %copy-start.7 = (bf16[2,32,384]{2,1,0:T(8,128)(2,1)S(1)}, bf16[2,32,384]{2,1,0:T(8,128)(2,1)}, u32[]{:S(2)}) copy-start(bf16[2,32,384]{2,1,0:T(8,128)(2,1)} %copy-done.6) | copy-start | bytes 147460
  44.5 29.2 %all-to-all-start.1 = ((bf16[16,2,32,256]{3,2,1,0:T(8,128)(2,1)}), bf16[16,2,32,256]{3,2,1,0:T(8,128)(2,1)S(1)}, u32[]{:S(2)}, u32[]{:S(2)}) async-start(bf16[16,2,32,256]{3,2,1,0:T(8,128)(2,1)} %get-tuple-element.33), calls=%async_computation.1 | async-start | bytes 1048576 | tf_op jit(solution)/shard_map/all_to_all | solution.py:808
  50.0 23.8 %collective-permute-start.2 = (bf16[2,32,384]{2,1,0:T(8,128)(2,1)S(1)}, bf16[2,32,384]{2,1,0:T(8,128)(2,1)S(1)}, u32[]{:S(2)}, u32[]{:S(2)}) collective-permute-start(bf16[2,32,384]{2,1,0:T(8,128)(2,1)S(1)} %get-tuple-element.30.top_ref), channel_id=1, source_target_pairs={{0,16},{16,32},{32,48},{48,64},{64,80},{80,96},{96,112},{1,17},{17... | collective-permute-start | bytes 147464 | tf_op jit(solution)/shard_map/ppermute | solution.py:782
  53.3 20.5 %collective-permute-start.3 = (bf16[2,32,384]{2,1,0:T(8,128)(2,1)S(1)}, bf16[2,32,384]{2,1,0:T(8,128)(2,1)S(1)}, u32[]{:S(2)}, u32[]{:S(2)}) collective-permute-start(bf16[2,32,384]{2,1,0:T(8,128)(2,1)S(1)} %get-tuple-element.31.low_ref), channel_id=1, source_target_pairs={{16,0},{32,16},{48,32},{64,48},{80,64},{96,80},{112,96},{17,1},{33... | collective-permute-start | bytes 147464 | tf_op jit(solution)/shard_map/ppermute | solution.py:782
  59.5 14.3 %copy-start.18 = (s32[16]{0:T(128)S(1)}, s32[16]{0:T(128)}, u32[]{:S(2)}) copy-start(s32[16]{0:T(128)} %fold_ref.1) | copy-start | bytes 196
